TPU v7x, 32 devices: a whole 2x2x4 slice. The times are simulated.
32 devices in a mesh: rows: 4 (over y, x), cols: 8 (over z, core).
Axes of the slice: x: 2, y: 2, z: 4, core: 2. Of those that a mesh axis runs over, the one named last changes fastest.
Arguments:
- tokens: bfloat16 [1024, 2048], P('rows', 'cols'), may hold values from -6 to 6
- segments: int32 [4, 256], P('rows'), may hold values from 0 to 3, never falling along the last dimension, each value on 1 to 128 neighbouring positions
- w_query: bfloat16 [2048, 2048], P('rows', 'cols'), may hold values from -0.125 to 0.125
- w_key: bfloat16 [2048, 2048], P('rows', 'cols'), may hold values from -0.125 to 0.125
- w_value: bfloat16 [2048, 2048], P('rows', 'cols'), may hold values from -0.125 to 0.125
- w_out: bfloat16 [2048, 2048], P('cols', 'rows'), may hold values from -0.75 to 0.75
- w_gate: bfloat16 [2048, 8192], P('rows', 'cols'), may hold values from -0.125 to 0.125
- w_up: bfloat16 [2048, 8192], P('rows', 'cols'), may hold values from -0.125 to 0.125
- w_down: bfloat16 [8192, 2048], P('cols', 'rows'), may hold values from -0.0625 to 0.0625
- cotangent: bfloat16 [1024, 2048], P('rows', 'cols'), may hold values from -6 to 6
Outputs:
- layer_out: bfloat16 [1024, 2048], P('rows', 'cols')
- grad_input: float32 [1024, 2048], P('rows', 'cols')
- grad_query: float32 [2048, 2048], P('rows', 'cols')
- grad_key: float32 [2048, 2048], P('rows', 'cols')
- grad_value: float32 [2048, 2048], P('rows', 'cols')
- grad_out: float32 [2048, 2048], P('cols', 'rows')
- grad_gate: float32 [2048, 8192], P('rows', 'cols')
- grad_up: float32 [2048, 8192], P('rows', 'cols')
- grad_down: float32 [8192, 2048], P('cols', 'rows')
Inputs may be any that keep to these rules, and one draw needn't show every extreme that they name: `segments`: segment numbers never fall along a sequence and start at 0; each document holds 1 to 128 tokens, and in each sequence one holds exactly 128.
All inputs are finite; a program needn't handle non-finite values.
Results may differ from a plain program's by a relative error of at most 0.017.
Values may be sent and summed in bfloat16 or wider, within the bound.
A program may use at most 128 MiB of HBM per device.

v0:
```python
import jax
import jax.numpy as jnp
from jax import lax
from jax.sharding import PartitionSpec as P

D = 2048
HD = 128


EPS = 1e-05
NEG = -1e30
BASE = 10000.0


def doc_positions(seg):
    count = seg.shape[0]
    index = jnp.arange(count, dtype=jnp.int32)
    first = jnp.concatenate([jnp.ones((1,), dtype=bool), seg[1:] != seg[:-1]])
    start = lax.cummax(jnp.where(first, index, 0), axis=0)
    return index - start


def rope_tables(pos):
    half = HD // 2
    freq = BASE ** (-(jnp.arange(half, dtype=jnp.float32) * 2.0) / HD)
    angle = pos.astype(jnp.float32)[:, None] * freq[None, :]
    cosine = jnp.cos(angle)
    sine = jnp.sin(angle)
    return (
        jnp.concatenate([cosine, cosine], 1)[:, None, :],
        jnp.concatenate([-sine, sine], 1)[:, None, :],
    )


def swap_halves(v):
    half = HD // 2
    return jnp.concatenate([v[..., half:], v[..., :half]], -1)


def rotate(v, cos_full, sin_full):
    return v * cos_full + swap_halves(v) * sin_full


def unrotate(grad, cos_full, sin_full):
    return grad * cos_full + swap_halves(grad * sin_full)


def times_trans(a, b):
    return lax.dot_general(a, b, (((1,), (1,)), ((), ())), preferred_element_type=jnp.float32)


def trans_times(a, b):
    return lax.dot_general(a, b, (((0,), (0,)), ((), ())), preferred_element_type=jnp.float32)


def moments(total, squares, width):
    mean = total / width
    return (mean, lax.rsqrt(squares / width - mean * mean + EPS))


def norm_back(grad, normed, rstd, width):
    first = jnp.sum(grad, 1, keepdims=True) / width
    second = jnp.sum(grad * normed, 1, keepdims=True) / width
    return rstd * (grad - first - normed * second)


def spread(block):
    return lax.all_gather(block, "cols", axis=1, tiled=True)


def whole_sum(part):
    return lax.psum(part, "cols")


def mask_for(seg_blk, idx_blk, seg, index):
    return (seg_blk[:, None] == seg[None, :]) & (idx_blk[:, None] >= index[None, :])


def attend(query, key, value, seg, block):
    length, heads, _ = query.shape
    count = length // block
    index = jnp.arange(length, dtype=jnp.int32)
    scale = HD ** (-0.5)

    def one_block(item):
        q_blk, seg_blk, idx_blk = item
        score = jnp.einsum("qhd,khd->hqk", q_blk, key, preferred_element_type=jnp.float32) * scale
        score = jnp.where(mask_for(seg_blk, idx_blk, seg, index)[None], score, NEG)
        top = jnp.max(score, -1, keepdims=True)
        expo = jnp.exp(score - top)
        total = jnp.sum(expo, -1, keepdims=True)
        prob = (expo / total).astype(jnp.bfloat16)
        mixed = jnp.einsum("hqk,khd->qhd", prob, value, preferred_element_type=jnp.float32)
        return (mixed.astype(jnp.bfloat16), (top + jnp.log(total))[..., 0])

    items = (
        query.reshape(count, block, heads, HD),
        seg.reshape(count, block),
        index.reshape(count, block),
    )
    mixed, lse = lax.map(one_block, items)
    return (mixed.reshape(length, heads * HD), lse)


def attend_back(query, key, value, grad_mix, lse, seg, block):
    length, heads, _ = query.shape
    count = length // block
    index = jnp.arange(length, dtype=jnp.int32)
    scale = HD ** (-0.5)

    def one_block(carry, item):
        grad_key, grad_value = carry
        q_blk, g_blk, lse_blk, seg_blk, idx_blk = item
        score = jnp.einsum("qhd,khd->hqk", q_blk, key, preferred_element_type=jnp.float32) * scale
        score = jnp.where(mask_for(seg_blk, idx_blk, seg, index)[None], score, NEG)
        prob = jnp.exp(score - lse_blk[..., None])
        grad_prob = jnp.einsum("qhd,khd->hqk", g_blk, value, preferred_element_type=jnp.float32)
        inner = jnp.sum(prob * grad_prob, -1, keepdims=True)
        grad_score = (prob * (grad_prob - inner)).astype(jnp.bfloat16)
        grad_query = (
            jnp.einsum("hqk,khd->qhd", grad_score, key, preferred_element_type=jnp.float32) * scale
        )
        grad_key = (
            grad_key
            + jnp.einsum("hqk,qhd->khd", grad_score, q_blk, preferred_element_type=jnp.float32)
            * scale
        )
        grad_value = grad_value + jnp.einsum(
            "hqk,qhd->khd", prob.astype(jnp.bfloat16), g_blk, preferred_element_type=jnp.float32
        )
        return ((grad_key, grad_value), grad_query)

    zeros = jnp.zeros((length, heads, HD), jnp.float32)
    items = (
        query.reshape(count, block, heads, HD),
        grad_mix.reshape(count, block, heads, HD),
        lse,
        seg.reshape(count, block),
        index.reshape(count, block),
    )
    (grad_key, grad_value), grad_query = lax.scan(one_block, (zeros, zeros), items)
    return (grad_query.reshape(length, heads, HD), grad_key, grad_value)


def body(tokens, segments, w_query, w_key, w_value, w_out, w_gate, w_up, w_down, cotangent):
    seg = segments[0]
    length = seg.shape[0]
    share = tokens.shape[1]
    heads = w_query.shape[1] // HD
    block = min(512, length)
    offset = lax.axis_index("cols") * share
    cos_full, sin_full = rope_tables(doc_positions(seg))
    x_full = spread(tokens).astype(jnp.float32)
    mean1, rstd1 = moments(
        jnp.sum(x_full, 1, keepdims=True), jnp.sum(x_full * x_full, 1, keepdims=True), D
    )
    normed1 = (x_full - mean1) * rstd1
    h1 = normed1.astype(jnp.bfloat16)
    full_query, full_key, full_value, full_gate, full_up = (
        lax.all_gather(w_query, "rows", axis=0, tiled=True),
        lax.all_gather(w_key, "rows", axis=0, tiled=True),
        lax.all_gather(w_value, "rows", axis=0, tiled=True),
        lax.all_gather(w_gate, "rows", axis=0, tiled=True),
        lax.all_gather(w_up, "rows", axis=0, tiled=True),
    )
    full_out, full_down = (
        lax.all_gather(w_out, "rows", axis=1, tiled=True),
        lax.all_gather(w_down, "rows", axis=1, tiled=True),
    )
    query = rotate(
        jnp.dot(h1, full_query, preferred_element_type=jnp.float32).reshape(length, heads, HD),
        cos_full,
        sin_full,
    ).astype(jnp.bfloat16)
    key = rotate(
        jnp.dot(h1, full_key, preferred_element_type=jnp.float32).reshape(length, heads, HD),
        cos_full,
        sin_full,
    ).astype(jnp.bfloat16)
    value = (
        jnp.dot(h1, full_value, preferred_element_type=jnp.float32)
        .astype(jnp.bfloat16)
        .reshape(length, heads, HD)
    )
    mixed, lse = attend(query, key, value, seg, block)
    attn_part = jnp.dot(mixed, full_out, preferred_element_type=jnp.float32)
    resid_full = x_full + whole_sum(attn_part)
    resid = lax.dynamic_slice_in_dim(resid_full, offset, share, 1)
    mean2, rstd2 = moments(
        jnp.sum(resid_full, 1, keepdims=True), jnp.sum(resid_full * resid_full, 1, keepdims=True), D
    )
    normed2 = (resid_full - mean2) * rstd2
    h2 = normed2.astype(jnp.bfloat16)
    gate = jnp.dot(h2, full_gate, preferred_element_type=jnp.float32)
    up = jnp.dot(h2, full_up, preferred_element_type=jnp.float32)
    sigma = jax.nn.sigmoid(gate)
    silu = gate * sigma
    hid = (silu * up).astype(jnp.bfloat16)
    ffn_part = jnp.dot(hid, full_down, preferred_element_type=jnp.float32)
    layer_out = (
        resid
        + lax.psum_scatter(
            ffn_part.astype(jnp.bfloat16), "cols", scatter_dimension=1, tiled=True
        ).astype(jnp.float32)
    ).astype(jnp.bfloat16)
    grad_full = spread(cotangent)
    grad_hid = times_trans(grad_full, full_down)
    down_part = trans_times(hid, grad_full)
    grad_gate = (grad_hid * up * sigma * (1.0 + gate * (1.0 - sigma))).astype(jnp.bfloat16)
    grad_up = (grad_hid * silu).astype(jnp.bfloat16)
    gate_part = trans_times(h2, grad_gate)
    up_part = trans_times(h2, grad_up)
    back_mid = times_trans(grad_gate, full_gate) + times_trans(grad_up, full_up)
    resid_grad_full = grad_full.astype(jnp.float32) + norm_back(
        whole_sum(back_mid), normed2, rstd2, D
    )
    resid_grad = lax.dynamic_slice_in_dim(resid_grad_full, offset, share, 1)
    grad_mix_full = resid_grad_full.astype(jnp.bfloat16)
    out_part = trans_times(mixed, grad_mix_full)
    grad_attn = times_trans(grad_mix_full, full_out).astype(jnp.bfloat16).reshape(length, heads, HD)
    grad_rot_q, grad_rot_k, grad_val = attend_back(query, key, value, grad_attn, lse, seg, block)
    grad_q = (
        unrotate(grad_rot_q, cos_full, sin_full).reshape(length, heads * HD).astype(jnp.bfloat16)
    )
    grad_k = (
        unrotate(grad_rot_k, cos_full, sin_full).reshape(length, heads * HD).astype(jnp.bfloat16)
    )
    grad_v = grad_val.reshape(length, heads * HD).astype(jnp.bfloat16)
    query_part = trans_times(h1, grad_q)
    key_part = trans_times(h1, grad_k)
    value_part = trans_times(h1, grad_v)
    back_in = (
        times_trans(grad_q, full_query)
        + times_trans(grad_k, full_key)
        + times_trans(grad_v, full_value)
    )
    input_back = norm_back(whole_sum(back_in), normed1, rstd1, D)
    grad_input = resid_grad + lax.dynamic_slice_in_dim(input_back, offset, share, 1)
    sum_query, sum_key, sum_value, sum_gate, sum_up = (
        lax.psum_scatter(
            query_part.astype(jnp.bfloat16), "rows", scatter_dimension=0, tiled=True
        ).astype(jnp.float32),
        lax.psum_scatter(
            key_part.astype(jnp.bfloat16), "rows", scatter_dimension=0, tiled=True
        ).astype(jnp.float32),
        lax.psum_scatter(
            value_part.astype(jnp.bfloat16), "rows", scatter_dimension=0, tiled=True
        ).astype(jnp.float32),
        lax.psum_scatter(
            gate_part.astype(jnp.bfloat16), "rows", scatter_dimension=0, tiled=True
        ).astype(jnp.float32),
        lax.psum_scatter(
            up_part.astype(jnp.bfloat16), "rows", scatter_dimension=0, tiled=True
        ).astype(jnp.float32),
    )
    sum_out, sum_down = (
        lax.psum_scatter(
            out_part.astype(jnp.bfloat16), "rows", scatter_dimension=1, tiled=True
        ).astype(jnp.float32),
        lax.psum_scatter(
            down_part.astype(jnp.bfloat16), "rows", scatter_dimension=1, tiled=True
        ).astype(jnp.float32),
    )
    return (
        layer_out,
        grad_input,
        sum_query,
        sum_key,
        sum_value,
        sum_out,
        sum_gate,
        sum_up,
        sum_down,
    )


def solution(mesh):
    in_specs = (
        P("rows", "cols"),
        P("rows", None),
        P("rows", "cols"),
        P("rows", "cols"),
        P("rows", "cols"),
        P("cols", "rows"),
        P("rows", "cols"),
        P("rows", "cols"),
        P("cols", "rows"),
        P("rows", "cols"),
    )
    out_specs = (
        P("rows", "cols"),
        P("rows", "cols"),
        P("rows", "cols"),
        P("rows", "cols"),
        P("rows", "cols"),
        P("cols", "rows"),
        P("rows", "cols"),
        P("rows", "cols"),
        P("cols", "rows"),
    )
    return jax.shard_map(body, mesh=mesh, in_specs=in_specs, out_specs=out_specs, check_vma=False)
```

profile of v0, /device:TPU:0, one launch (start us, length us, event | category | flops | bytes accessed | tf_op | source)
XLA Modules:
  0.0 886.9 jit_solution(5812176209013936590)
XLA Ops:
  14.1 22.1 %all-gather.10.cloned.1.call-done = bf16[256,2048]{1,0:T(8,128)(2,1)} async-done(((bf16[256,256]{1,0:T(8,128)(2,1)}), bf16[256,2048]{1,0:T(8,128)(2,1)}) %all-gather.10.cloned.1.call-update) | async-done | bytes 1048592 | tf_op jit(solution)/shard_map/all_gather | solution.py:68
  39.5 23.9 %all-gather.16.cloned.1.call-done = bf16[2048,256]{1,0:T(8,128)(2,1)} async-done(((bf16[512,256]{1,0:T(8,128)(2,1)}), bf16[2048,256]{1,0:T(8,128)(2,1)}) %all-gather.16.cloned.1.call-update) | async-done | bytes 1048592 | tf_op jit(solution)/shard_map/all_gather | solution.py:161
  65.1 26.6 %all-gather.14.cloned.1.call-done = bf16[2048,256]{1,0:T(8,128)(2,1)} async-done(((bf16[512,256]{1,0:T(8,128)(2,1)}), bf16[2048,256]{1,0:T(8,128)(2,1)}) %all-gather.14.cloned.1.call-update) | async-done | bytes 1048592 | tf_op jit(solution)/shard_map/all_gather | solution.py:160
  94.0 25.9 %all-gather.12.cloned.1.call-done = bf16[2048,256]{1,0:T(8,128)(2,1)} async-done(((bf16[512,256]{1,0:T(8,128)(2,1)}), bf16[2048,256]{1,0:T(8,128)(2,1)}) %all-gather.12.cloned.1.call-update) | async-done | bytes 1048592 | tf_op jit(solution)/shard_map/all_gather | solution.py:162
  122.0 26.0 %all-gather.18.cloned.1.call-done = bf16[256,2048]{1,0:T(8,128)(2,1)} async-done(((bf16[256,512]{1,0:T(8,128)(2,1)}), bf16[256,2048]{1,0:T(8,128)(2,1)}) %all-gather.18.cloned.1.call-update) | async-done | bytes 1048592 | tf_op jit(solution)/shard_map/all_gather | solution.py:167
  153.9 62.4 %all-reduce.4.cloned.1.call-done = f32[256,2048]{1,0:T(8,128)} async-done(((f32[256,2048]{1,0:T(8,128)}), f32[256,2048]{1,0:T(8,128)}) %all-reduce.4.cloned.1.call-update) | async-done | bytes 2097168 | tf_op jit(solution)/shard_map/psum | solution.py:72
  219.8 50.5 %all-gather.22.cloned.1.call-done = bf16[2048,1024]{1,0:T(8,128)(2,1)} async-done(((bf16[512,1024]{1,0:T(8,128)(2,1)}), bf16[2048,1024]{1,0:T(8,128)(2,1)}) %all-gather.22.cloned.1.call-update) | async-done | bytes 4194320 | tf_op jit(solution)/shard_map/all_gather | solution.py:164
  270.3 4.7 fusion.37
  275.1 49.7 %all-gather.20.cloned.1.call-done = bf16[2048,1024]{1,0:T(8,128)(2,1)} async-done(((bf16[512,1024]{1,0:T(8,128)(2,1)}), bf16[2048,1024]{1,0:T(8,128)(2,1)}) %all-gather.20.cloned.1.call-update) | async-done | bytes 4194320 | tf_op jit(solution)/shard_map/all_gather | solution.py:163
  324.8 4.7 fusion.36
  329.5 20.8 %all-gather.26.cloned.1.call-done = bf16[256,2048]{1,0:T(8,128)(2,1)} async-done(((bf16[256,256]{1,0:T(8,128)(2,1)}), bf16[256,2048]{1,0:T(8,128)(2,1)}) %all-gather.26.cloned.1.call-update) | async-done | bytes 1048592 | tf_op jit(solution)/shard_map/all_gather | solution.py:68
  350.3 52.9 %all-gather.24.cloned.1.call-done = bf16[1024,2048]{1,0:T(8,128)(2,1)} async-done(((bf16[1024,512]{1,0:T(8,128)(2,1)}), bf16[1024,2048]{1,0:T(8,128)(2,1)}) %all-gather.24.cloned.1.call-update) | async-done | bytes 4194320 | tf_op jit(solution)/shard_map/all_gather | solution.py:168
  403.2 5.7 multiply_convert_fusion
  414.3 65.0 %all-reduce.6.cloned.1.call-done = f32[256,2048]{1,0:T(8,128)} async-done(((f32[256,2048]{1,0:T(8,128)}), f32[256,2048]{1,0:T(8,128)}) %all-reduce.6.cloned.1.call-update) | async-done | bytes 2097168 | tf_op jit(solution)/shard_map/psum | solution.py:72
  502.9 4.6 convolution_convert_fusion
  517.7 37.5 %all-reduce.8.cloned.1.call-done = f32[256,2048]{1,0:T(8,128)} async-done(((f32[256,2048]{1,0:T(8,128)}), f32[256,2048]{1,0:T(8,128)}) %all-reduce.8.cloned.1.call-update) | async-done | bytes 2097168 | tf_op jit(solution)/shard_map/psum | solution.py:72
  558.6 31.2 %reduce-scatter.9.cloned.1.call-done = bf16[256,256]{1,0:T(8,128)(2,1)} async-done(((bf16[256,2048]{1,0:T(8,128)(2,1)}), bf16[256,256]{1,0:T(8,128)(2,1)}) %reduce-scatter.9.cloned.1.call-update) | async-done | bytes 131088 | tf_op jit(solution)/shard_map/reduce_scatter | solution.py:202
  593.4 25.3 %reduce-scatter.17.cloned.1.call-done = bf16[256,512]{1,0:T(8,128)(2,1)} async-done(((bf16[256,2048]{1,0:T(8,128)(2,1)}), bf16[256,512]{1,0:T(8,128)(2,1)}) %reduce-scatter.17.cloned.1.call-update) | async-done | bytes 262160 | tf_op jit(solution)/shard_map/reduce_scatter | solution.py:257
  620.5 28.9 %reduce-scatter.11.cloned.1.call-done = bf16[512,256]{1,0:T(8,128)(2,1)} async-done(((bf16[2048,256]{1,0:T(8,128)(2,1)}), bf16[512,256]{1,0:T(8,128)(2,1)}) %reduce-scatter.11.cloned.1.call-update) | async-done | bytes 262160 | tf_op jit(solution)/shard_map/reduce_scatter | solution.py:240
  651.2 29.0 %reduce-scatter.15.cloned.1.call-done = bf16[512,256]{1,0:T(8,128)(2,1)} async-done(((bf16[2048,256]{1,0:T(8,128)(2,1)}), bf16[512,256]{1,0:T(8,128)(2,1)}) %reduce-scatter.15.cloned.1.call-update) | async-done | bytes 262160 | tf_op jit(solution)/shard_map/reduce_scatter | solution.py:246
  681.9 28.9 %reduce-scatter.13.cloned.1.call-done = bf16[512,256]{1,0:T(8,128)(2,1)} async-done(((bf16[2048,256]{1,0:T(8,128)(2,1)}), bf16[512,256]{1,0:T(8,128)(2,1)}) %reduce-scatter.13.cloned.1.call-update) | async-done | bytes 262160 | tf_op jit(solution)/shard_map/reduce_scatter | solution.py:243
  712.6 53.7 %reduce-scatter.23.cloned.1.call-done = bf16[1024,512]{1,0:T(8,128)(2,1)} async-done(((bf16[1024,2048]{1,0:T(8,128)(2,1)}), bf16[1024,512]{1,0:T(8,128)(2,1)}) %reduce-scatter.23.cloned.1.call-update) | async-done | bytes 1048592 | tf_op jit(solution)/shard_map/reduce_scatter | solution.py:260
  769.1 52.7 %reduce-scatter.21.cloned.1.call-done = bf16[512,1024]{1,0:T(8,128)(2,1)} async-done(((bf16[2048,1024]{1,0:T(8,128)(2,1)}), bf16[512,1024]{1,0:T(8,128)(2,1)}) %reduce-scatter.21.cloned.1.call-update) | async-done | bytes 1048592 | tf_op jit(solution)/shard_map/reduce_scatter | solution.py:252
  824.6 52.6 %reduce-scatter.19.cloned.1.call-done = bf16[512,1024]{1,0:T(8,128)(2,1)} async-done(((bf16[2048,1024]{1,0:T(8,128)(2,1)}), bf16[512,1024]{1,0:T(8,128)(2,1)}) %reduce-scatter.19.cloned.1.call-update) | async-done | bytes 1048592 | tf_op jit(solution)/shard_map/reduce_scatter | solution.py:249
  (145 shorter events, 86.7 us)
Async XLA Ops:
  7.2 29.0 %all-gather.10.cloned.1.call-start = ((), (), s32[]{:S(2)}) async-start(), calls=%async_computation.8 | async-start | bytes 1179648 | tf_op jit(solution)/shard_map/all_gather | solution.py:68
  7.9 55.4 %all-gather.16.cloned.1.call-start = ((), (), s32[]{:S(2)}) async-start(), calls=%async_computation.11 | async-start | bytes 1310720 | tf_op jit(solution)/shard_map/all_gather | solution.py:161
  8.7 83.1 %all-gather.14.cloned.1.call-start = ((), (), s32[]{:S(2)}) async-start(), calls=%async_computation.10 | async-start | bytes 1310720 | tf_op jit(solution)/shard_map/all_gather | solution.py:160
  9.4 110.5 %all-gather.12.cloned.1.call-start = ((), (), s32[]{:S(2)}) async-start(), calls=%async_computation.9 | async-start | bytes 1310720 | tf_op jit(solution)/shard_map/all_gather | solution.py:162
  10.0 138.0 %all-gather.18.cloned.1.call-start = ((), (), s32[]{:S(2)}) async-start(), calls=%async_computation.12 | async-start | bytes 1310720 | tf_op jit(solution)/shard_map/all_gather | solution.py:167
  10.6 205.7 %all-reduce.4.cloned.1.call-start = ((), (), s32[]{:S(2)}) async-start(), calls=%async_computation.13 | async-start | bytes 4194304 | tf_op jit(solution)/shard_map/psum | solution.py:72
  93.9 28.0 %copy-start.3 = (f32[2,256,256]{1,2,0:T(8,128)}, f32[2,256,256]{1,2,0:T(8,128)S(1)}, u32[]{:S(2)}) copy-start(f32[2,256,256]{1,2,0:T(8,128)S(1)} %get-tuple-element.111) | copy-start | bytes 1572868
  121.7 29.3 %copy-start.15 = (bf16[256,256]{0,1:T(8,128)(2,1)}, bf16[256,256]{0,1:T(8,128)(2,1)S(1)}, u32[]{:S(2)}) copy-start(bf16[256,256]{0,1:T(8,128)(2,1)S(1)} %convolution_convert_fusion.11) | copy-start | bytes 393220
  122.0 29.1 %copy-start.14 = (bf16[2,128,256]{2,1,0:T(8,128)(2,1)}, bf16[2,128,256]{2,1,0:T(8,128)(2,1)S(1)}, u32[]{:S(2)}) copy-start(bf16[2,128,256]{2,1,0:T(8,128)(2,1)S(1)} %convolution_convert_fusion.9) | copy-start | bytes 393220
  151.1 119.3 %all-gather.22.cloned.1.call-start = ((), (), s32[]{:S(2)}) async-start(), calls=%async_computation.15 | async-start | bytes 5242880 | tf_op jit(solution)/shard_map/all_gather | solution.py:164
  151.8 173.0 %all-gather.20.cloned.1.call-start = ((), (), s32[]{:S(2)}) async-start(), calls=%async_computation.14 | async-start | bytes 5242880 | tf_op jit(solution)/shard_map/all_gather | solution.py:163
  152.6 197.7 %all-gather.26.cloned.1.call-start = ((), (), s32[]{:S(2)}) async-start(), calls=%async_computation.18 | async-start | bytes 1179648 | tf_op jit(solution)/shard_map/all_gather | solution.py:68
  153.3 249.9 %all-gather.24.cloned.1.call-start = ((), (), s32[]{:S(2)}) async-start(), calls=%async_computation.16 | async-start | bytes 5242880 | tf_op jit(solution)/shard_map/all_gather | solution.py:168
  153.9 325.5 %all-reduce.6.cloned.1.call-start = ((), (), s32[]{:S(2)}) async-start(), calls=%async_computation.19 | async-start | bytes 4194304 | tf_op jit(solution)/shard_map/psum | solution.py:72
  414.1 141.1 %all-reduce.8.cloned.1.call-start = ((), (), s32[]{:S(2)}) async-start(), calls=%async_computation.20 | async-start | bytes 4194304 | tf_op jit(solution)/shard_map/psum | solution.py:72
  490.3 99.5 %reduce-scatter.9.cloned.1.call-start = ((), (), s32[]{:S(2)}) async-start(), calls=%async_computation.17 | async-start | bytes 1179648 | tf_op jit(solution)/shard_map/reduce_scatter | solution.py:202
  495.0 123.7 %reduce-scatter.17.cloned.1.call-start = ((), (), s32[]{:S(2)}) async-start(), calls=%async_computation.24 | async-start | bytes 1310720 | tf_op jit(solution)/shard_map/reduce_scatter | solution.py:257
  498.2 151.2 %reduce-scatter.11.cloned.1.call-start = ((), (), s32[]{:S(2)}) async-start(), calls=%async_computation.21 | async-start | bytes 1310720 | tf_op jit(solution)/shard_map/reduce_scatter | solution.py:240
  499.7 180.4 %reduce-scatter.15.cloned.1.call-start = ((), (), s32[]{:S(2)}) async-start(), calls=%async_computation.23 | async-start | bytes 1310720 | tf_op jit(solution)/shard_map/reduce_scatter | solution.py:246
  501.3 209.5 %reduce-scatter.13.cloned.1.call-start = ((), (), s32[]{:S(2)}) async-start(), calls=%async_computation.22 | async-start | bytes 1310720 | tf_op jit(solution)/shard_map/reduce_scatter | solution.py:243
  502.8 263.4 %reduce-scatter.23.cloned.1.call-start = ((), (), s32[]{:S(2)}) async-start(), calls=%async_computation.27 | async-start | bytes 5242880 | tf_op jit(solution)/shard_map/reduce_scatter | solution.py:260
  507.6 314.3 %reduce-scatter.21.cloned.1.call-start = ((), (), s32[]{:S(2)}) async-start(), calls=%async_computation.26 | async-start | bytes 5242880 | tf_op jit(solution)/shard_map/reduce_scatter | solution.py:252
  513.1 364.1 %reduce-scatter.19.cloned.1.call-start = ((), (), s32[]{:S(2)}) async-start(), calls=%async_computation.25 | async-start | bytes 5242880 | tf_op jit(solution)/shard_map/reduce_scatter | solution.py:249
  517.7 37.5 %copy-start.2 = (bf16[256,2048]{1,0:T(8,128)(2,1)S(1)}, bf16[256,2048]{1,0:T(8,128)(2,1)}, u32[]{:S(2)}) copy-start(bf16[256,2048]{1,0:T(8,128)(2,1)} %all-gather.10.cloned.1.call-done) | copy-start | bytes 3145732
  (16 other events, 29.5 us)
Sparse Core Ops, SparseCore 0:
  9.6 26.5 all-gather.9
  38.1 25.2 all-gather.15
  65.2 26.4 all-gather.13
  93.4 26.4 all-gather.11
  121.6 26.3 all-gather.17
  151.2 65.0 all-reduce.3
  218.1 52.1 all-gather.21
  272.2 52.5 all-gather.19
  326.4 23.8 all-gather.25
  352.0 51.1 all-gather.23
  414.2 65.0 all-reduce.5
  490.4 64.7 all-reduce.7
  557.5 32.2 reduce-scatter.8
  592.5 26.0 reduce-scatter.16
  621.4 27.9 reduce-scatter.10
  652.1 27.9 reduce-scatter.14
  682.9 27.9 reduce-scatter.12
  713.6 52.5 reduce-scatter.22
  769.2 52.5 reduce-scatter.20
  824.6 52.5 reduce-scatter.18
where the time goes:
time: 888 us; the launch traced here: 887 us
  waiting for transfers between devices  772 us (87%)
  matrix products  57.4 us (6%)
  other arithmetic  36 us (4%)
  between operations  14.7 us (2%)
    psum x3, waiting for transfers between devices, whole_sum(): return lax.psum(part, 'cols')  165 us
    reduce_scatter x1, waiting for transfers between devices, body(): lax.psum_scatter(down_part.astype(jnp.bfloat16), 'rows', scatter_dimensio...  53.7 us
    all_gather x1, waiting for transfers between devices, body(): lax.all_gather(w_down, 'rows', axis=1, tiled=True)  52.9 us
    reduce_scatter x1, waiting for transfers between devices, body(): lax.psum_scatter(up_part.astype(jnp.bfloat16), 'rows', scatter_dimension=...  52.7 us
    reduce_scatter x1, waiting for transfers between devices, body(): lax.psum_scatter(gate_part.astype(jnp.bfloat16), 'rows', scatter_dimensio...  52.6 us
    all_gather x1, waiting for transfers between devices, body(): lax.all_gather(w_up, 'rows', axis=0, tiled=True)  50.5 us
    all_gather x1, waiting for transfers between devices, body(): lax.all_gather(w_gate, 'rows', axis=0, tiled=True)  49.7 us
    all_gather x2, waiting for transfers between devices, spread(): return lax.all_gather(block, 'cols', axis=1, tiled=True)  42.9 us
  transfers between devices with their start and end apart: 20, of which 20 were waited for; matrix products, arithmetic and copies ran while one was open for 8% of the time, Pallas kernels for 0%

commit v1 on v0

v1 whole, which is shorter than its diff:
```python
import functools
import jax
import jax.numpy as jnp
import numpy as np
from jax import lax
from jax.experimental import pallas as pl
from jax.experimental.pallas import tpu as pltpu
from jax.sharding import PartitionSpec as P

HD = 128
EPS = 1e-05
NEG = -1e30
BASE = 10000.0
F32 = jnp.float32
BF = jnp.bfloat16
MESH = pl.DeviceIdType.MESH


def nn(a, b):
    return jnp.dot(a, b, preferred_element_type=F32)


def nt(a, b):
    return lax.dot_general(a, b, (((1,), (1,)), ((), ())), preferred_element_type=F32)


def tn(a, b):
    return lax.dot_general(a, b, (((0,), (0,)), ((), ())), preferred_element_type=F32)


def at(start, size, step=None):
    return pl.ds(pl.multiple_of(start, step or size), size)


class Net:
    def __init__(self, send, recv):
        self.send, self.recv, self.all = send, recv, []

    def __call__(self, src, dst, **peer):
        i = len(self.all)
        c = pltpu.make_async_remote_copy(
            src_ref=src, dst_ref=dst, send_sem=self.send.at[i], recv_sem=self.recv.at[i],
            device_id=peer, device_id_type=MESH)
        c.start()
        self.all.append(c)
        return c

    def drain(self):
        for c in self.all:
            c.wait_send()


class Local:
    def __init__(self, sem):
        self.sem, self.n = sem, 0

    def __call__(self, src, dst):
        c = pltpu.make_async_copy(src, dst, self.sem.at[self.n])
        self.n += 1
        c.start()
        return c


def step_kernel(g, *refs):
    (tok, cot, segr, segc, freq, wq, wk, wv, wo, wg, wu, wd,
     o_out, gi_out, h1w_out, gw_out, h2w_out, dg_out, du_out, hd_out, dqkv_out, go_out,
     xb, h1, xtl, gtl, h1w, gw, h2w, h2t, wqf, wkf, wvf, wof, wgv, wuv, wdv,
     p1, p1a, p1s, p1r, p2, p2a, p2s, p2r, p3, p3a, p3s, p3r, p4, p4a, p4s, p4r,
     x1, n2, dhs, dhr, dho, gus, gur, guo, hda, dga, dua, dh2s, dh2t, dxt, dmt, dmix,
     qb, kb, vb, att, lse, cosb, sinb, mskb, dqkv, gop, gor, fs, ft, lot, git, lob, gib,
     send, recv, loc) = refs
    R, C, L, TL, D, DR, DC, HC, H = (g[k] for k in ("R", "C", "L", "TL", "D", "DR", "DC", "HC", "H"))
    Z = C // 2
    r = lax.axis_index("rows")
    c = lax.axis_index("cols")
    z = c // 2
    core = c % 2
    net = Net(send, recv)
    local = Local(loc)
    scale = HD ** (-0.5)
    my_tl = at(c * TL, TL)

    bar = pltpu.get_barrier_semaphore()
    for k in range(1, R):
        pl.semaphore_signal(bar, inc=1, device_id={"rows": r ^ k}, device_id_type=MESH)
    for k in range(1, C):
        pl.semaphore_signal(bar, inc=1, device_id={"cols": c ^ k}, device_id_type=MESH)

    lx = local(tok, xb.at[:, at(c * DC, DC)])
    lg = local(cot.at[my_tl, :], gtl.at[:, at(c * DC, DC)])
    lws = [local(wq, wqf.at[at(r * DR, DR), :]), local(wk, wkf.at[at(r * DR, DR), :]),
           local(wv, wvf.at[at(r * DR, DR), :]), local(wo, wof.at[:, at(r * DR, DR)])]
    lff = [local(wd, wdv), local(wg, wgv), local(wu, wuv)]

    pl.semaphore_wait(bar, R + C - 2)

    def rows_gather(src, dst):
        return [net(src, dst, rows=r ^ k) for k in range(1, R)]

    def cols_start(blk):
        zs = [net(blk(c), blk(c), cols=c ^ (2 * m)) for m in range(1, Z)]
        return zs, net(blk(c), blk(c), cols=c ^ 1)

    def cols_forward(blk, zs):
        fw = []
        for m in range(1, Z):
            zs[m - 1].wait_recv()
            fw.append(net(blk(c ^ (2 * m)), blk(c ^ (2 * m)), cols=c ^ 1))
        return fw

    def cols_finish(own, fw):
        own.wait_recv()
        for f in fw:
            f.wait_recv()

    def xblk(j):
        return xb.at[:, at(j * DC, DC)]

    xz = [net(tok, xblk(c), cols=c ^ (2 * m)) for m in range(1, Z)]
    xp = net(tok, xblk(c), cols=c ^ 1)
    ga = [net(cot.at[at((c ^ k) * TL, TL), :], gtl.at[:, at(c * DC, DC)], cols=c ^ k) for k in range(1, C)]
    cq = rows_gather(wq, wqf.at[at(r * DR, DR), :])
    ck = rows_gather(wk, wkf.at[at(r * DR, DR), :])

    sr = jnp.broadcast_to(segr[...], (L, L))
    sc = jnp.broadcast_to(segc[...][:, :1], (L, L))
    qi = lax.broadcasted_iota(jnp.int32, (L, L), 0)
    ki = lax.broadcasted_iota(jnp.int32, (L, L), 1)
    ok = (sr == sc) & (qi >= ki)
    okf = jnp.where(ok, 1.0, 0.0)
    mskb[...] = jnp.where(ok, 0.0, NEG)
    pos = jnp.sum(okf, 1, keepdims=True) - 1.0
    angle = pos * freq[...]
    lane = lax.broadcasted_iota(jnp.int32, (L, HD), 1)
    cosb[...] = jnp.cos(angle)
    sn = jnp.sin(angle)
    sinb[...] = jnp.where(lane < HD // 2, -sn, sn)

    lx.wait()
    xf = cols_forward(xblk, xz)
    cols_finish(xp, xf)

    def stats(v):
        mean = jnp.sum(v, 1, keepdims=True) / D
        sq = jnp.sum(v * v, 1, keepdims=True) / D
        return mean, lax.rsqrt(sq - mean * mean + EPS)

    def norm_rows(i, _):
        rows = at(i * 32, 32)
        v = xb[rows, :].astype(F32)
        mean, rstd = stats(v)
        h1[rows, :] = ((v - mean) * rstd).astype(BF)
        return 0

    lax.fori_loop(0, L // 32, norm_rows, 0)

    lg.wait()
    for k in ga:
        k.wait_recv()

    def to_ws(src, dst):
        cps = [net(src.at[:, at((r ^ k) * DR, DR)], dst.at[r, my_tl, :], rows=r ^ k) for k in range(1, R)]
        return cps, local(src.at[:, at(r * DR, DR)], dst.at[r, my_tl, :])

    def landed(cl):
        for k in cl[0]:
            k.wait_recv()
        cl[1].wait()

    a_g = to_ws(gtl, gw)
    a_h = to_ws(h1.at[my_tl, :], h1w)
    cv = rows_gather(wv, wvf.at[at(r * DR, DR), :])
    co = rows_gather(wo, wof.at[:, at(r * DR, DR)])

    def wsblk(buf):
        return lambda j: buf.at[:, at(j * TL, TL), :]

    heads = HC // HD

    def rope(v):
        return jnp.concatenate(
            [v[:, h * HD:(h + 1) * HD] * cosb[...]
             + pltpu.roll(v[:, h * HD:(h + 1) * HD], HD // 2, 1) * sinb[...] for h in range(heads)], 1)

    def unrope(v):
        return v * cosb[...] + pltpu.roll(v * sinb[...], HD // 2, 1)

    lws[0].wait()
    for k in cq:
        k.wait_recv()
    qb[...] = rope(nn(h1[...], wqf[...])).astype(BF)
    landed(a_g)
    g_z, g_p = cols_start(wsblk(gw))
    landed(a_h)
    h_z, h_p = cols_start(wsblk(h1w))
    lws[1].wait()
    for k in ck:
        k.wait_recv()
    kb[...] = rope(nn(h1[...], wkf[...])).astype(BF)
    lws[2].wait()
    for k in cv:
        k.wait_recv()
    vb[...] = nn(h1[...], wvf[...]).astype(BF)

    for h in range(heads):
        hs = slice(h * HD, (h + 1) * HD)
        s = nt(qb[:, hs], kb[:, hs]) * scale
        s = jnp.where(mskb[...] < 0.0, NEG, s)
        top = jnp.max(s, 1, keepdims=True)
        e = jnp.exp(s - top)
        tot = jnp.sum(e, 1, keepdims=True)
        lse[:, hs] = jnp.broadcast_to(top + jnp.log(tot), (L, HD))
        att[:, hs] = nn((e / tot).astype(BF), vb[:, hs]).astype(BF)

    def parts_store(dst, val, i=None):
        for j in range(C):
            v = val[j * TL:(j + 1) * TL, :].astype(BF)
            if i is None:
                dst[j % 2, j // 2, :, :] = v
            else:
                dst[j % 2, j // 2, i, :, :] = v

    lws[3].wait()
    for k in co:
        k.wait_recv()
    W1 = min(512, D)
    for n in range(D // W1):
        ns = slice(n * W1, (n + 1) * W1)
        val = nn(att[...], wof[:, ns])
        for j in range(C):
            p1[j % 2, j // 2, :, ns] = val[j * TL:(j + 1) * TL, :].astype(BF)

    def pre(p, pa):
        return net(p.at[1 - core], pa, cols=c ^ 1)

    def zsend(p, pa, ps, pr):
        out = []
        for m in range(1, Z):
            ps[m] = (p[core, z ^ m].astype(F32) + pa[z ^ m].astype(F32)).astype(BF)
            out.append(net(ps.at[m], pr.at[m], cols=c ^ (2 * m)))
        return out

    def zsum(p, pa, pr, cps):
        tot = p[core, z].astype(F32) + pa[z].astype(F32)
        for m in range(1, Z):
            cps[m - 1].wait_recv()
            tot = tot + pr[m].astype(F32)
        return tot

    k1 = pre(p1, p1a)
    g_f = cols_forward(wsblk(gw), g_z)
    k1.wait_recv()
    z1 = zsend(p1, p1a, p1s, p1r)
    h_f = cols_forward(wsblk(h1w), h_z)
    cols_finish(g_p, g_f)
    cols_finish(h_p, h_f)
    lout = [local(gw, gw_out), local(h1w, h1w_out)]

    lff[0].wait()

    def dhid_block(s, put):
        def one(n, _):
            ns = at(n * 256, 256)
            put(ns, nt(gw[s], wdv[ns, :]))
            return 0
        lax.fori_loop(0, wdv.shape[0] // 256, one, 0)

    order = list(range(1, R))
    dh = {}
    for k in order:
        def put(ns, v, k=k):
            dhs[k, :, ns] = v.astype(BF)
        dhid_block(r ^ k, put)
        if k < R - 1:
            dh[k] = net(dhs.at[k], dhr.at[k], rows=r ^ k)

    def put0(ns, v):
        dho[:, ns] = v
    dhid_block(r, put0)

    xv = xb[my_tl, :].astype(F32)
    xm, xr_ = stats(xv)
    xtl[...] = (xv - xm) * xr_
    v = xv + zsum(p1, p1a, p1r, z1)
    x1[...] = v
    mean2, rstd2 = stats(v)
    n2v = (v - mean2) * rstd2
    n2[...] = n2v
    h2t[...] = n2v.astype(BF)
    a_2 = to_ws(h2t, h2w)
    dh[R - 1] = net(dhs.at[R - 1], dhr.at[R - 1], rows=r ^ (R - 1))
    landed(a_2)
    h2_z, h2_p = cols_start(wsblk(h2w))
    lff[1].wait()
    lff[2].wait()
    h2_f = cols_forward(wsblk(h2w), h2_z)
    cols_finish(h2_p, h2_f)
    lout.append(local(h2w, h2w_out))

    FC = wgv.shape[1]
    QN = g["QN"]
    QW = FC // QN
    gu = {}
    for q in range(QN):
        qs = slice(q * QW, (q + 1) * QW)
        for k in order + [0]:
            ga_ = nn(h2w[r ^ k], wgv[:, qs])
            up_ = nn(h2w[r ^ k], wuv[:, qs])
            if k:
                gus[k, q, 0] = ga_.astype(BF)
                gus[k, q, 1] = up_.astype(BF)
                gu[k, q] = net(gus.at[k, q], gur.at[k, q], rows=r ^ k)
            else:
                guo[q, 0] = ga_
                guo[q, 1] = up_

    for k in order:
        dh[k].wait_recv()
    dgu, hdc = {}, {}
    for q in range(QN):
        for k in order:
            gu[k, q].wait_recv()

        def act(i, _, q=q):
            rows = at(i * 32, 32)
            gate, up = guo[q, 0, rows, :], guo[q, 1, rows, :]
            dhid = dho[rows, q * QW:(q + 1) * QW]
            for k in order:
                gate = gate + gur[k, q, 0, rows, :].astype(F32)
                up = up + gur[k, q, 1, rows, :].astype(F32)
                dhid = dhid + dhr[k, rows, q * QW:(q + 1) * QW].astype(F32)
            sig = 1.0 / (1.0 + jnp.exp(-gate))
            silu = gate * sig
            hda[q, r, rows, :] = (silu * up).astype(BF)
            dga[q, r, rows, :] = (dhid * up * sig * (1.0 + gate * (1.0 - sig))).astype(BF)
            dua[q, r, rows, :] = (dhid * silu).astype(BF)
            return 0
        lax.fori_loop(0, L // 32, act, 0)
        for k in order:
            dgu[k, q, 0] = net(dga.at[q, r], dga.at[q, r], rows=r ^ k)
            dgu[k, q, 1] = net(dua.at[q, r], dua.at[q, r], rows=r ^ k)
    for k in order[:-1]:
        for q in range(QN):
            hdc[k, q] = net(hda.at[q, r], hda.at[q, r], rows=r ^ k)

    k2 = {}

    def dh2_block(k):
        s = r ^ k
        tot = None
        for q in range(QN):
            qs = slice(q * QW, (q + 1) * QW)
            t = nt(dga[q, s], wgv[:, qs]) + nt(dua[q, s], wuv[:, qs])
            tot = t if tot is None else tot + t
        for j in range(C):
            p2[j % 2, k, j // 2] = tot[j * TL:(j + 1) * TL, :].astype(BF)
        k2[k] = net(p2.at[1 - core, k], p2a.at[k], cols=c ^ 1)

    dh2_block(0)
    z2 = {}

    def z2_send(k):
        k2[k].wait_recv()
        for m in range(1, Z):
            p2s[k, m] = (p2[core, k, z ^ m].astype(F32) + p2a[k, z ^ m].astype(F32)).astype(BF)
            z2[k, m] = net(p2s.at[k, m], p2r.at[k, m], cols=c ^ (2 * m))

    for n, k in enumerate(order):
        for q in range(QN):
            dgu[k, q, 0].wait_recv()
            dgu[k, q, 1].wait_recv()
        dh2_block(k)
        z2_send(n)
    z2_send(R - 1)
    lout += [local(dga, dg_out), local(dua, du_out)]

    a_d = []
    for k in range(R):
        tot = p2[core, k, z].astype(F32) + p2a[k, z].astype(F32)
        for m in range(1, Z):
            z2[k, m].wait_recv()
            tot = tot + p2r[k, m].astype(F32)
        dh2s[k] = tot
        if k:
            a_d.append(net(dh2s.at[k], dh2t.at[:, at(r * DR, DR)], rows=r ^ k))
        else:
            l_d = local(dh2s.at[0], dh2t.at[:, at(r * DR, DR)])
    for q in range(QN):
        k = order[-1]
        hdc[k, q] = net(hda.at[q, r], hda.at[q, r], rows=r ^ k)
    l_d.wait()
    for k in a_d:
        k.wait_recv()

    def norm_back(grad, normed, rstd):
        a = jnp.sum(grad, 1, keepdims=True) / D
        b = jnp.sum(grad * normed, 1, keepdims=True) / D
        return rstd * (grad - a - normed * b)

    _, rstd2b = stats(x1[...])
    dxv = gtl[...].astype(F32) + norm_back(dh2t[...], n2[...], rstd2b)
    dxt[...] = dxv
    dmt[...] = dxv.astype(BF)
    l_m = local(dmt, dmix.at[my_tl, :])

    def dblk(j):
        return dmix.at[at(j * TL, TL), :]
    m_z = [net(dmt, dblk(c), cols=c ^ (2 * m)) for m in range(1, Z)]
    m_p = net(dmt, dblk(c), cols=c ^ 1)

    for k in order:
        for q in range(QN):
            if k != order[-1]:
                hdc[k, q].wait_recv()

    def ffn_block(k):
        s = r ^ k
        tot = None
        for q in range(QN):
            t = nn(hda[q, s], wdv[q * QW:(q + 1) * QW, :])
            tot = t if tot is None else tot + t
        for j in range(C):
            p3[j % 2, j // 2, k] = tot[j * TL:(j + 1) * TL, :].astype(BF)

    for k in range(R - 1):
        ffn_block(k)
    m_f = cols_forward(dblk, m_z)
    l_m.wait()
    cols_finish(m_p, m_f)

    da = nt(dmix[...], wof[...]).astype(BF)
    for h in range(heads):
        hs = slice(h * HD, (h + 1) * HD)
        s = nt(qb[:, hs], kb[:, hs]) * scale
        s = jnp.where(mskb[...] < 0.0, NEG, s)
        pr = jnp.exp(s - lse[:, h * HD:h * HD + 1])
        dp = nt(da[:, hs], vb[:, hs])
        inner = jnp.sum(pr * dp, 1, keepdims=True)
        ds = (pr * (dp - inner)).astype(BF)
        dqkv[0, r, :, hs] = unrope(nn(ds, kb[:, hs]) * scale).astype(BF)
        dqkv[1, r, :, hs] = unrope(tn(ds, qb[:, hs]) * scale).astype(BF)
        dqkv[2, r, :, hs] = tn(pr.astype(BF), da[:, hs]).astype(BF)
    cd = [net(dqkv.at[i, r], dqkv.at[i, r], rows=r ^ k) for k in order for i in range(3)]

    for n in range(D // W1):
        ns = slice(n * W1, (n + 1) * W1)
        val = (nt(dqkv[0, r], wqf[ns, :]) + nt(dqkv[1, r], wkf[ns, :]) + nt(dqkv[2, r], wvf[ns, :]))
        for j in range(C):
            p4[j % 2, j // 2, :, ns] = val[j * TL:(j + 1) * TL, :].astype(BF)
    k4 = pre(p4, p4a)
    for s in range(R):
        gop[s] = tn(att[...], dmix[:, s * DR:(s + 1) * DR]).astype(BF)
    cgo = [net(gop.at[r ^ k], gor.at[r], rows=r ^ k) for k in order]
    l_go = local(gop.at[r], gor.at[r])
    k4.wait_recv()
    z4 = zsend(p4, p4a, p4s, p4r)

    for q in range(QN):
        hdc[order[-1], q].wait_recv()
    ffn_block(R - 1)
    lout.append(local(hda, hd_out))
    k3 = pre(p3, p3a)
    k3.wait_recv()
    z3 = zsend(p3, p3a, p3s, p3r)

    _, rstd1 = stats(xb[my_tl, :].astype(F32))
    git[...] = dxt[...] + norm_back(zsum(p4, p4a, p4r, z4), xtl[...], rstd1)

    def to_io(src, dst):
        cps = [net(src.at[:, at((c ^ k) * DC, DC)], dst.at[my_tl, :], cols=c ^ k) for k in range(1, C)]
        return cps, local(src.at[:, at(c * DC, DC)], dst.at[my_tl, :])

    i_g = to_io(git, gib)
    fs[...] = zsum(p3, p3a, p3r, z3)
    a_f = [net(fs.at[k], ft.at[:, at(r * DR, DR)], rows=r ^ k) for k in order]
    l_f = local(fs.at[0], ft.at[:, at(r * DR, DR)])
    l_f.wait()
    for k in a_f:
        k.wait_recv()
    lot[...] = (x1[...] + ft[...]).astype(BF)
    i_o = to_io(lot, lob)
    landed(i_g)
    lout.append(local(gib, gi_out))
    for k in cd:
        k.wait_recv()
    lout.append(local(dqkv, dqkv_out))
    l_go.wait()
    for k in cgo:
        k.wait_recv()
    lout.append(local(gor, go_out))
    landed(i_o)
    lout.append(local(lob, o_out))
    net.drain()
    for k in lout:
        k.wait()


def body(R, C, tokens, segments, w_query, w_key, w_value, w_out, w_gate, w_up, w_down, cotangent):
    L, DC = tokens.shape
    DR, HC = w_query.shape
    D = DR * R
    FC = w_gate.shape[1]
    TL = L // C
    Z = C // 2
    QN = 4 if FC % 1024 == 0 else 2
    QW = FC // QN
    g = dict(R=R, C=C, L=L, TL=TL, D=D, DR=DR, DC=DC, HC=HC, H=FC, QN=QN)
    half = HD // 2
    fr = (BASE ** (-(np.arange(half, dtype=np.float32) * np.float32(2.0)) / np.float32(HD))).astype(np.float32)
    freq = jnp.asarray(np.concatenate([fr, fr])[None, :])
    segc = jnp.broadcast_to(segments.reshape(L, 1), (L, 128))
    S = jax.ShapeDtypeStruct
    V = pltpu.VMEM
    outs = [
        S((L, DC), BF), S((L, DC), F32), S((R, L, DR), BF), S((R, L, DR), BF), S((R, L, DR), BF),
        S((QN, R, L, QW), BF), S((QN, R, L, QW), BF), S((QN, R, L, QW), BF),
        S((3, R, L, HC), BF), S((R, HC, DR), BF),
    ]
    seq = lambda w: [V((2, Z, TL, w), BF), V((Z, TL, w), BF), V((Z, TL, w), BF), V((Z, TL, w), BF)]
    seq4 = lambda: [V((2, Z, R, TL, DR), BF), V((Z, R, TL, DR), BF), V((Z, R, TL, DR), BF), V((Z, R, TL, DR), BF)]
    seq2 = lambda: [V((2, R, Z, TL, DR), BF), V((R, Z, TL, DR), BF), V((R, Z, TL, DR), BF), V((R, Z, TL, DR), BF)]
    scratch = [
        V((L, D), BF), V((L, D), BF), V((TL, D), F32), V((TL, D), BF),
        V((R, L, DR), BF), V((R, L, DR), BF), V((R, L, DR), BF), V((TL, D), BF),
        V((D, HC), BF), V((D, HC), BF), V((D, HC), BF), V((HC, D), BF),
        V((DR, FC), BF), V((DR, FC), BF), V((FC, DR), BF),
        *seq(D), *seq2(), *seq4(), *seq(D),
        V((TL, D), F32), V((TL, D), F32),
        V((R, L, FC), BF), V((R, L, FC), BF), V((L, FC), F32),
        V((R, QN, 2, L, QW), BF), V((R, QN, 2, L, QW), BF), V((QN, 2, L, QW), F32),
        V((QN, R, L, QW), BF), V((QN, R, L, QW), BF), V((QN, R, L, QW), BF),
        V((R, TL, DR), F32), V((TL, D), F32), V((TL, D), F32), V((TL, D), BF), V((L, D), BF),
        V((L, HC), BF), V((L, HC), BF), V((L, HC), BF), V((L, HC), BF), V((L, HC), F32),
        V((L, HD), F32), V((L, HD), F32), V((L, L), F32),
        V((3, R, L, HC), BF), V((R, HC, DR), BF), V((R, HC, DR), BF),
        V((R, TL, DR), F32), V((TL, D), F32), V((TL, D), BF), V((TL, D), F32), V((L, DC), BF), V((L, DC), F32),
        pltpu.SemaphoreType.DMA((g_sems(R, C, QN),)), pltpu.SemaphoreType.DMA((g_sems(R, C, QN),)),
        pltpu.SemaphoreType.DMA((40,)),
    ]
    A = pl.BlockSpec(memory_space=pl.ANY)
    B = pl.BlockSpec(memory_space=pltpu.VMEM)
    res = pl.pallas_call(
        functools.partial(step_kernel, g),
        out_shape=outs,
        in_specs=[A, A, B, B, B] + [A] * 7,
        out_specs=[A] * len(outs),
        scratch_shapes=scratch,
        compiler_params=pltpu.CompilerParams(
            collective_id=0, has_side_effects=True, vmem_limit_bytes=67043328),
        name="layer_step",
    )(tokens, cotangent, segments, segc, freq, w_query, w_key, w_value, w_out, w_gate, w_up, w_down)
    layer_out, grad_in, h1w, gw, h2w, dg, du, hd, dqkv, go = res
    T = R * L
    h1w, gw, h2w = (t.reshape(T, DR) for t in (h1w, gw, h2w))
    gq, gk, gv = (tn(h1w, dqkv[i].reshape(T, HC)) for i in range(3))
    ggate = jnp.einsum("td,qth->dqh", h2w, dg.reshape(QN, T, QW), preferred_element_type=F32).reshape(DR, FC)
    gup = jnp.einsum("td,qth->dqh", h2w, du.reshape(QN, T, QW), preferred_element_type=F32).reshape(DR, FC)
    gdown = jnp.einsum("qth,td->qhd", hd.reshape(QN, T, QW), gw, preferred_element_type=F32).reshape(FC, DR)
    gout = jnp.sum(go.astype(F32), 0)
    return layer_out, grad_in, gq, gk, gv, gout, ggate, gup, gdown


def g_sems(R, C, QN):
    return 12 * (R - 1) + 8 * C + 8 * C + (R - 1) * (12 + 4 * QN) + R * C + 8 * C


def solution(mesh):
    R, C = mesh.shape["rows"], mesh.shape["cols"]
    rc, cr = P("rows", "cols"), P("cols", "rows")
    in_specs = (rc, P("rows", None), rc, rc, rc, cr, rc, rc, cr, rc)
    out_specs = (rc, rc, rc, rc, rc, cr, rc, rc, cr)
    return jax.shard_map(functools.partial(body, R, C), mesh=mesh, in_specs=in_specs,
                         out_specs=out_specs, check_vma=False)
```

time: 888 us -> 309 us (0.35)
  waiting for transfers between devices: 772 us -> 0 us
  Pallas kernels: 0 us -> 279 us
  matrix products: 57.4 us -> 16.7 us
  other arithmetic: 36 us -> 2.37 us
  between operations: 14.7 us -> 0.7 us
    reduce_scatter x8 -> x0, waiting for transfers between devices: 302 us -> none  [the longest x1 53.7 us: body(): lax.psum_scatter(down_part.astype(jnp.bfloat16), 'rows', scatter_dimensio...]
    all_gather x9 -> x0, waiting for transfers between devices: 298 us -> none  [the longest x1 52.9 us: body(): lax.all_gather(w_down, 'rows', axis=1, tiled=True)]
    pallas_call x0 -> x1, Pallas kernels: none -> 279 us  [body(): pl.pallas_call(functools.partial(step_kernel, g), out_shape=outs, in_spec...]
    psum x3 -> x0, waiting for transfers between devices: 165 us -> none  [whole_sum(): return lax.psum(part, 'cols')]
    dot_general x27 -> x6, matrix products: 57.4 us -> 16.7 us  [the longest x1 4.36 us: body(): jnp.einsum('td,qth->dqh', h2w, du.reshape(QN, T, QW), preferred_element_t...]
    convert_element_type x14 -> x0, other arithmetic: 20.3 us -> none  [the longest x5 10.9 us: body(): sum_query, sum_key, sum_value, sum_gate, sum_up = (lax.psum_scatter(query...]
  transfers between devices with their start and end apart: 20 -> 0, of which waited for: 20 -> 0; matrix products, arithmetic and copies ran while one was open for 8% -> 0% of each run, Pallas kernels for 0% -> 0%
where the time goes in v1:
time: 309 us
  Pallas kernels  279 us (90%)
  matrix products  16.7 us (5%)
  local copies, waits for them, and re-layouts  10.1 us (3%)
    pallas_call x1, Pallas kernels, body(): pl.pallas_call(functools.partial(step_kernel, g), out_shape=outs, in_spec...  279 us

profile of v1, /device:TPU:0, one launch (start us, length us, event | category | flops | bytes accessed | tf_op | source)
XLA Modules:
  0.0 308.8 jit_solution(5789361954139607956)
XLA Ops:
  0.6 1.4 broadcast_in_dim.8.refs_3_
  2.1 278.9 %layer_step.1 = (bf16[256,256]{1,0:T(8,128)(2,1)}, f32[256,256]{1,0:T(8,128)}, bf16[4,256,512]{2,1,0:T(8,128)(2,1)}, bf16[4,256,512]{2,1,0:T(8,128)(2,1)}, bf16[...) custom-call(bf16[256,256]{1,0:T(8,128)(2,1)} %refs_0_.1, ...), custom_call_target="tpu_custom_call" | custom-call | tf_op jit(solution)/shard_map/layer_step/pallas_call | solution.py:542
  281.0 0.0 copy-start.3
  281.0 0.0 copy-start.8
  281.0 2.4 convert_reduce_fusion
  283.3 0.0 copy-done.3
  283.3 0.1 fusion
  283.5 0.0 copy-done.8
  283.5 1.3 fusion.3
  284.7 1.3 fusion.2
  286.0 1.3 fusion.1
  287.3 0.0 copy-done.2
  287.3 2.4 copy.20
  289.6 0.0 copy-done.7
  289.6 4.4 %fusion.4 = f32[512,1024]{1,0:T(8,128)} fusion(bf16[1024,512]{1,0:T(8,128)(2,1)S(1)} %bitcast.42, bf16[1024,1024]{1,0:T(8,128)(2,1)} %bitcast.36), kind=kOutput, calls=%fused_computation.5 | convolution fusion | flops 1073741824 | bytes 5242880 | tf_op jit(solution)/shard_map/td,qth->dqh/dot_general | solution.py:556
  294.0 0.0 copy-done.1
  294.0 2.4 copy.21
  296.4 4.4 %fusion.5 = f32[512,1024]{1,0:T(8,128)} fusion(bf16[1024,512]{1,0:T(8,128)(2,1)S(1)} %bitcast.43, bf16[1024,1024]{1,0:T(8,128)(2,1)} %bitcast.34), kind=kOutput, calls=%fused_computation.6 | convolution fusion | flops 1073741824 | bytes 5242880 | tf_op jit(solution)/shard_map/td,qth->dqh/dot_general | solution.py:557
  300.7 0.0 copy-done
  300.7 2.5 copy.22
  303.2 0.0 copy-done.6
  303.2 4.2 %fusion.6 = f32[1024,512]{1,0:T(8,128)} fusion(bf16[1024,1024]{1,0:T(8,128)(2,1)} %bitcast.35, bf16[1024,512]{1,0:T(8,128)(2,1)S(1)} %bitcast.41), kind=kOutput, calls=%fused_computation.7 | convolution fusion | flops 1073741824 | bytes 5242880 | tf_op jit(solution)/shard_map/qth,td->qhd/dot_general | solution.py:558
  307.4 0.7 copy.25
  308.1 0.7 copy.26
  (9 shorter events, 0.0 us)
Async XLA Ops:
  281.0 2.4 copy-start.3
  281.0 2.5 copy-start.8
  284.7 2.5 copy-start.2
  287.3 2.4 copy-start.7
  289.6 4.4 %copy-start.1 = (bf16[4,4,256,256]{3,2,1,0:T(8,128)(2,1)S(1)}, bf16[4,4,256,256]{3,2,1,0:T(8,128)(2,1)}, u32[]{:S(2)}) copy-start(bf16[4,4,256,256]{3,2,1,0:T(8,128)(2,1)} %get-tuple-element.26) | copy-start | bytes 6291460
  296.4 4.4 %copy-start = (bf16[4,4,256,256]{3,2,1,0:T(8,128)(2,1)S(1)}, bf16[4,4,256,256]{3,2,1,0:T(8,128)(2,1)}, u32[]{:S(2)}) copy-start(bf16[4,4,256,256]{3,2,1,0:T(8,128)(2,1)} %get-tuple-element.27) | copy-start | bytes 6291460
  300.7 2.5 copy-start.6
  303.2 4.2 %copy-start.5 = (bf16[256,256]{1,0:T(8,128)(2,1)S(1)}, bf16[256,256]{1,0:T(8,128)(2,1)}, u32[]{:S(2)}) copy-start(bf16[256,256]{1,0:T(8,128)(2,1)} %get-tuple-element.41) | copy-start | bytes 393220
  303.2 4.9 %copy-start.4 = (f32[256,256]{1,0:T(8,128)S(1)}, f32[256,256]{1,0:T(8,128)}, u32[]{:S(2)}) copy-start(f32[256,256]{1,0:T(8,128)} %get-tuple-element.42) | copy-start | bytes 786436

commit v2 on v1

--- a/solution.py
+++ b/solution.py
@@ -42,32 +42,53 @@
             src_ref=src, dst_ref=dst, send_sem=self.send.at[i], recv_sem=self.recv.at[i],
             device_id=peer, device_id_type=MESH)
         c.start()
-        self.all.append(c)
-        return c
+        self.all.append(Copy(c))
+        return self.all[-1]
 
     def drain(self):
         for c in self.all:
-            c.wait_send()
+            c.c.wait_send()
+
+
+class Copy:
+    def __init__(self, c):
+        self.c, self.open = c, True
+
+    def wait_recv(self):
+        if self.open:
+            self.c.wait_recv()
+        self.open = False
+
+
+class LCopy:
+    def __init__(self, c):
+        self.c, self.open = c, True
+
+    def wait(self):
+        if self.open:
+            self.c.wait()
+        self.open = False
 
 
 class Local:
     def __init__(self, sem):
-        self.sem, self.n = sem, 0
+        self.sem, self.n, self.all = sem, 0, []
 
     def __call__(self, src, dst):
         c = pltpu.make_async_copy(src, dst, self.sem.at[self.n])
         self.n += 1
         c.start()
-        return c
+        self.all.append(LCopy(c))
+        return self.all[-1]
 
 
 def step_kernel(g, *refs):
-    (tok, cot, segr, segc, freq, wq, wk, wv, wo, wg, wu, wd,
+    (tok, cot, segr, freq, wq, wk, wv, wo, wg, wu, wd,
      o_out, gi_out, h1w_out, gw_out, h2w_out, dg_out, du_out, hd_out, dqkv_out, go_out,
      xb, h1, xtl, gtl, h1w, gw, h2w, h2t, wqf, wkf, wvf, wof, wgv, wuv, wdv,
      p1, p1a, p1s, p1r, p2, p2a, p2s, p2r, p3, p3a, p3s, p3r, p4, p4a, p4s, p4r,
      x1, n2, dhs, dhr, dho, gus, gur, guo, hda, dga, dua, dh2s, dh2t, dxt, dmt, dmix,
-     qb, kb, vb, att, lse, cosb, sinb, mskb, dqkv, gop, gor, fs, ft, lot, git, lob, gib,
+     qb, kb, vb, att, lse, cosb, sinb, mskb, dqkv, gop, gor, gof, fs, ft, lot, git, lob, gib,
      send, recv, loc) = refs
     R, C, L, TL, D, DR, DC, HC, H = (g[k] for k in ("R", "C", "L", "TL", "D", "DR", "DC", "HC", "H"))
     Z = C // 2
@@ -122,8 +143,8 @@
     cq = rows_gather(wq, wqf.at[at(r * DR, DR), :])
     ck = rows_gather(wk, wkf.at[at(r * DR, DR), :])
 
-    sr = jnp.broadcast_to(segr[...], (L, L))
-    sc = jnp.broadcast_to(segc[...][:, :1], (L, L))
+    sr = jnp.broadcast_to(segr[...].astype(F32), (L, L))
+    sc = sr.T
     qi = lax.broadcasted_iota(jnp.int32, (L, L), 0)
     ki = lax.broadcasted_iota(jnp.int32, (L, L), 1)
     ok = (sr == sc) & (qi >= ki)
@@ -321,7 +342,9 @@
         for k in order:
             gu[k, q].wait_recv()
 
-        def act(i, _, q=q):
+        qs = slice(q * QW, (q + 1) * QW)
+
+        def act(i, _, q=q, qs=qs):
             rows = at(i * 32, 32)
             gate, up = guo[q, 0, rows, :], guo[q, 1, rows, :]
             dhid = dho[rows, q * QW:(q + 1) * QW]
@@ -331,27 +354,22 @@
                 dhid = dhid + dhr[k, rows, q * QW:(q + 1) * QW].astype(F32)
             sig = 1.0 / (1.0 + jnp.exp(-gate))
             silu = gate * sig
-            hda[q, r, rows, :] = (silu * up).astype(BF)
-            dga[q, r, rows, :] = (dhid * up * sig * (1.0 + gate * (1.0 - sig))).astype(BF)
-            dua[q, r, rows, :] = (dhid * silu).astype(BF)
+            hda[r, rows, qs] = (silu * up).astype(BF)
+            dga[r, rows, qs] = (dhid * up * sig * (1.0 + gate * (1.0 - sig))).astype(BF)
+            dua[r, rows, qs] = (dhid * silu).astype(BF)
             return 0
         lax.fori_loop(0, L // 32, act, 0)
         for k in order:
-            dgu[k, q, 0] = net(dga.at[q, r], dga.at[q, r], rows=r ^ k)
-            dgu[k, q, 1] = net(dua.at[q, r], dua.at[q, r], rows=r ^ k)
+            dgu[k, q, 0] = net(dga.at[r, :, qs], dga.at[r, :, qs], rows=r ^ k)
+            dgu[k, q, 1] = net(dua.at[r, :, qs], dua.at[r, :, qs], rows=r ^ k)
     for k in order[:-1]:
-        for q in range(QN):
-            hdc[k, q] = net(hda.at[q, r], hda.at[q, r], rows=r ^ k)
+        hdc[k] = net(hda.at[r], hda.at[r], rows=r ^ k)
 
     k2 = {}
 
     def dh2_block(k):
         s = r ^ k
-        tot = None
-        for q in range(QN):
-            qs = slice(q * QW, (q + 1) * QW)
-            t = nt(dga[q, s], wgv[:, qs]) + nt(dua[q, s], wuv[:, qs])
-            tot = t if tot is None else tot + t
+        tot = nt(dga[s], wgv[...]) + nt(dua[s], wuv[...])
         for j in range(C):
             p2[j % 2, k, j // 2] = tot[j * TL:(j + 1) * TL, :].astype(BF)
         k2[k] = net(p2.at[1 - core, k], p2a.at[k], cols=c ^ 1)
@@ -385,9 +403,8 @@
             a_d.append(net(dh2s.at[k], dh2t.at[:, at(r * DR, DR)], rows=r ^ k))
         else:
             l_d = local(dh2s.at[0], dh2t.at[:, at(r * DR, DR)])
-    for q in range(QN):
-        k = order[-1]
-        hdc[k, q] = net(hda.at[q, r], hda.at[q, r], rows=r ^ k)
+    k = order[-1]
+    hdc[k] = net(hda.at[r], hda.at[r], rows=r ^ k)
     l_d.wait()
     for k in a_d:
         k.wait_recv()
@@ -408,17 +425,12 @@
     m_z = [net(dmt, dblk(c), cols=c ^ (2 * m)) for m in range(1, Z)]
     m_p = net(dmt, dblk(c), cols=c ^ 1)
 
-    for k in order:
-        for q in range(QN):
-            if k != order[-1]:
-                hdc[k, q].wait_recv()
+    for k in order[:-1]:
+        hdc[k].wait_recv()
 
     def ffn_block(k):
         s = r ^ k
-        tot = None
-        for q in range(QN):
-            t = nn(hda[q, s], wdv[q * QW:(q + 1) * QW, :])
-            tot = t if tot is None else tot + t
+        tot = nn(hda[s], wdv[...])
         for j in range(C):
             p3[j % 2, j // 2, k] = tot[j * TL:(j + 1) * TL, :].astype(BF)
 
@@ -450,13 +462,11 @@
     k4 = pre(p4, p4a)
     for s in range(R):
         gop[s] = tn(att[...], dmix[:, s * DR:(s + 1) * DR]).astype(BF)
-    cgo = [net(gop.at[r ^ k], gor.at[r], rows=r ^ k) for k in order]
-    l_go = local(gop.at[r], gor.at[r])
+    cgo = [net(gop.at[r ^ k], gor.at[k], rows=r ^ k) for k in order]
     k4.wait_recv()
     z4 = zsend(p4, p4a, p4s, p4r)
 
-    for q in range(QN):
-        hdc[order[-1], q].wait_recv()
+    hdc[order[-1]].wait_recv()
     ffn_block(R - 1)
     lout.append(local(hda, hd_out))
     k3 = pre(p3, p3a)
@@ -484,10 +494,13 @@
     for k in cd:
         k.wait_recv()
     lout.append(local(dqkv, dqkv_out))
-    l_go.wait()
     for k in cgo:
         k.wait_recv()
-    lout.append(local(gor, go_out))
+    gsum = gop[r].astype(F32)
+    for k in order:
+        gsum = gsum + gor[k].astype(F32)
+    gof[...] = gsum
+    lout.append(local(gof, go_out))
     landed(i_o)
     lout.append(local(lob, o_out))
     net.drain()
@@ -508,13 +521,12 @@
     half = HD // 2
     fr = (BASE ** (-(np.arange(half, dtype=np.float32) * np.float32(2.0)) / np.float32(HD))).astype(np.float32)
     freq = jnp.asarray(np.concatenate([fr, fr])[None, :])
-    segc = jnp.broadcast_to(segments.reshape(L, 1), (L, 128))
     S = jax.ShapeDtypeStruct
     V = pltpu.VMEM
     outs = [
         S((L, DC), BF), S((L, DC), F32), S((R, L, DR), BF), S((R, L, DR), BF), S((R, L, DR), BF),
-        S((QN, R, L, QW), BF), S((QN, R, L, QW), BF), S((QN, R, L, QW), BF),
-        S((3, R, L, HC), BF), S((R, HC, DR), BF),
+        S((R, L, FC), BF), S((R, L, FC), BF), S((R, L, FC), BF),
+        S((3, R, L, HC), BF), S((HC, DR), F32),
     ]
     seq = lambda w: [V((2, Z, TL, w), BF), V((Z, TL, w), BF), V((Z, TL, w), BF), V((Z, TL, w), BF)]
     seq4 = lambda: [V((2, Z, R, TL, DR), BF), V((Z, R, TL, DR), BF), V((Z, R, TL, DR), BF), V((Z, R, TL, DR), BF)]
@@ -528,11 +540,11 @@
         V((TL, D), F32), V((TL, D), F32),
         V((R, L, FC), BF), V((R, L, FC), BF), V((L, FC), F32),
         V((R, QN, 2, L, QW), BF), V((R, QN, 2, L, QW), BF), V((QN, 2, L, QW), F32),
-        V((QN, R, L, QW), BF), V((QN, R, L, QW), BF), V((QN, R, L, QW), BF),
+        V((R, L, FC), BF), V((R, L, FC), BF), V((R, L, FC), BF),
         V((R, TL, DR), F32), V((TL, D), F32), V((TL, D), F32), V((TL, D), BF), V((L, D), BF),
         V((L, HC), BF), V((L, HC), BF), V((L, HC), BF), V((L, HC), BF), V((L, HC), F32),
         V((L, HD), F32), V((L, HD), F32), V((L, L), F32),
-        V((3, R, L, HC), BF), V((R, HC, DR), BF), V((R, HC, DR), BF),
+        V((3, R, L, HC), BF), V((R, HC, DR), BF), V((R, HC, DR), BF), V((HC, DR), F32),
         V((R, TL, DR), F32), V((TL, D), F32), V((TL, D), BF), V((TL, D), F32), V((L, DC), BF), V((L, DC), F32),
         pltpu.SemaphoreType.DMA((g_sems(R, C, QN),)), pltpu.SemaphoreType.DMA((g_sems(R, C, QN),)),
         pltpu.SemaphoreType.DMA((40,)),
@@ -542,22 +554,19 @@
     res = pl.pallas_call(
         functools.partial(step_kernel, g),
         out_shape=outs,
-        in_specs=[A, A, B, B, B] + [A] * 7,
+        in_specs=[A, A, B, B] + [A] * 7,
         out_specs=[A] * len(outs),
         scratch_shapes=scratch,
         compiler_params=pltpu.CompilerParams(
             collective_id=0, has_side_effects=True, vmem_limit_bytes=67043328),
         name="layer_step",
-    )(tokens, cotangent, segments, segc, freq, w_query, w_key, w_value, w_out, w_gate, w_up, w_down)
+    )(tokens, cotangent, segments, freq, w_query, w_key, w_value, w_out, w_gate, w_up, w_down)
     layer_out, grad_in, h1w, gw, h2w, dg, du, hd, dqkv, go = res
     T = R * L
     h1w, gw, h2w = (t.reshape(T, DR) for t in (h1w, gw, h2w))
     gq, gk, gv = (tn(h1w, dqkv[i].reshape(T, HC)) for i in range(3))
-    ggate = jnp.einsum("td,qth->dqh", h2w, dg.reshape(QN, T, QW), preferred_element_type=F32).reshape(DR, FC)
-    gup = jnp.einsum("td,qth->dqh", h2w, du.reshape(QN, T, QW), preferred_element_type=F32).reshape(DR, FC)
-    gdown = jnp.einsum("qth,td->qhd", hd.reshape(QN, T, QW), gw, preferred_element_type=F32).reshape(FC, DR)
-    gout = jnp.sum(go.astype(F32), 0)
-    return layer_out, grad_in, gq, gk, gv, gout, ggate, gup, gdown
+    ggate, gup, gdown = tn(h2w, dg.reshape(T, FC)), tn(h2w, du.reshape(T, FC)), tn(hd.reshape(T, FC), gw)
+    return layer_out, grad_in, gq, gk, gv, go, ggate, gup, gdown
 
 
 def g_sems(R, C, QN):

time: 309 us -> 295 us (0.955)
  local copies, waits for them, and re-layouts: 10.1 us -> 3.87 us
  matrix products: 16.7 us -> 11.6 us
    dot_general x3 -> x0, matrix products: 12.9 us -> none  [the longest x1 4.36 us: body(): jnp.einsum('td,qth->dqh', h2w, du.reshape(QN, T, QW), preferred_element_t...]
    dot_general x3 -> x6, matrix products: 3.81 us -> 11.6 us  [tn(): lax.dot_general(a, b, (((0,), (0,)), ((), ())), preferred_element_type=F32)]
    reshape x3 -> x0, local copies, waits for them, and re-layouts: 7.22 us -> none  [the longest x1 2.49 us: body(): hd.reshape(QN, T, QW)]
where the time goes in v2:
time: 295 us
  Pallas kernels  279 us (95%)
  matrix products  11.6 us (4%)
  local copies, waits for them, and re-layouts  3.87 us (1%)
    pallas_call x1, Pallas kernels, body(): pl.pallas_call(functools.partial(step_kernel, g), out_shape=outs, in_spec...  279 us
    dot_general x6, matrix products, tn(): lax.dot_general(a, b, (((0,), (0,)), ((), ())), preferred_element_type=F32)  11.6 us

profile of v2, /device:TPU:0, one launch (start us, length us, event | category | flops | bytes accessed | tf_op | source)
XLA Modules:
  0.0 294.8 jit_solution(4932304372200720800)
XLA Ops:
  0.6 278.6 %layer_step.1 = (bf16[256,256]{1,0:T(8,128)(2,1)}, f32[256,256]{1,0:T(8,128)}, bf16[4,256,512]{2,1,0:T(8,128)(2,1)}, bf16[4,256,512]{2,1,0:T(8,128)(2,1)}, bf16[...) custom-call(bf16[256,256]{1,0:T(8,128)(2,1)} %refs_0_.1, ...), custom_call_target="tpu_custom_call" | custom-call | tf_op jit(solution)/shard_map/layer_step/pallas_call | solution.py:554
  279.3 0.0 copy-start.8
  279.3 1.5 fusion
  280.9 0.1 copy-done.8
  281.0 1.3 fusion.3
  282.3 0.0 copy-start
  282.3 0.0 copy-start.2
  282.3 1.3 fusion.2
  283.5 1.3 fusion.1
  284.8 0.0 copy-done
  284.8 0.0 copy-done.2
  284.8 2.6 convolution_bitcast_fusion.2
  287.4 0.0 copy-done.1
  287.4 2.6 convolution_bitcast_fusion.1
  290.0 0.0 copy-done.6
  290.0 0.0 copy-done.7
  290.0 0.0 copy-start.3
  290.0 2.6 convolution_bitcast_fusion
  292.6 0.0 copy-done.5
  292.6 0.7 copy.29
  293.3 0.0 copy-done.4
  293.3 0.7 copy.30
  294.0 0.0 copy-done.3
  294.0 0.8 copy.31
  (5 shorter events, 0.0 us)
Async XLA Ops:
  279.3 1.7 copy-start.8
  282.3 2.5 copy-start
  282.3 2.5 copy-start.2
  284.8 2.6 copy-start.1
  287.4 2.6 copy-start.6
  287.4 2.6 copy-start.7
  290.0 2.6 copy-start.5
  290.0 3.3 %copy-start.4 = (f32[256,256]{1,0:T(8,128)S(1)}, f32[256,256]{1,0:T(8,128)}, u32[]{:S(2)}) copy-start(f32[256,256]{1,0:T(8,128)} %get-tuple-element.42) | copy-start | bytes 786436
  290.0 4.0 %copy-start.3 = (f32[256,512]{1,0:T(8,128)S(1)}, f32[256,512]{1,0:T(8,128)}, u32[]{:S(2)}) copy-start(f32[256,512]{1,0:T(8,128)} %get-tuple-element.46) | copy-start | bytes 1572868

commit v3 on v2

--- a/solution.py
+++ b/solution.py
@@ -38,6 +38,7 @@
 
     def __call__(self, src, dst, **peer):
         i = len(self.all)
+        assert i < self.send.shape[0]
         c = pltpu.make_async_remote_copy(
             src_ref=src, dst_ref=dst, send_sem=self.send.at[i], recv_sem=self.recv.at[i],
             device_id=peer, device_id_type=MESH)
@@ -60,6 +61,53 @@
         self.open = False
 
 
+class Gather:
+    def __init__(self, net, R, r, own, blk):
+        self.net, self.r, self.two, self.blk, self.c = net, r, R == 4, blk, {}
+        todo = [(1, 0), (2, 1), (1, 1), (2, 0)] if self.two else [(k, h) for k in range(1, R) for h in range(2)]
+        for k, h in todo:
+            self.c[k, h] = net(own(h), blk(r, h), rows=r ^ k)
+
+    def forward(self):
+        if self.two:
+            for k, h in ((1, 0), (2, 1)):
+                self.c[k, h].wait_recv()
+                b = self.blk(self.r ^ k, h)
+                self.c[3, h] = self.net(b, b, rows=self.r ^ (3 - k))
+
+    def wait(self, k):
+        for h in range(2):
+            self.c[k, h].wait_recv()
+
+
+class Reduce:
+    def __init__(self, net, R, r, snd, rcv):
+        self.net, self.r, self.two, self.snd, self.rcv, self.c = net, r, R == 4, snd, rcv, {}
+        self.ks = (1, 2) if self.two else tuple(range(1, R))
+        if self.two:
+            for k, h in ((1, 0), (2, 1)):
+                self.c[3, h] = net(snd(3, h), rcv(3, h), rows=r ^ k)
+            for k, h in ((1, 0), (2, 1)):
+                self.c[k, h] = net(snd(k, h), rcv(k, h), rows=r ^ k)
+        else:
+            for k in self.ks:
+                for h in range(2):
+                    self.c[k, h] = net(snd(k, h), rcv(k, h), rows=r ^ k)
+
+    def relay(self):
+        if self.two:
+            for k, h in ((2, 0), (1, 1)):
+                self.c[3, h].wait_recv()
+                a = self.snd(k, h)
+                a[...] = (a[...].astype(F32) + self.rcv(3, h)[...].astype(F32)).astype(BF)
+                self.c[k, h] = self.net(a, self.rcv(k, h), rows=self.r ^ k)
+
+    def wait(self):
+        for k in self.ks:
+            for h in range(2):
+                self.c[k, h].wait_recv()
+
+
 class LCopy:
     def __init__(self, c):
         self.c, self.open = c, True
@@ -87,7 +135,7 @@
      o_out, gi_out, h1w_out, gw_out, h2w_out, dg_out, du_out, hd_out, dqkv_out, go_out,
      xb, h1, xtl, gtl, h1w, gw, h2w, h2t, wqf, wkf, wvf, wof, wgv, wuv, wdv,
      p1, p1a, p1s, p1r, p2, p2a, p2s, p2r, p3, p3a, p3s, p3r, p4, p4a, p4s, p4r,
-     x1, n2, dhs, dhr, dho, gus, gur, guo, hda, dga, dua, dh2s, dh2t, dxt, dmt, dmix,
+     x1, n2, dhs, dhr, dho, gus, gur, guo, hda, dgu, dh2s, dh2t, dxt, dmt, dmix,
      qb, kb, vb, att, lse, cosb, sinb, mskb, dqkv, gop, gor, gof, fs, ft, lot, git, lob, gib,
      send, recv, loc) = refs
     R, C, L, TL, D, DR, DC, HC, H = (g[k] for k in ("R", "C", "L", "TL", "D", "DR", "DC", "HC", "H"))
@@ -115,8 +163,12 @@
 
     pl.semaphore_wait(bar, R + C - 2)
 
-    def rows_gather(src, dst):
-        return [net(src, dst, rows=r ^ k) for k in range(1, R)]
+    def half(n, h):
+        return slice(h * (n // 2), (h + 1) * (n // 2))
+
+    def w_in(w, full):
+        n = DR // 2
+        return Gather(net, R, r, lambda h: w.at[half(DR, h), :], lambda j, h: full.at[at(j * DR + h * n, n), :])
 
     def cols_start(blk):
         zs = [net(blk(c), blk(c), cols=c ^ (2 * m)) for m in range(1, Z)]
@@ -137,11 +189,11 @@
     def xblk(j):
         return xb.at[:, at(j * DC, DC)]
 
+    cq = w_in(wq, wqf)
     xz = [net(tok, xblk(c), cols=c ^ (2 * m)) for m in range(1, Z)]
     xp = net(tok, xblk(c), cols=c ^ 1)
     ga = [net(cot.at[at((c ^ k) * TL, TL), :], gtl.at[:, at(c * DC, DC)], cols=c ^ k) for k in range(1, C)]
-    cq = rows_gather(wq, wqf.at[at(r * DR, DR), :])
-    ck = rows_gather(wk, wkf.at[at(r * DR, DR), :])
+    ck = w_in(wk, wkf)
 
     sr = jnp.broadcast_to(segr[...].astype(F32), (L, L))
     sc = sr.T
@@ -157,8 +209,24 @@
     sn = jnp.sin(angle)
     sinb[...] = jnp.where(lane < HD // 2, -sn, sn)
 
+    def to_ws(src, dst):
+        cps = [net(src.at[:, at((r ^ k) * DR, DR)], dst.at[r, my_tl, :], rows=r ^ k) for k in range(1, R)]
+        return cps, local(src.at[:, at(r * DR, DR)], dst.at[r, my_tl, :])
+
+    def landed(cl):
+        for k in cl[0]:
+            k.wait_recv()
+        cl[1].wait()
+
+    cq.forward()
+    cv = w_in(wv, wvf)
     lx.wait()
     xf = cols_forward(xblk, xz)
+    lg.wait()
+    for k in ga:
+        k.wait_recv()
+    a_g = to_ws(gtl, gw)
+    ck.forward()
     cols_finish(xp, xf)
 
     def stats(v):
@@ -175,23 +243,8 @@
 
     lax.fori_loop(0, L // 32, norm_rows, 0)
 
-    lg.wait()
-    for k in ga:
-        k.wait_recv()
-
-    def to_ws(src, dst):
-        cps = [net(src.at[:, at((r ^ k) * DR, DR)], dst.at[r, my_tl, :], rows=r ^ k) for k in range(1, R)]
-        return cps, local(src.at[:, at(r * DR, DR)], dst.at[r, my_tl, :])
-
-    def landed(cl):
-        for k in cl[0]:
-            k.wait_recv()
-        cl[1].wait()
-
-    a_g = to_ws(gtl, gw)
-    a_h = to_ws(h1.at[my_tl, :], h1w)
-    cv = rows_gather(wv, wvf.at[at(r * DR, DR), :])
-    co = rows_gather(wo, wof.at[:, at(r * DR, DR)])
+    cv.forward()
+    co = Gather(net, R, r, lambda h: wo.at[half(HC, h), :], lambda j, h: wof.at[half(HC, h), at(j * DR, DR)])
 
     def wsblk(buf):
         return lambda j: buf.at[:, at(j * TL, TL), :]
@@ -206,21 +259,20 @@
     def unrope(v):
         return v * cosb[...] + pltpu.roll(v * sinb[...], HD // 2, 1)
 
-    lws[0].wait()
-    for k in cq:
-        k.wait_recv()
-    qb[...] = rope(nn(h1[...], wqf[...])).astype(BF)
+    def arrived(g):
+        for k in range(1, R):
+            g.wait(k)
+
     landed(a_g)
     g_z, g_p = cols_start(wsblk(gw))
-    landed(a_h)
-    h_z, h_p = cols_start(wsblk(h1w))
+    lws[0].wait()
+    arrived(cq)
+    qb[...] = rope(nn(h1[...], wqf[...])).astype(BF)
     lws[1].wait()
-    for k in ck:
-        k.wait_recv()
+    arrived(ck)
     kb[...] = rope(nn(h1[...], wkf[...])).astype(BF)
     lws[2].wait()
-    for k in cv:
-        k.wait_recv()
+    arrived(cv)
     vb[...] = nn(h1[...], wvf[...]).astype(BF)
 
     for h in range(heads):
@@ -241,9 +293,9 @@
             else:
                 dst[j % 2, j // 2, i, :, :] = v
 
+    co.forward()
     lws[3].wait()
-    for k in co:
-        k.wait_recv()
+    arrived(co)
     W1 = min(512, D)
     for n in range(D // W1):
         ns = slice(n * W1, (n + 1) * W1)
@@ -272,32 +324,27 @@
     g_f = cols_forward(wsblk(gw), g_z)
     k1.wait_recv()
     z1 = zsend(p1, p1a, p1s, p1r)
-    h_f = cols_forward(wsblk(h1w), h_z)
     cols_finish(g_p, g_f)
-    cols_finish(h_p, h_f)
-    lout = [local(gw, gw_out), local(h1w, h1w_out)]
+    lout = [local(gw, gw_out)]
 
     lff[0].wait()
-
-    def dhid_block(s, put):
-        def one(n, _):
-            ns = at(n * 256, 256)
-            put(ns, nt(gw[s], wdv[ns, :]))
-            return 0
-        lax.fori_loop(0, wdv.shape[0] // 256, one, 0)
-
     order = list(range(1, R))
-    dh = {}
-    for k in order:
-        def put(ns, v, k=k):
-            dhs[k, :, ns] = v.astype(BF)
-        dhid_block(r ^ k, put)
-        if k < R - 1:
-            dh[k] = net(dhs.at[k], dhr.at[k], rows=r ^ k)
-
-    def put0(ns, v):
-        dho[:, ns] = v
-    dhid_block(r, put0)
+    FC = wgv.shape[1]
+    DN = 2
+    DW = FC // DN
+
+    def dhid_chunk(n):
+        for k in order:
+            dhs[k, :, n * DW:(n + 1) * DW] = nt(gw[r ^ k], wdv[n * DW:(n + 1) * DW, :]).astype(BF)
+
+    def dhid_send(n):
+        ns = slice(n * DW, (n + 1) * DW)
+        return Reduce(net, R, r, lambda k, h: dhs.at[k, half(L, h), ns], lambda k, h: dhr.at[k, half(L, h), ns])
+
+    dhid_chunk(0)
+    dh = [dhid_send(0)]
+    for n in range(1, DN):
+        dhid_chunk(n)
 
     xv = xb[my_tl, :].astype(F32)
     xm, xr_ = stats(xv)
@@ -309,73 +356,86 @@
     n2[...] = n2v
     h2t[...] = n2v.astype(BF)
     a_2 = to_ws(h2t, h2w)
-    dh[R - 1] = net(dhs.at[R - 1], dhr.at[R - 1], rows=r ^ (R - 1))
+    for n in range(1, DN):
+        dh.append(dhid_send(n))
+    for n in range(DN):
+        dho[:, n * DW:(n + 1) * DW] = nt(gw[r], wdv[n * DW:(n + 1) * DW, :])
     landed(a_2)
     h2_z, h2_p = cols_start(wsblk(h2w))
+    for d in dh:
+        d.relay()
+    a_h = to_ws(h1.at[my_tl, :], h1w)
     lff[1].wait()
     lff[2].wait()
     h2_f = cols_forward(wsblk(h2w), h2_z)
     cols_finish(h2_p, h2_f)
     lout.append(local(h2w, h2w_out))
 
-    FC = wgv.shape[1]
     QN = g["QN"]
     QW = FC // QN
-    gu = {}
-    for q in range(QN):
+    gu = []
+
+    def gu_chunk(q):
         qs = slice(q * QW, (q + 1) * QW)
-        for k in order + [0]:
+        for k in order[::-1] + [0]:
             ga_ = nn(h2w[r ^ k], wgv[:, qs])
             up_ = nn(h2w[r ^ k], wuv[:, qs])
             if k:
                 gus[k, q, 0] = ga_.astype(BF)
                 gus[k, q, 1] = up_.astype(BF)
-                gu[k, q] = net(gus.at[k, q], gur.at[k, q], rows=r ^ k)
             else:
                 guo[q, 0] = ga_
                 guo[q, 1] = up_
-
-    for k in order:
-        dh[k].wait_recv()
-    dgu, hdc = {}, {}
+        gu.append(Reduce(net, R, r, lambda k, h: gus.at[k, q, :, half(L, h), :],
+                         lambda k, h: gur.at[k, q, :, half(L, h), :]))
+
     for q in range(QN):
-        for k in order:
-            gu[k, q].wait_recv()
-
+        gu_chunk(q)
+        if q:
+            gu[q - 1].relay()
+    gu[QN - 1].relay()
+    landed(a_h)
+    h_z, h_p = cols_start(wsblk(h1w))
+
+    for d in dh:
+        d.wait()
+    dgt = []
+    for q in range(QN):
+        gu[q].wait()
         qs = slice(q * QW, (q + 1) * QW)
 
         def act(i, _, q=q, qs=qs):
             rows = at(i * 32, 32)
             gate, up = guo[q, 0, rows, :], guo[q, 1, rows, :]
             dhid = dho[rows, q * QW:(q + 1) * QW]
-            for k in order:
+            for k in gu[q].ks:
                 gate = gate + gur[k, q, 0, rows, :].astype(F32)
                 up = up + gur[k, q, 1, rows, :].astype(F32)
                 dhid = dhid + dhr[k, rows, q * QW:(q + 1) * QW].astype(F32)
             sig = 1.0 / (1.0 + jnp.exp(-gate))
             silu = gate * sig
             hda[r, rows, qs] = (silu * up).astype(BF)
-            dga[r, rows, qs] = (dhid * up * sig * (1.0 + gate * (1.0 - sig))).astype(BF)
-            dua[r, rows, qs] = (dhid * silu).astype(BF)
+            dgu[0, r, rows, qs] = (dhid * up * sig * (1.0 + gate * (1.0 - sig))).astype(BF)
+            dgu[1, r, rows, qs] = (dhid * silu).astype(BF)
             return 0
         lax.fori_loop(0, L // 32, act, 0)
-        for k in order:
-            dgu[k, q, 0] = net(dga.at[r, :, qs], dga.at[r, :, qs], rows=r ^ k)
-            dgu[k, q, 1] = net(dua.at[r, :, qs], dua.at[r, :, qs], rows=r ^ k)
-    for k in order[:-1]:
-        hdc[k] = net(hda.at[r], hda.at[r], rows=r ^ k)
+        dgt.append(Gather(net, R, r, lambda h, qs=qs: dgu.at[:, r, half(L, h), qs],
+                          lambda j, h, qs=qs: dgu.at[:, j, half(L, h), qs]))
 
     k2 = {}
 
     def dh2_block(k):
         s = r ^ k
-        tot = nt(dga[s], wgv[...]) + nt(dua[s], wuv[...])
+        tot = nt(dgu[0, s], wgv[...]) + nt(dgu[1, s], wuv[...])
         for j in range(C):
             p2[j % 2, k, j // 2] = tot[j * TL:(j + 1) * TL, :].astype(BF)
         k2[k] = net(p2.at[1 - core, k], p2a.at[k], cols=c ^ 1)
 
     dh2_block(0)
     z2 = {}
+    for q in range(QN):
+        dgt[q].forward()
+    hdc = Gather(net, R, r, lambda h: hda.at[r, half(L, h), :], lambda j, h: hda.at[j, half(L, h), :])
 
     def z2_send(k):
         k2[k].wait_recv()
@@ -385,12 +445,13 @@
 
     for n, k in enumerate(order):
         for q in range(QN):
-            dgu[k, q, 0].wait_recv()
-            dgu[k, q, 1].wait_recv()
+            dgt[q].wait(k)
         dh2_block(k)
         z2_send(n)
     z2_send(R - 1)
-    lout += [local(dga, dg_out), local(dua, du_out)]
+    lout += [local(dgu.at[0], dg_out), local(dgu.at[1], du_out)]
+    h_f = cols_forward(wsblk(h1w), h_z)
+    hdc.forward()
 
     a_d = []
     for k in range(R):
@@ -403,8 +464,6 @@
             a_d.append(net(dh2s.at[k], dh2t.at[:, at(r * DR, DR)], rows=r ^ k))
         else:
             l_d = local(dh2s.at[0], dh2t.at[:, at(r * DR, DR)])
-    k = order[-1]
-    hdc[k] = net(hda.at[r], hda.at[r], rows=r ^ k)
     l_d.wait()
     for k in a_d:
         k.wait_recv()
@@ -425,21 +484,28 @@
     m_z = [net(dmt, dblk(c), cols=c ^ (2 * m)) for m in range(1, Z)]
     m_p = net(dmt, dblk(c), cols=c ^ 1)
 
-    for k in order[:-1]:
-        hdc[k].wait_recv()
-
     def ffn_block(k):
         s = r ^ k
         tot = nn(hda[s], wdv[...])
         for j in range(C):
             p3[j % 2, j // 2, k] = tot[j * TL:(j + 1) * TL, :].astype(BF)
 
-    for k in range(R - 1):
+    ffn_block(0)
+    for k in order:
+        hdc.wait(k)
         ffn_block(k)
+    k3 = pre(p3, p3a)
+    cols_finish(h_p, h_f)
+    lout += [local(hda, hd_out), local(h1w, h1w_out)]
+    k3.wait_recv()
+    z3 = zsend(p3, p3a, p3s, p3r)
     m_f = cols_forward(dblk, m_z)
     l_m.wait()
     cols_finish(m_p, m_f)
 
+    for k in order:
+        gop[k] = tn(att[...], dmix[:, at((r ^ k) * DR, DR)]).astype(BF)
+    cgo = Reduce(net, R, r, lambda k, h: gop.at[k, half(HC, h), :], lambda k, h: gor.at[k, half(HC, h), :])
     da = nt(dmix[...], wof[...]).astype(BF)
     for h in range(heads):
         hs = slice(h * HD, (h + 1) * HD)
@@ -452,7 +518,7 @@
         dqkv[0, r, :, hs] = unrope(nn(ds, kb[:, hs]) * scale).astype(BF)
         dqkv[1, r, :, hs] = unrope(tn(ds, qb[:, hs]) * scale).astype(BF)
         dqkv[2, r, :, hs] = tn(pr.astype(BF), da[:, hs]).astype(BF)
-    cd = [net(dqkv.at[i, r], dqkv.at[i, r], rows=r ^ k) for k in order for i in range(3)]
+    cd = Gather(net, R, r, lambda h: dqkv.at[:, r, half(L, h), :], lambda j, h: dqkv.at[:, j, half(L, h), :])
 
     for n in range(D // W1):
         ns = slice(n * W1, (n + 1) * W1)
@@ -460,19 +526,15 @@
         for j in range(C):
             p4[j % 2, j // 2, :, ns] = val[j * TL:(j + 1) * TL, :].astype(BF)
     k4 = pre(p4, p4a)
-    for s in range(R):
-        gop[s] = tn(att[...], dmix[:, s * DR:(s + 1) * DR]).astype(BF)
-    cgo = [net(gop.at[r ^ k], gor.at[k], rows=r ^ k) for k in order]
+    cgo.relay()
+    gof[...] = tn(att[...], dmix[:, at(r * DR, DR)])
     k4.wait_recv()
     z4 = zsend(p4, p4a, p4s, p4r)
-
-    hdc[order[-1]].wait_recv()
-    ffn_block(R - 1)
-    lout.append(local(hda, hd_out))
-    k3 = pre(p3, p3a)
-    k3.wait_recv()
-    z3 = zsend(p3, p3a, p3s, p3r)
-
+    cd.forward()
+
+    fs[...] = zsum(p3, p3a, p3r, z3)
+    a_f = [net(fs.at[k], ft.at[:, at(r * DR, DR)], rows=r ^ k) for k in order]
+    l_f = local(fs.at[0], ft.at[:, at(r * DR, DR)])
     _, rstd1 = stats(xb[my_tl, :].astype(F32))
     git[...] = dxt[...] + norm_back(zsum(p4, p4a, p4r, z4), xtl[...], rstd1)
 
@@ -481,9 +543,6 @@
         return cps, local(src.at[:, at(c * DC, DC)], dst.at[my_tl, :])
 
     i_g = to_io(git, gib)
-    fs[...] = zsum(p3, p3a, p3r, z3)
-    a_f = [net(fs.at[k], ft.at[:, at(r * DR, DR)], rows=r ^ k) for k in order]
-    l_f = local(fs.at[0], ft.at[:, at(r * DR, DR)])
     l_f.wait()
     for k in a_f:
         k.wait_recv()
@@ -491,13 +550,11 @@
     i_o = to_io(lot, lob)
     landed(i_g)
     lout.append(local(gib, gi_out))
-    for k in cd:
-        k.wait_recv()
+    arrived(cd)
     lout.append(local(dqkv, dqkv_out))
-    for k in cgo:
-        k.wait_recv()
-    gsum = gop[r].astype(F32)
-    for k in order:
+    cgo.wait()
+    gsum = gof[...]
+    for k in cgo.ks:
         gsum = gsum + gor[k].astype(F32)
     gof[...] = gsum
     lout.append(local(gof, go_out))
@@ -540,7 +597,7 @@
         V((TL, D), F32), V((TL, D), F32),
         V((R, L, FC), BF), V((R, L, FC), BF), V((L, FC), F32),
         V((R, QN, 2, L, QW), BF), V((R, QN, 2, L, QW), BF), V((QN, 2, L, QW), F32),
-        V((R, L, FC), BF), V((R, L, FC), BF), V((R, L, FC), BF),
+        V((R, L, FC), BF), V((2, R, L, FC), BF),
         V((R, TL, DR), F32), V((TL, D), F32), V((TL, D), F32), V((TL, D), BF), V((L, D), BF),
         V((L, HC), BF), V((L, HC), BF), V((L, HC), BF), V((L, HC), BF), V((L, HC), F32),
         V((L, HD), F32), V((L, HD), F32), V((L, L), F32),
@@ -570,7 +627,7 @@
 
 
 def g_sems(R, C, QN):
-    return 12 * (R - 1) + 8 * C + 8 * C + (R - 1) * (12 + 4 * QN) + R * C + 8 * C
+    return 2 * (R - 1) * (6 + QN) + 2 * R * (3 + QN) + 5 * (R - 1) + 7 * C + (R + 3) * C // 2 + 2 * C
 
 
 def solution(mesh):

time: 295 us -> 237 us (0.80)
  Pallas kernels: 279 us -> 221 us
    pallas_call x1, Pallas kernels: 279 us -> 221 us  [body(): pl.pallas_call(functools.partial(step_kernel, g), out_shape=outs, in_spec...]
where the time goes in v3:
time: 237 us
  Pallas kernels  221 us (93%)
  matrix products  11.6 us (5%)
  local copies, waits for them, and re-layouts  3.87 us (2%)
    pallas_call x1, Pallas kernels, body(): pl.pallas_call(functools.partial(step_kernel, g), out_shape=outs, in_spec...  221 us
    dot_general x6, matrix products, tn(): lax.dot_general(a, b, (((0,), (0,)), ((), ())), preferred_element_type=F32)  11.6 us

profile of v3, /device:TPU:0, one launch (start us, length us, event | category | flops | bytes accessed | tf_op | source)
XLA Modules:
  0.0 237.1 jit_solution(4131219698124840475)
XLA Ops:
  0.6 221.0 %layer_step.1 = (bf16[256,256]{1,0:T(8,128)(2,1)}, f32[256,256]{1,0:T(8,128)}, bf16[4,256,512]{2,1,0:T(8,128)(2,1)}, bf16[4,256,512]{2,1,0:T(8,128)(2,1)}, bf16[...) custom-call(bf16[256,256]{1,0:T(8,128)(2,1)} %refs_0_.1, ...), custom_call_target="tpu_custom_call" | custom-call | tf_op jit(solution)/shard_map/layer_step/pallas_call | solution.py:611
  221.6 0.0 copy-start.8
  221.6 1.5 fusion
  223.2 0.1 copy-done.8
  223.3 1.3 fusion.3
  224.6 0.0 copy-start
  224.6 0.0 copy-start.2
  224.6 1.3 fusion.2
  225.9 1.3 fusion.1
  227.1 0.0 copy-done
  227.1 0.0 copy-done.2
  227.1 2.6 %convolution_bitcast_fusion.2 = f32[512,1024]{1,0:T(8,128)} fusion(bf16[4,256,512]{2,1,0:T(8,128)(2,1)S(1)} %copy-done, bf16[4,256,1024]{2,1,0:T(8,128)(2,1)S(1)} %copy-done.2), kind=kOutput, calls=%fused_computation.2 | convolution fusion | flops 1073741824 | bytes 5242880 | tf_op jit(solution)/shard_map/dot_general | solution.py:28
  229.7 0.0 copy-done.1
  229.7 2.6 %convolution_bitcast_fusion.1 = f32[512,1024]{1,0:T(8,128)} fusion(bf16[4,256,512]{2,1,0:T(8,128)(2,1)S(1)} %copy-done, bf16[4,256,1024]{2,1,0:T(8,128)(2,1)S(1)} %copy-done.1), kind=kOutput, calls=%fused_computation.1 | convolution fusion | flops 1073741824 | bytes 5242880 | tf_op jit(solution)/shard_map/dot_general | solution.py:28
  232.3 0.0 copy-done.6
  232.3 0.0 copy-done.7
  232.3 0.0 copy-start.3
  232.4 2.6 %convolution_bitcast_fusion = f32[1024,512]{1,0:T(8,128)} fusion(bf16[4,256,1024]{2,1,0:T(8,128)(2,1)S(1)} %copy-done.6, bf16[4,256,512]{2,1,0:T(8,128)(2,1)S(1)} %copy-done.7), kind=kOutput, calls=%fused_computation | convolution fusion | flops 1073741824 | bytes 5242880 | tf_op jit(solution)/shard_map/dot_general | solution.py:28
  234.9 0.0 copy-done.5
  235.0 0.7 copy.29
  235.6 0.0 copy-done.4
  235.6 0.7 copy.30
  236.3 0.0 copy-done.3
  236.3 0.8 copy.31
  (5 shorter events, 0.0 us)
Async XLA Ops:
  221.6 1.7 copy-start.8
  224.6 2.5 %copy-start = (bf16[4,256,512]{2,1,0:T(8,128)(2,1)S(1)}, bf16[4,256,512]{2,1,0:T(8,128)(2,1)}, u32[]{:S(2)}) copy-start(bf16[4,256,512]{2,1,0:T(8,128)(2,1)} %get-tuple-element.24) | copy-start | bytes 3145732
  224.6 2.5 %copy-start.2 = (bf16[4,256,1024]{2,1,0:T(8,128)(2,1)S(1)}, bf16[4,256,1024]{2,1,0:T(8,128)(2,1)}, u32[]{:S(2)}) copy-start(bf16[4,256,1024]{2,1,0:T(8,128)(2,1)} %get-tuple-element.25) | copy-start | bytes 6291460
  227.1 2.6 %copy-start.1 = (bf16[4,256,1024]{2,1,0:T(8,128)(2,1)S(1)}, bf16[4,256,1024]{2,1,0:T(8,128)(2,1)}, u32[]{:S(2)}) copy-start(bf16[4,256,1024]{2,1,0:T(8,128)(2,1)} %get-tuple-element.26) | copy-start | bytes 6291460
  229.7 2.6 %copy-start.6 = (bf16[4,256,1024]{2,1,0:T(8,128)(2,1)S(1)}, bf16[4,256,1024]{2,1,0:T(8,128)(2,1)}, u32[]{:S(2)}) copy-start(bf16[4,256,1024]{2,1,0:T(8,128)(2,1)} %get-tuple-element.27) | copy-start | bytes 6291460
  229.7 2.6 %copy-start.7 = (bf16[4,256,512]{2,1,0:T(8,128)(2,1)S(1)}, bf16[4,256,512]{2,1,0:T(8,128)(2,1)}, u32[]{:S(2)}) copy-start(bf16[4,256,512]{2,1,0:T(8,128)(2,1)} %get-tuple-element.28) | copy-start | bytes 3145732
  232.3 2.6 %copy-start.5 = (bf16[256,256]{1,0:T(8,128)(2,1)S(1)}, bf16[256,256]{1,0:T(8,128)(2,1)}, u32[]{:S(2)}) copy-start(bf16[256,256]{1,0:T(8,128)(2,1)} %get-tuple-element.41) | copy-start | bytes 393220
  232.3 3.3 %copy-start.4 = (f32[256,256]{1,0:T(8,128)S(1)}, f32[256,256]{1,0:T(8,128)}, u32[]{:S(2)}) copy-start(f32[256,256]{1,0:T(8,128)} %get-tuple-element.42) | copy-start | bytes 786436
  232.3 4.0 %copy-start.3 = (f32[256,512]{1,0:T(8,128)S(1)}, f32[256,512]{1,0:T(8,128)}, u32[]{:S(2)}) copy-start(f32[256,512]{1,0:T(8,128)} %get-tuple-element.46) | copy-start | bytes 1572868

commit v4 on v3

--- a/solution.py
+++ b/solution.py
@@ -131,12 +131,12 @@
 
 
 def step_kernel(g, *refs):
-    (tok, cot, segr, freq, wq, wk, wv, wo, wg, wu, wd,
-     o_out, gi_out, h1w_out, gw_out, h2w_out, dg_out, du_out, hd_out, dqkv_out, go_out,
+    (tok, cot, seg_in, freq_in, wq, wk, wv, wo, wg, wu, wd,
+     o_out, gi_out, h1w_out, gw_out, h2w_out, dg_out, du_out, hd_out, dq_out, dk_out, dv_out, go_out,
      xb, h1, xtl, gtl, h1w, gw, h2w, h2t, wqf, wkf, wvf, wof, wgv, wuv, wdv,
      p1, p1a, p1s, p1r, p2, p2a, p2s, p2r, p3, p3a, p3s, p3r, p4, p4a, p4s, p4r,
      x1, n2, dhs, dhr, dho, gus, gur, guo, hda, dgu, dh2s, dh2t, dxt, dmt, dmix,
-     qb, kb, vb, att, lse, cosb, sinb, mskb, dqkv, gop, gor, gof, fs, ft, lot, git, lob, gib,
+     qb, kb, vb, att, lse, cosb, sinb, mskb, dqkv, gop, gor, gof, fs, ft, lot, git, lob, gib, gif, segr, freq,
      send, recv, loc) = refs
     R, C, L, TL, D, DR, DC, HC, H = (g[k] for k in ("R", "C", "L", "TL", "D", "DR", "DC", "HC", "H"))
     Z = C // 2
@@ -155,6 +155,7 @@
     for k in range(1, C):
         pl.semaphore_signal(bar, inc=1, device_id={"cols": c ^ k}, device_id_type=MESH)
 
+    lsm = [local(seg_in, segr), local(freq_in, freq)]
     lx = local(tok, xb.at[:, at(c * DC, DC)])
     lg = local(cot.at[my_tl, :], gtl.at[:, at(c * DC, DC)])
     lws = [local(wq, wqf.at[at(r * DR, DR), :]), local(wk, wkf.at[at(r * DR, DR), :]),
@@ -195,6 +196,8 @@
     ga = [net(cot.at[at((c ^ k) * TL, TL), :], gtl.at[:, at(c * DC, DC)], cols=c ^ k) for k in range(1, C)]
     ck = w_in(wk, wkf)
 
+    for k in lsm:
+        k.wait()
     sr = jnp.broadcast_to(segr[...].astype(F32), (L, L))
     sc = sr.T
     qi = lax.broadcasted_iota(jnp.int32, (L, L), 0)
@@ -435,7 +438,12 @@
     z2 = {}
     for q in range(QN):
         dgt[q].forward()
-    hdc = Gather(net, R, r, lambda h: hda.at[r, half(L, h), :], lambda j, h: hda.at[j, half(L, h), :])
+
+    def hid_send(n):
+        ns = slice(n * DW, (n + 1) * DW)
+        return Gather(net, R, r, lambda h: hda.at[r, half(L, h), ns], lambda j, h: hda.at[j, half(L, h), ns])
+
+    hdc = [hid_send(0)]
 
     def z2_send(k):
         k2[k].wait_recv()
@@ -450,8 +458,7 @@
         z2_send(n)
     z2_send(R - 1)
     lout += [local(dgu.at[0], dg_out), local(dgu.at[1], du_out)]
-    h_f = cols_forward(wsblk(h1w), h_z)
-    hdc.forward()
+    hdc[0].forward()
 
     a_d = []
     for k in range(R):
@@ -459,11 +466,12 @@
         for m in range(1, Z):
             z2[k, m].wait_recv()
             tot = tot + p2r[k, m].astype(F32)
-        dh2s[k] = tot
+        dh2s[k] = tot.astype(BF)
         if k:
             a_d.append(net(dh2s.at[k], dh2t.at[:, at(r * DR, DR)], rows=r ^ k))
         else:
             l_d = local(dh2s.at[0], dh2t.at[:, at(r * DR, DR)])
+    hdc += [hid_send(n) for n in range(1, DN)]
     l_d.wait()
     for k in a_d:
         k.wait_recv()
@@ -474,7 +482,7 @@
         return rstd * (grad - a - normed * b)
 
     _, rstd2b = stats(x1[...])
-    dxv = gtl[...].astype(F32) + norm_back(dh2t[...], n2[...], rstd2b)
+    dxv = gtl[...].astype(F32) + norm_back(dh2t[...].astype(F32), n2[...], rstd2b)
     dxt[...] = dxv
     dmt[...] = dxv.astype(BF)
     l_m = local(dmt, dmix.at[my_tl, :])
@@ -491,15 +499,19 @@
             p3[j % 2, j // 2, k] = tot[j * TL:(j + 1) * TL, :].astype(BF)
 
     ffn_block(0)
+    h_f = cols_forward(wsblk(h1w), h_z)
+    for d in hdc[1:]:
+        d.forward()
     for k in order:
-        hdc.wait(k)
+        for d in hdc:
+            d.wait(k)
         ffn_block(k)
     k3 = pre(p3, p3a)
     cols_finish(h_p, h_f)
     lout += [local(hda, hd_out), local(h1w, h1w_out)]
     k3.wait_recv()
+    m_f = cols_forward(dblk, m_z)
     z3 = zsend(p3, p3a, p3s, p3r)
-    m_f = cols_forward(dblk, m_z)
     l_m.wait()
     cols_finish(m_p, m_f)
 
@@ -532,11 +544,11 @@
     z4 = zsend(p4, p4a, p4s, p4r)
     cd.forward()
 
-    fs[...] = zsum(p3, p3a, p3r, z3)
+    fs[...] = zsum(p3, p3a, p3r, z3).astype(BF)
     a_f = [net(fs.at[k], ft.at[:, at(r * DR, DR)], rows=r ^ k) for k in order]
     l_f = local(fs.at[0], ft.at[:, at(r * DR, DR)])
     _, rstd1 = stats(xb[my_tl, :].astype(F32))
-    git[...] = dxt[...] + norm_back(zsum(p4, p4a, p4r, z4), xtl[...], rstd1)
+    git[...] = (dxt[...] + norm_back(zsum(p4, p4a, p4r, z4), xtl[...], rstd1)).astype(BF)
 
     def to_io(src, dst):
         cps = [net(src.at[:, at((c ^ k) * DC, DC)], dst.at[my_tl, :], cols=c ^ k) for k in range(1, C)]
@@ -546,12 +558,13 @@
     l_f.wait()
     for k in a_f:
         k.wait_recv()
-    lot[...] = (x1[...] + ft[...]).astype(BF)
+    lot[...] = (x1[...] + ft[...].astype(F32)).astype(BF)
     i_o = to_io(lot, lob)
     landed(i_g)
-    lout.append(local(gib, gi_out))
+    gif[...] = gib[...].astype(F32)
+    lout.append(local(gif, gi_out))
     arrived(cd)
-    lout.append(local(dqkv, dqkv_out))
+    lout += [local(dqkv.at[0], dq_out), local(dqkv.at[1], dk_out), local(dqkv.at[2], dv_out)]
     cgo.wait()
     gsum = gof[...]
     for k in cgo.ks:
@@ -583,7 +596,7 @@
     outs = [
         S((L, DC), BF), S((L, DC), F32), S((R, L, DR), BF), S((R, L, DR), BF), S((R, L, DR), BF),
         S((R, L, FC), BF), S((R, L, FC), BF), S((R, L, FC), BF),
-        S((3, R, L, HC), BF), S((HC, DR), F32),
+        S((R, L, HC), BF), S((R, L, HC), BF), S((R, L, HC), BF), S((HC, DR), F32),
     ]
     seq = lambda w: [V((2, Z, TL, w), BF), V((Z, TL, w), BF), V((Z, TL, w), BF), V((Z, TL, w), BF)]
     seq4 = lambda: [V((2, Z, R, TL, DR), BF), V((Z, R, TL, DR), BF), V((Z, R, TL, DR), BF), V((Z, R, TL, DR), BF)]
@@ -598,36 +611,36 @@
         V((R, L, FC), BF), V((R, L, FC), BF), V((L, FC), F32),
         V((R, QN, 2, L, QW), BF), V((R, QN, 2, L, QW), BF), V((QN, 2, L, QW), F32),
         V((R, L, FC), BF), V((2, R, L, FC), BF),
-        V((R, TL, DR), F32), V((TL, D), F32), V((TL, D), F32), V((TL, D), BF), V((L, D), BF),
+        V((R, TL, DR), BF), V((TL, D), BF), V((TL, D), F32), V((TL, D), BF), V((L, D), BF),
         V((L, HC), BF), V((L, HC), BF), V((L, HC), BF), V((L, HC), BF), V((L, HC), F32),
         V((L, HD), F32), V((L, HD), F32), V((L, L), F32),
         V((3, R, L, HC), BF), V((R, HC, DR), BF), V((R, HC, DR), BF), V((HC, DR), F32),
-        V((R, TL, DR), F32), V((TL, D), F32), V((TL, D), BF), V((TL, D), F32), V((L, DC), BF), V((L, DC), F32),
+        V((R, TL, DR), BF), V((TL, D), BF), V((TL, D), BF), V((TL, D), BF), V((L, DC), BF), V((L, DC), BF), V((L, DC), F32),
+        V((1, L), jnp.int32), V((1, HD), F32),
         pltpu.SemaphoreType.DMA((g_sems(R, C, QN),)), pltpu.SemaphoreType.DMA((g_sems(R, C, QN),)),
         pltpu.SemaphoreType.DMA((40,)),
     ]
     A = pl.BlockSpec(memory_space=pl.ANY)
-    B = pl.BlockSpec(memory_space=pltpu.VMEM)
     res = pl.pallas_call(
         functools.partial(step_kernel, g),
         out_shape=outs,
-        in_specs=[A, A, B, B] + [A] * 7,
+        in_specs=[A] * 11,
         out_specs=[A] * len(outs),
         scratch_shapes=scratch,
         compiler_params=pltpu.CompilerParams(
             collective_id=0, has_side_effects=True, vmem_limit_bytes=67043328),
         name="layer_step",
     )(tokens, cotangent, segments, freq, w_query, w_key, w_value, w_out, w_gate, w_up, w_down)
-    layer_out, grad_in, h1w, gw, h2w, dg, du, hd, dqkv, go = res
+    layer_out, grad_in, h1w, gw, h2w, dg, du, hd, dq, dk, dv, go = res
     T = R * L
     h1w, gw, h2w = (t.reshape(T, DR) for t in (h1w, gw, h2w))
-    gq, gk, gv = (tn(h1w, dqkv[i].reshape(T, HC)) for i in range(3))
+    gq, gk, gv = (tn(h1w, t.reshape(T, HC)) for t in (dq, dk, dv))
     ggate, gup, gdown = tn(h2w, dg.reshape(T, FC)), tn(h2w, du.reshape(T, FC)), tn(hd.reshape(T, FC), gw)
     return layer_out, grad_in, gq, gk, gv, go, ggate, gup, gdown
 
 
 def g_sems(R, C, QN):
-    return 2 * (R - 1) * (6 + QN) + 2 * R * (3 + QN) + 5 * (R - 1) + 7 * C + (R + 3) * C // 2 + 2 * C
+    return 2 * (R - 1) * (7 + QN) + 2 * R * (3 + QN) + 5 * (R - 1) + 7 * C + (R + 3) * C // 2 + 2 * C
 
 
 def solution(mesh):

time: 237 us -> 221 us (0.932)
  Pallas kernels: 221 us -> 205 us
    pallas_call x1, Pallas kernels: 221 us -> 205 us  [body(): pl.pallas_call(functools.partial(step_kernel, g), out_shape=outs, in_spec...]
where the time goes in v4:
time: 221 us
  Pallas kernels  205 us (93%)
  matrix products  13.1 us (6%)
    pallas_call x1, Pallas kernels, body(): pl.pallas_call(functools.partial(step_kernel, g), out_shape=outs, in_spec...  205 us
    dot_general x6, matrix products, tn(): lax.dot_general(a, b, (((0,), (0,)), ((), ())), preferred_element_type=F32)  13.1 us

profile of v4, /device:TPU:0, one launch (start us, length us, event | category | flops | bytes accessed | tf_op | source)
XLA Modules:
  0.0 220.6 jit_solution(2630757025901272061)
XLA Ops:
  0.6 204.6 %layer_step.1 = (bf16[256,256]{1,0:T(8,128)(2,1)}, f32[256,256]{1,0:T(8,128)}, bf16[4,256,512]{2,1,0:T(8,128)(2,1)}, bf16[4,256,512]{2,1,0:T(8,128)(2,1)}, bf16[...) custom-call(bf16[256,256]{1,0:T(8,128)(2,1)} %refs_0_.1, ...), custom_call_target="tpu_custom_call" | custom-call | tf_op jit(solution)/shard_map/layer_step/pallas_call | solution.py:624
  205.3 0.0 copy-start.8
  205.3 0.0 copy-start.10
  205.3 0.0 copy-start.9
  205.3 2.8 %convolution_bitcast_fusion.5 = f32[512,256]{1,0:T(8,128)} fusion(bf16[4,256,512]{2,1,0:T(8,128)(2,1)} %get-tuple-element.23, bf16[4,256,256]{2,1,0:T(8,128)(2,1)} %get-tuple-element.24), kind=kOutput, calls=%fused_computation.5 | convolution fusion | flops 268435456 | bytes 2097152 | tf_op jit(solution)/shard_map/dot_general | solution.py:28
  208.1 0.0 copy-done.8
  208.1 0.0 copy-done.10
  208.1 0.0 copy-start.2
  208.1 1.3 convolution_bitcast_fusion.4
  209.4 0.0 copy-done.9
  209.4 1.3 convolution_bitcast_fusion.3
  210.6 0.0 copy-done
  210.6 0.0 copy-done.2
  210.6 2.6 %convolution_bitcast_fusion.2 = f32[512,1024]{1,0:T(8,128)} fusion(bf16[4,256,512]{2,1,0:T(8,128)(2,1)S(1)} %copy-done, bf16[4,256,1024]{2,1,0:T(8,128)(2,1)S(1)} %copy-done.2), kind=kOutput, calls=%fused_computation.2 | convolution fusion | flops 1073741824 | bytes 5242880 | tf_op jit(solution)/shard_map/dot_general | solution.py:28
  213.2 0.0 copy-done.1
  213.2 2.6 %convolution_bitcast_fusion.1 = f32[512,1024]{1,0:T(8,128)} fusion(bf16[4,256,512]{2,1,0:T(8,128)(2,1)S(1)} %copy-done, bf16[4,256,1024]{2,1,0:T(8,128)(2,1)S(1)} %copy-done.1), kind=kOutput, calls=%fused_computation.1 | convolution fusion | flops 1073741824 | bytes 5242880 | tf_op jit(solution)/shard_map/dot_general | solution.py:28
  215.8 0.0 copy-done.6
  215.8 0.0 copy-done.7
  215.8 0.0 copy-start.3
  215.8 2.6 %convolution_bitcast_fusion = f32[1024,512]{1,0:T(8,128)} fusion(bf16[4,256,1024]{2,1,0:T(8,128)(2,1)S(1)} %copy-done.6, bf16[4,256,512]{2,1,0:T(8,128)(2,1)S(1)} %copy-done.7), kind=kOutput, calls=%fused_computation | convolution fusion | flops 1073741824 | bytes 5242880 | tf_op jit(solution)/shard_map/dot_general | solution.py:28
  218.4 0.7 copy.35
  219.1 0.7 copy.36
  219.8 0.0 copy-done.3
  219.8 0.8 copy.37
  (8 shorter events, 0.0 us)
Async XLA Ops:
  205.3 2.8 %copy-start.8 = (bf16[4,256,512]{2,1,0:T(8,128)(2,1)S(1)}, bf16[4,256,512]{2,1,0:T(8,128)(2,1)}, u32[]{:S(2)}) copy-start(bf16[4,256,512]{2,1,0:T(8,128)(2,1)} %get-tuple-element.23) | copy-start | bytes 3145732
  205.3 2.8 %copy-start.10 = (bf16[4,256,256]{2,1,0:T(8,128)(2,1)S(1)}, bf16[4,256,256]{2,1,0:T(8,128)(2,1)}, u32[]{:S(2)}) copy-start(bf16[4,256,256]{2,1,0:T(8,128)(2,1)} %get-tuple-element.25) | copy-start | bytes 1572868
  205.3 4.1 %copy-start.9 = (bf16[4,256,256]{2,1,0:T(8,128)(2,1)S(1)}, bf16[4,256,256]{2,1,0:T(8,128)(2,1)}, u32[]{:S(2)}) copy-start(bf16[4,256,256]{2,1,0:T(8,128)(2,1)} %get-tuple-element.26) | copy-start | bytes 1572868
  208.1 2.6 %copy-start = (bf16[4,256,512]{2,1,0:T(8,128)(2,1)S(1)}, bf16[4,256,512]{2,1,0:T(8,128)(2,1)}, u32[]{:S(2)}) copy-start(bf16[4,256,512]{2,1,0:T(8,128)(2,1)} %get-tuple-element.28) | copy-start | bytes 3145732
  208.1 2.6 %copy-start.2 = (bf16[4,256,1024]{2,1,0:T(8,128)(2,1)S(1)}, bf16[4,256,1024]{2,1,0:T(8,128)(2,1)}, u32[]{:S(2)}) copy-start(bf16[4,256,1024]{2,1,0:T(8,128)(2,1)} %get-tuple-element.29) | copy-start | bytes 6291460
  210.6 2.6 %copy-start.1 = (bf16[4,256,1024]{2,1,0:T(8,128)(2,1)S(1)}, bf16[4,256,1024]{2,1,0:T(8,128)(2,1)}, u32[]{:S(2)}) copy-start(bf16[4,256,1024]{2,1,0:T(8,128)(2,1)} %get-tuple-element.30) | copy-start | bytes 6291460
  213.2 2.6 %copy-start.6 = (bf16[4,256,1024]{2,1,0:T(8,128)(2,1)S(1)}, bf16[4,256,1024]{2,1,0:T(8,128)(2,1)}, u32[]{:S(2)}) copy-start(bf16[4,256,1024]{2,1,0:T(8,128)(2,1)} %get-tuple-element.31) | copy-start | bytes 6291460
  213.2 2.6 %copy-start.7 = (bf16[4,256,512]{2,1,0:T(8,128)(2,1)S(1)}, bf16[4,256,512]{2,1,0:T(8,128)(2,1)}, u32[]{:S(2)}) copy-start(bf16[4,256,512]{2,1,0:T(8,128)(2,1)} %get-tuple-element.32) | copy-start | bytes 3145732
  215.8 2.6 %copy-start.5 = (bf16[256,256]{1,0:T(8,128)(2,1)S(1)}, bf16[256,256]{1,0:T(8,128)(2,1)}, u32[]{:S(2)}) copy-start(bf16[256,256]{1,0:T(8,128)(2,1)} %get-tuple-element.42) | copy-start | bytes 393220
  215.8 3.3 %copy-start.4 = (f32[256,256]{1,0:T(8,128)S(1)}, f32[256,256]{1,0:T(8,128)}, u32[]{:S(2)}) copy-start(f32[256,256]{1,0:T(8,128)} %get-tuple-element.43) | copy-start | bytes 786436
  215.8 4.0 %copy-start.3 = (f32[256,512]{1,0:T(8,128)S(1)}, f32[256,512]{1,0:T(8,128)}, u32[]{:S(2)}) copy-start(f32[256,512]{1,0:T(8,128)} %get-tuple-element.47) | copy-start | bytes 1572868

commit v5 on v4

--- a/solution.py
+++ b/solution.py
@@ -138,7 +138,8 @@
      x1, n2, dhs, dhr, dho, gus, gur, guo, hda, dgu, dh2s, dh2t, dxt, dmt, dmix,
      qb, kb, vb, att, lse, cosb, sinb, mskb, dqkv, gop, gor, gof, fs, ft, lot, git, lob, gib, gif, segr, freq,
      send, recv, loc) = refs
-    R, C, L, TL, D, DR, DC, HC, H = (g[k] for k in ("R", "C", "L", "TL", "D", "DR", "DC", "HC", "H"))
+    R, C, L, TL, D, DR, DC, HC, NT = (g[k] for k in ("R", "C", "L", "TL", "D", "DR", "DC", "HC", "NT"))
+    LH, TH = L // NT, TL // NT
     Z = C // 2
     r = lax.axis_index("rows")
     c = lax.axis_index("cols")
@@ -147,7 +148,10 @@
     net = Net(send, recv)
     local = Local(loc)
     scale = HD ** (-0.5)
-    my_tl = at(c * TL, TL)
+    my_th = at(c * TH, TH)
+
+    def piece(val, j, t):
+        return val[t * LH + j * TH:t * LH + (j + 1) * TH, :]
 
     bar = pltpu.get_barrier_semaphore()
     for k in range(1, R):
@@ -156,8 +160,8 @@
         pl.semaphore_signal(bar, inc=1, device_id={"cols": c ^ k}, device_id_type=MESH)
 
     lsm = [local(seg_in, segr), local(freq_in, freq)]
-    lx = local(tok, xb.at[:, at(c * DC, DC)])
-    lg = local(cot.at[my_tl, :], gtl.at[:, at(c * DC, DC)])
+    lx = local(tok, xb.at[:, :, at(c * DC, DC)])
+    lg = local(cot.at[:, my_th, :], gtl.at[:, :, at(c * DC, DC)])
     lws = [local(wq, wqf.at[at(r * DR, DR), :]), local(wk, wkf.at[at(r * DR, DR), :]),
            local(wv, wvf.at[at(r * DR, DR), :]), local(wo, wof.at[:, at(r * DR, DR)])]
     lff = [local(wd, wdv), local(wg, wgv), local(wu, wuv)]
@@ -188,12 +192,12 @@
             f.wait_recv()
 
     def xblk(j):
-        return xb.at[:, at(j * DC, DC)]
+        return xb.at[:, :, at(j * DC, DC)]
 
     cq = w_in(wq, wqf)
     xz = [net(tok, xblk(c), cols=c ^ (2 * m)) for m in range(1, Z)]
     xp = net(tok, xblk(c), cols=c ^ 1)
-    ga = [net(cot.at[at((c ^ k) * TL, TL), :], gtl.at[:, at(c * DC, DC)], cols=c ^ k) for k in range(1, C)]
+    ga = [net(cot.at[:, at((c ^ k) * TH, TH), :], gtl.at[:, :, at(c * DC, DC)], cols=c ^ k) for k in range(1, C)]
     ck = w_in(wk, wkf)
 
     for k in lsm:
@@ -212,9 +216,9 @@
     sn = jnp.sin(angle)
     sinb[...] = jnp.where(lane < HD // 2, -sn, sn)
 
-    def to_ws(src, dst):
-        cps = [net(src.at[:, at((r ^ k) * DR, DR)], dst.at[r, my_tl, :], rows=r ^ k) for k in range(1, R)]
-        return cps, local(src.at[:, at(r * DR, DR)], dst.at[r, my_tl, :])
+    def to_ws(src, dst, t=slice(None)):
+        cps = [net(src.at[t, :, at((r ^ k) * DR, DR)], dst.at[r, t, my_th, :], rows=r ^ k) for k in range(1, R)]
+        return cps, local(src.at[t, :, at(r * DR, DR)], dst.at[r, t, my_th, :])
 
     def landed(cl):
         for k in cl[0]:
@@ -237,20 +241,21 @@
         sq = jnp.sum(v * v, 1, keepdims=True) / D
         return mean, lax.rsqrt(sq - mean * mean + EPS)
 
-    def norm_rows(i, _):
-        rows = at(i * 32, 32)
-        v = xb[rows, :].astype(F32)
-        mean, rstd = stats(v)
-        h1[rows, :] = ((v - mean) * rstd).astype(BF)
-        return 0
-
-    lax.fori_loop(0, L // 32, norm_rows, 0)
+    for t in range(NT):
+        def norm_rows(i, _, t=t):
+            rows = at(i * 32, 32)
+            v = xb[t, rows, :].astype(F32)
+            mean, rstd = stats(v)
+            h1[t, rows, :] = ((v - mean) * rstd).astype(BF)
+            return 0
+
+        lax.fori_loop(0, LH // 32, norm_rows, 0)
 
     cv.forward()
     co = Gather(net, R, r, lambda h: wo.at[half(HC, h), :], lambda j, h: wof.at[half(HC, h), at(j * DR, DR)])
 
-    def wsblk(buf):
-        return lambda j: buf.at[:, at(j * TL, TL), :]
+    def wsblk(buf, t=slice(None)):
+        return lambda j: buf.at[:, t, at(j * TH, TH), :]
 
     heads = HC // HD
 
@@ -270,13 +275,13 @@
     g_z, g_p = cols_start(wsblk(gw))
     lws[0].wait()
     arrived(cq)
-    qb[...] = rope(nn(h1[...], wqf[...])).astype(BF)
+    qb[...] = rope(nn(h1[...].reshape(L, D), wqf[...])).astype(BF)
     lws[1].wait()
     arrived(ck)
-    kb[...] = rope(nn(h1[...], wkf[...])).astype(BF)
+    kb[...] = rope(nn(h1[...].reshape(L, D), wkf[...])).astype(BF)
     lws[2].wait()
     arrived(cv)
-    vb[...] = nn(h1[...], wvf[...]).astype(BF)
+    vb[...] = nn(h1[...].reshape(L, D), wvf[...]).astype(BF)
 
     for h in range(heads):
         hs = slice(h * HD, (h + 1) * HD)
@@ -288,14 +293,6 @@
         lse[:, hs] = jnp.broadcast_to(top + jnp.log(tot), (L, HD))
         att[:, hs] = nn((e / tot).astype(BF), vb[:, hs]).astype(BF)
 
-    def parts_store(dst, val, i=None):
-        for j in range(C):
-            v = val[j * TL:(j + 1) * TL, :].astype(BF)
-            if i is None:
-                dst[j % 2, j // 2, :, :] = v
-            else:
-                dst[j % 2, j // 2, i, :, :] = v
-
     co.forward()
     lws[3].wait()
     arrived(co)
@@ -304,7 +301,8 @@
         ns = slice(n * W1, (n + 1) * W1)
         val = nn(att[...], wof[:, ns])
         for j in range(C):
-            p1[j % 2, j // 2, :, ns] = val[j * TL:(j + 1) * TL, :].astype(BF)
+            for t in range(NT):
+                p1[t, j % 2, j // 2, :, ns] = piece(val, j, t).astype(BF)
 
     def pre(p, pa):
         return net(p.at[1 - core], pa, cols=c ^ 1)
@@ -323,10 +321,12 @@
             tot = tot + pr[m].astype(F32)
         return tot
 
-    k1 = pre(p1, p1a)
+    k1 = [pre(p1.at[t], p1a.at[t]) for t in range(NT)]
     g_f = cols_forward(wsblk(gw), g_z)
-    k1.wait_recv()
-    z1 = zsend(p1, p1a, p1s, p1r)
+    z1 = []
+    for t in range(NT):
+        k1[t].wait_recv()
+        z1.append(zsend(p1.at[t], p1a.at[t], p1s.at[t], p1r.at[t]))
     cols_finish(g_p, g_f)
     lout = [local(gw, gw_out)]
 
@@ -338,7 +338,7 @@
 
     def dhid_chunk(n):
         for k in order:
-            dhs[k, :, n * DW:(n + 1) * DW] = nt(gw[r ^ k], wdv[n * DW:(n + 1) * DW, :]).astype(BF)
+            dhs[k, :, n * DW:(n + 1) * DW] = nt(gw[r ^ k].reshape(L, DR), wdv[n * DW:(n + 1) * DW, :]).astype(BF)
 
     def dhid_send(n):
         ns = slice(n * DW, (n + 1) * DW)
@@ -349,81 +349,97 @@
     for n in range(1, DN):
         dhid_chunk(n)
 
-    xv = xb[my_tl, :].astype(F32)
+    xv = xb[:, my_th, :].reshape(TL, D).astype(F32)
     xm, xr_ = stats(xv)
     xtl[...] = (xv - xm) * xr_
-    v = xv + zsum(p1, p1a, p1r, z1)
-    x1[...] = v
-    mean2, rstd2 = stats(v)
-    n2v = (v - mean2) * rstd2
-    n2[...] = n2v
-    h2t[...] = n2v.astype(BF)
-    a_2 = to_ws(h2t, h2w)
-    for n in range(1, DN):
-        dh.append(dhid_send(n))
-    for n in range(DN):
-        dho[:, n * DW:(n + 1) * DW] = nt(gw[r], wdv[n * DW:(n + 1) * DW, :])
-    landed(a_2)
-    h2_z, h2_p = cols_start(wsblk(h2w))
-    for d in dh:
+
+    def second_norm(t):
+        rows = slice(t * TH, (t + 1) * TH)
+        v = xb[t, my_th, :].astype(F32) + zsum(p1.at[t], p1a.at[t], p1r.at[t], z1[t])
+        x1[rows, :] = v
+        mean2, rstd2 = stats(v)
+        n2v = (v - mean2) * rstd2
+        n2[rows, :] = n2v
+        h2t[t] = n2v.astype(BF)
+        return to_ws(h2t, h2w, t)
+
+    h2_c = []
+    for t in range(NT):
+        a_2 = second_norm(t)
+        if t == 0:
+            for n in range(1, DN):
+                dh.append(dhid_send(n))
+            for n in range(DN):
+                dho[:, n * DW:(n + 1) * DW] = nt(gw[r].reshape(L, DR), wdv[n * DW:(n + 1) * DW, :])
+        else:
+            dh[0].relay()
+        landed(a_2)
+        h2_c.append(cols_start(wsblk(h2w, t)))
+    for d in dh[min(NT, 2) - 1:]:
         d.relay()
-    a_h = to_ws(h1.at[my_tl, :], h1w)
+    a_h = to_ws(h1.at[:, my_th, :], h1w)
     lff[1].wait()
     lff[2].wait()
-    h2_f = cols_forward(wsblk(h2w), h2_z)
-    cols_finish(h2_p, h2_f)
-    lout.append(local(h2w, h2w_out))
 
     QN = g["QN"]
     QW = FC // QN
     gu = []
-
-    def gu_chunk(q):
+    parts = [(t, q) for t in range(NT) for q in range(QN)]
+
+    def gu_chunk(t, q):
         qs = slice(q * QW, (q + 1) * QW)
         for k in order[::-1] + [0]:
-            ga_ = nn(h2w[r ^ k], wgv[:, qs])
-            up_ = nn(h2w[r ^ k], wuv[:, qs])
+            ga_ = nn(h2w[r ^ k, t], wgv[:, qs])
+            up_ = nn(h2w[r ^ k, t], wuv[:, qs])
             if k:
-                gus[k, q, 0] = ga_.astype(BF)
-                gus[k, q, 1] = up_.astype(BF)
+                gus[k, t, q, 0] = ga_.astype(BF)
+                gus[k, t, q, 1] = up_.astype(BF)
             else:
-                guo[q, 0] = ga_
-                guo[q, 1] = up_
-        gu.append(Reduce(net, R, r, lambda k, h: gus.at[k, q, :, half(L, h), :],
-                         lambda k, h: gur.at[k, q, :, half(L, h), :]))
-
-    for q in range(QN):
-        gu_chunk(q)
-        if q:
-            gu[q - 1].relay()
-    gu[QN - 1].relay()
+                guo[t, q, 0] = ga_
+                guo[t, q, 1] = up_
+        gu.append(Reduce(net, R, r, lambda k, h: gus.at[k, t, q, :, half(LH, h), :],
+                         lambda k, h: gur.at[k, t, q, :, half(LH, h), :]))
+
+    for t, q in parts:
+        if q == 0:
+            cols_finish(h2_c[t][1], cols_forward(wsblk(h2w, t), h2_c[t][0]))
+        gu_chunk(t, q)
+        if len(gu) > 1:
+            gu[-2].relay()
+    gu[-1].relay()
+    lout.append(local(h2w, h2w_out))
     landed(a_h)
     h_z, h_p = cols_start(wsblk(h1w))
 
     for d in dh:
         d.wait()
     dgt = []
-    for q in range(QN):
-        gu[q].wait()
+    AR = 16
+    for n, (t, q) in enumerate(parts):
+        gu[n].wait()
         qs = slice(q * QW, (q + 1) * QW)
 
-        def act(i, _, q=q, qs=qs):
-            rows = at(i * 32, 32)
-            gate, up = guo[q, 0, rows, :], guo[q, 1, rows, :]
-            dhid = dho[rows, q * QW:(q + 1) * QW]
-            for k in gu[q].ks:
-                gate = gate + gur[k, q, 0, rows, :].astype(F32)
-                up = up + gur[k, q, 1, rows, :].astype(F32)
-                dhid = dhid + dhr[k, rows, q * QW:(q + 1) * QW].astype(F32)
+        def act(i, _, n=n, t=t, q=q, qs=qs):
+            part = at(i * AR, AR)
+            rows = at(t * LH + i * AR, AR)
+            gate, up = guo[t, q, 0, part, :], guo[t, q, 1, part, :]
+            dhid = dho[rows, qs]
+            for k in gu[n].ks:
+                gate = gate + gur[k, t, q, 0, part, :].astype(F32)
+                up = up + gur[k, t, q, 1, part, :].astype(F32)
+                dhid = dhid + dhr[k, rows, qs].astype(F32)
             sig = 1.0 / (1.0 + jnp.exp(-gate))
             silu = gate * sig
             hda[r, rows, qs] = (silu * up).astype(BF)
             dgu[0, r, rows, qs] = (dhid * up * sig * (1.0 + gate * (1.0 - sig))).astype(BF)
             dgu[1, r, rows, qs] = (dhid * silu).astype(BF)
             return 0
-        lax.fori_loop(0, L // 32, act, 0)
-        dgt.append(Gather(net, R, r, lambda h, qs=qs: dgu.at[:, r, half(L, h), qs],
-                          lambda j, h, qs=qs: dgu.at[:, j, half(L, h), qs]))
+        lax.fori_loop(0, LH // AR, act, 0)
+
+        def tok_half(h, t=t):
+            return slice(t * LH + h * (LH // 2), t * LH + (h + 1) * (LH // 2))
+        dgt.append(Gather(net, R, r, lambda h, qs=qs, f=tok_half: dgu.at[:, r, f(h), qs],
+                          lambda j, h, qs=qs, f=tok_half: dgu.at[:, j, f(h), qs]))
 
     k2 = {}
 
@@ -431,13 +447,14 @@
         s = r ^ k
         tot = nt(dgu[0, s], wgv[...]) + nt(dgu[1, s], wuv[...])
         for j in range(C):
-            p2[j % 2, k, j // 2] = tot[j * TL:(j + 1) * TL, :].astype(BF)
+            for t in range(NT):
+                p2[j % 2, k, j // 2, t * TH:(t + 1) * TH] = piece(tot, j, t).astype(BF)
         k2[k] = net(p2.at[1 - core, k], p2a.at[k], cols=c ^ 1)
 
     dh2_block(0)
     z2 = {}
-    for q in range(QN):
-        dgt[q].forward()
+    for d in dgt:
+        d.forward()
 
     def hid_send(n):
         ns = slice(n * DW, (n + 1) * DW)
@@ -452,8 +469,8 @@
             z2[k, m] = net(p2s.at[k, m], p2r.at[k, m], cols=c ^ (2 * m))
 
     for n, k in enumerate(order):
-        for q in range(QN):
-            dgt[q].wait(k)
+        for d in dgt:
+            d.wait(k)
         dh2_block(k)
         z2_send(n)
     z2_send(R - 1)
@@ -482,13 +499,13 @@
         return rstd * (grad - a - normed * b)
 
     _, rstd2b = stats(x1[...])
-    dxv = gtl[...].astype(F32) + norm_back(dh2t[...].astype(F32), n2[...], rstd2b)
+    dxv = gtl[...].reshape(TL, D).astype(F32) + norm_back(dh2t[...].astype(F32), n2[...], rstd2b)
     dxt[...] = dxv
-    dmt[...] = dxv.astype(BF)
-    l_m = local(dmt, dmix.at[my_tl, :])
+    dmt[...] = dxv.astype(BF).reshape(NT, TH, D)
+    l_m = local(dmt, dmix.at[:, my_th, :])
 
     def dblk(j):
-        return dmix.at[at(j * TL, TL), :]
+        return dmix.at[:, at(j * TH, TH), :]
     m_z = [net(dmt, dblk(c), cols=c ^ (2 * m)) for m in range(1, Z)]
     m_p = net(dmt, dblk(c), cols=c ^ 1)
 
@@ -496,7 +513,8 @@
         s = r ^ k
         tot = nn(hda[s], wdv[...])
         for j in range(C):
-            p3[j % 2, j // 2, k] = tot[j * TL:(j + 1) * TL, :].astype(BF)
+            for t in range(NT):
+                p3[j % 2, j // 2, k, t * TH:(t + 1) * TH] = piece(tot, j, t).astype(BF)
 
     ffn_block(0)
     h_f = cols_forward(wsblk(h1w), h_z)
@@ -516,9 +534,9 @@
     cols_finish(m_p, m_f)
 
     for k in order:
-        gop[k] = tn(att[...], dmix[:, at((r ^ k) * DR, DR)]).astype(BF)
+        gop[k] = tn(att[...], dmix[:, :, at((r ^ k) * DR, DR)].reshape(L, DR)).astype(BF)
     cgo = Reduce(net, R, r, lambda k, h: gop.at[k, half(HC, h), :], lambda k, h: gor.at[k, half(HC, h), :])
-    da = nt(dmix[...], wof[...]).astype(BF)
+    da = nt(dmix[...].reshape(L, D), wof[...]).astype(BF)
     for h in range(heads):
         hs = slice(h * HD, (h + 1) * HD)
         s = nt(qb[:, hs], kb[:, hs]) * scale
@@ -536,31 +554,41 @@
         ns = slice(n * W1, (n + 1) * W1)
         val = (nt(dqkv[0, r], wqf[ns, :]) + nt(dqkv[1, r], wkf[ns, :]) + nt(dqkv[2, r], wvf[ns, :]))
         for j in range(C):
-            p4[j % 2, j // 2, :, ns] = val[j * TL:(j + 1) * TL, :].astype(BF)
-    k4 = pre(p4, p4a)
+            for t in range(NT):
+                p4[t, j % 2, j // 2, :, ns] = piece(val, j, t).astype(BF)
+    k4 = [pre(p4.at[t], p4a.at[t]) for t in range(NT)]
+    z4 = []
+    for t in range(NT):
+        k4[t].wait_recv()
+        z4.append(zsend(p4.at[t], p4a.at[t], p4s.at[t], p4r.at[t]))
+    gof[...] = tn(att[...], dmix[:, :, at(r * DR, DR)].reshape(L, DR))
     cgo.relay()
-    gof[...] = tn(att[...], dmix[:, at(r * DR, DR)])
-    k4.wait_recv()
-    z4 = zsend(p4, p4a, p4s, p4r)
-    cd.forward()
 
     fs[...] = zsum(p3, p3a, p3r, z3).astype(BF)
     a_f = [net(fs.at[k], ft.at[:, at(r * DR, DR)], rows=r ^ k) for k in order]
     l_f = local(fs.at[0], ft.at[:, at(r * DR, DR)])
-    _, rstd1 = stats(xb[my_tl, :].astype(F32))
-    git[...] = (dxt[...] + norm_back(zsum(p4, p4a, p4r, z4), xtl[...], rstd1)).astype(BF)
-
-    def to_io(src, dst):
-        cps = [net(src.at[:, at((c ^ k) * DC, DC)], dst.at[my_tl, :], cols=c ^ k) for k in range(1, C)]
-        return cps, local(src.at[:, at(c * DC, DC)], dst.at[my_tl, :])
-
-    i_g = to_io(git, gib)
+    cd.forward()
+
+    def to_io(src, dst, t=slice(None)):
+        cps = [net(src.at[t, :, at((c ^ k) * DC, DC)], dst.at[t, my_th, :], cols=c ^ k) for k in range(1, C)]
+        return cps, local(src.at[t, :, at(c * DC, DC)], dst.at[t, my_th, :])
+
     l_f.wait()
     for k in a_f:
         k.wait_recv()
-    lot[...] = (x1[...] + ft[...].astype(F32)).astype(BF)
+    lot[...] = (x1[...] + ft[...].astype(F32)).astype(BF).reshape(NT, TH, D)
     i_o = to_io(lot, lob)
-    landed(i_g)
+    i_g = []
+    for t in range(NT):
+        rows = slice(t * TH, (t + 1) * TH)
+        _, rstd1 = stats(xb[t, my_th, :].astype(F32))
+        dh1 = zsum(p4.at[t], p4a.at[t], p4r.at[t], z4[t])
+        git[t] = (dxt[rows, :] + norm_back(dh1, xtl[rows, :], rstd1)).astype(BF)
+        i_g.append(to_io(git, gib, t))
+    landed(i_o)
+    lout.append(local(lob, o_out))
+    for k in i_g:
+        landed(k)
     gif[...] = gib[...].astype(F32)
     lout.append(local(gif, gi_out))
     arrived(cd)
@@ -571,8 +599,6 @@
         gsum = gsum + gor[k].astype(F32)
     gof[...] = gsum
     lout.append(local(gof, go_out))
-    landed(i_o)
-    lout.append(local(lob, o_out))
     net.drain()
     for k in lout:
         k.wait()
@@ -585,40 +611,43 @@
     FC = w_gate.shape[1]
     TL = L // C
     Z = C // 2
-    QN = 4 if FC % 1024 == 0 else 2
+    NT = 2 if TL % 32 == 0 else 1
+    LH, TH = L // NT, TL // NT
+    QN = 4 // NT if FC % 1024 == 0 else 2
     QW = FC // QN
-    g = dict(R=R, C=C, L=L, TL=TL, D=D, DR=DR, DC=DC, HC=HC, H=FC, QN=QN)
+    g = dict(R=R, C=C, L=L, TL=TL, D=D, DR=DR, DC=DC, HC=HC, NT=NT, QN=QN)
     half = HD // 2
     fr = (BASE ** (-(np.arange(half, dtype=np.float32) * np.float32(2.0)) / np.float32(HD))).astype(np.float32)
     freq = jnp.asarray(np.concatenate([fr, fr])[None, :])
     S = jax.ShapeDtypeStruct
     V = pltpu.VMEM
     outs = [
-        S((L, DC), BF), S((L, DC), F32), S((R, L, DR), BF), S((R, L, DR), BF), S((R, L, DR), BF),
+        S((NT, LH, DC), BF), S((NT, LH, DC), F32), *[S((R, NT, LH, DR), BF)] * 3,
         S((R, L, FC), BF), S((R, L, FC), BF), S((R, L, FC), BF),
         S((R, L, HC), BF), S((R, L, HC), BF), S((R, L, HC), BF), S((HC, DR), F32),
     ]
-    seq = lambda w: [V((2, Z, TL, w), BF), V((Z, TL, w), BF), V((Z, TL, w), BF), V((Z, TL, w), BF)]
+    seq = lambda w: [V((NT, 2, Z, TH, w), BF)] + [V((NT, Z, TH, w), BF)] * 3
     seq4 = lambda: [V((2, Z, R, TL, DR), BF), V((Z, R, TL, DR), BF), V((Z, R, TL, DR), BF), V((Z, R, TL, DR), BF)]
     seq2 = lambda: [V((2, R, Z, TL, DR), BF), V((R, Z, TL, DR), BF), V((R, Z, TL, DR), BF), V((R, Z, TL, DR), BF)]
     scratch = [
-        V((L, D), BF), V((L, D), BF), V((TL, D), F32), V((TL, D), BF),
-        V((R, L, DR), BF), V((R, L, DR), BF), V((R, L, DR), BF), V((TL, D), BF),
+        V((NT, LH, D), BF), V((NT, LH, D), BF), V((TL, D), F32), V((NT, TH, D), BF),
+        *[V((R, NT, LH, DR), BF)] * 3, V((NT, TH, D), BF),
         V((D, HC), BF), V((D, HC), BF), V((D, HC), BF), V((HC, D), BF),
         V((DR, FC), BF), V((DR, FC), BF), V((FC, DR), BF),
         *seq(D), *seq2(), *seq4(), *seq(D),
         V((TL, D), F32), V((TL, D), F32),
         V((R, L, FC), BF), V((R, L, FC), BF), V((L, FC), F32),
-        V((R, QN, 2, L, QW), BF), V((R, QN, 2, L, QW), BF), V((QN, 2, L, QW), F32),
+        V((R, NT, QN, 2, LH, QW), BF), V((R, NT, QN, 2, LH, QW), BF), V((NT, QN, 2, LH, QW), F32),
         V((R, L, FC), BF), V((2, R, L, FC), BF),
-        V((R, TL, DR), BF), V((TL, D), BF), V((TL, D), F32), V((TL, D), BF), V((L, D), BF),
+        V((R, TL, DR), BF), V((TL, D), BF), V((TL, D), F32), V((NT, TH, D), BF), V((NT, LH, D), BF),
         V((L, HC), BF), V((L, HC), BF), V((L, HC), BF), V((L, HC), BF), V((L, HC), F32),
         V((L, HD), F32), V((L, HD), F32), V((L, L), F32),
         V((3, R, L, HC), BF), V((R, HC, DR), BF), V((R, HC, DR), BF), V((HC, DR), F32),
-        V((R, TL, DR), BF), V((TL, D), BF), V((TL, D), BF), V((TL, D), BF), V((L, DC), BF), V((L, DC), BF), V((L, DC), F32),
+        V((R, TL, DR), BF), V((TL, D), BF), V((NT, TH, D), BF), V((NT, TH, D), BF),
+        V((NT, LH, DC), BF), V((NT, LH, DC), BF), V((NT, LH, DC), F32),
         V((1, L), jnp.int32), V((1, HD), F32),
-        pltpu.SemaphoreType.DMA((g_sems(R, C, QN),)), pltpu.SemaphoreType.DMA((g_sems(R, C, QN),)),
-        pltpu.SemaphoreType.DMA((40,)),
+        pltpu.SemaphoreType.DMA((g_sems(R, C, NT * QN),)), pltpu.SemaphoreType.DMA((g_sems(R, C, NT * QN),)),
+        pltpu.SemaphoreType.DMA((48,)),
     ]
     A = pl.BlockSpec(memory_space=pl.ANY)
     res = pl.pallas_call(
@@ -630,17 +659,17 @@
         compiler_params=pltpu.CompilerParams(
             collective_id=0, has_side_effects=True, vmem_limit_bytes=67043328),
         name="layer_step",
-    )(tokens, cotangent, segments, freq, w_query, w_key, w_value, w_out, w_gate, w_up, w_down)
+    )(tokens.reshape(NT, LH, DC), cotangent.reshape(NT, LH, DC), segments, freq, w_query, w_key, w_value, w_out, w_gate, w_up, w_down)
     layer_out, grad_in, h1w, gw, h2w, dg, du, hd, dq, dk, dv, go = res
     T = R * L
     h1w, gw, h2w = (t.reshape(T, DR) for t in (h1w, gw, h2w))
     gq, gk, gv = (tn(h1w, t.reshape(T, HC)) for t in (dq, dk, dv))
     ggate, gup, gdown = tn(h2w, dg.reshape(T, FC)), tn(h2w, du.reshape(T, FC)), tn(hd.reshape(T, FC), gw)
-    return layer_out, grad_in, gq, gk, gv, go, ggate, gup, gdown
-
-
-def g_sems(R, C, QN):
-    return 2 * (R - 1) * (7 + QN) + 2 * R * (3 + QN) + 5 * (R - 1) + 7 * C + (R + 3) * C // 2 + 2 * C
+    return layer_out.reshape(L, DC), grad_in.reshape(L, DC), gq, gk, gv, go, ggate, gup, gdown
+
+
+def g_sems(R, C, n):
+    return 2 * (R - 1) * (8 + n) + 2 * R * (3 + n) + 8 * (R - 1) + 16 * C + (R + 4) * C // 2
 
 
 def solution(mesh):

time: 221 us -> 214 us (0.968)
  Pallas kernels: 205 us -> 198 us
    pallas_call x1, Pallas kernels: 205 us -> 198 us  [body(): pl.pallas_call(functools.partial(step_kernel, g), out_shape=outs, in_spec...]
where the time goes in v5:
time: 214 us
  Pallas kernels  198 us (93%)
  matrix products  13.1 us (6%)
  local copies, waits for them, and re-layouts  2.19 us (1%)
    pallas_call x1, Pallas kernels, body(): pl.pallas_call(functools.partial(step_kernel, g), out_shape=outs, in_spec...  198 us
    dot_general x6, matrix products, tn(): lax.dot_general(a, b, (((0,), (0,)), ((), ())), preferred_element_type=F32)  13.1 us

profile of v5, /device:TPU:0, one launch (start us, length us, event | category | flops | bytes accessed | tf_op | source)
XLA Modules:
  0.0 213.5 jit_solution(12899425960018311414)
XLA Ops:
  0.6 197.6 %layer_step.1 = (bf16[2,128,256]{2,1,0:T(8,128)(2,1)}, f32[2,128,256]{2,1,0:T(8,128)}, bf16[4,2,128,512]{3,2,1,0:T(8,128)(2,1)}, bf16[4,2,128,512]{3,2,1,0:T(8,1...) custom-call(bf16[2,128,256]{2,1,0:T(8,128)(2,1)} %bitcast.31, ...), custom_call_target="tpu_custom_call" | custom-call | tf_op jit(solution)/shard_map/layer_step/pallas_call | solution.py:653
  198.2 0.0 copy-start.8
  198.2 0.0 copy-start.10
  198.2 0.0 copy-start.9
  198.2 2.8 %fusion.2 = f32[512,256]{1,0:T(8,128)} fusion(bf16[1024,512]{1,0:T(8,128)(2,1)} %bitcast.35, bf16[1024,256]{1,0:T(8,128)(2,1)} %bitcast.40), kind=kOutput, calls=%fused_computation.2 | convolution fusion | flops 268435456 | bytes 2097152 | tf_op jit(solution)/shard_map/dot_general | solution.py:28
  201.0 0.0 copy-done.8
  201.0 0.0 copy-done.10
  201.0 0.0 copy-start.2
  201.0 1.3 fusion.1
  202.3 0.0 copy-done.9
  202.3 1.3 fusion
  203.6 0.0 copy-done
  203.6 0.0 copy-done.2
  203.6 2.6 %fusion.4 = f32[512,1024]{1,0:T(8,128)} fusion(bf16[1024,512]{1,0:T(8,128)(2,1)S(1)} %bitcast.25, bf16[1024,1024]{1,0:T(8,128)(2,1)S(1)} %bitcast.28), kind=kOutput, calls=%fused_computation.4 | convolution fusion | flops 1073741824 | bytes 5242880 | tf_op jit(solution)/shard_map/dot_general | solution.py:28
  206.2 0.0 copy-done.1
  206.2 2.6 %fusion.3 = f32[512,1024]{1,0:T(8,128)} fusion(bf16[1024,512]{1,0:T(8,128)(2,1)S(1)} %bitcast.26, bf16[1024,1024]{1,0:T(8,128)(2,1)S(1)} %bitcast.27), kind=kOutput, calls=%fused_computation.3 | convolution fusion | flops 1073741824 | bytes 5242880 | tf_op jit(solution)/shard_map/dot_general | solution.py:28
  208.8 0.0 copy-done.6
  208.8 0.0 copy-done.7
  208.8 0.0 copy-start.3
  208.8 2.6 %fusion.5 = f32[1024,512]{1,0:T(8,128)} fusion(bf16[1024,1024]{1,0:T(8,128)(2,1)S(1)} %bitcast.33, bf16[1024,512]{1,0:T(8,128)(2,1)S(1)} %bitcast.34), kind=kOutput, calls=%fused_computation.5 | convolution fusion | flops 1073741824 | bytes 5242880 | tf_op jit(solution)/shard_map/dot_general | solution.py:28
  211.4 0.0 copy-done.5
  211.4 0.7 copy.23
  212.0 0.7 copy.24
  212.8 0.8 copy.25
  (8 shorter events, 0.0 us)
Async XLA Ops:
  198.2 2.8 %copy-start.8 = (bf16[4,2,128,512]{3,2,1,0:T(8,128)(2,1)S(1)}, bf16[4,2,128,512]{3,2,1,0:T(8,128)(2,1)}, u32[]{:S(2)}) copy-start(bf16[4,2,128,512]{3,2,1,0:T(8,128)(2,1)} %get-tuple-element.23) | copy-start | bytes 3145732
  198.2 2.8 %copy-start.10 = (bf16[4,256,256]{2,1,0:T(8,128)(2,1)S(1)}, bf16[4,256,256]{2,1,0:T(8,128)(2,1)}, u32[]{:S(2)}) copy-start(bf16[4,256,256]{2,1,0:T(8,128)(2,1)} %get-tuple-element.25) | copy-start | bytes 1572868
  198.2 4.1 %copy-start.9 = (bf16[4,256,256]{2,1,0:T(8,128)(2,1)S(1)}, bf16[4,256,256]{2,1,0:T(8,128)(2,1)}, u32[]{:S(2)}) copy-start(bf16[4,256,256]{2,1,0:T(8,128)(2,1)} %get-tuple-element.24) | copy-start | bytes 1572868
  201.0 2.6 %copy-start = (bf16[4,2,128,512]{3,2,1,0:T(8,128)(2,1)S(1)}, bf16[4,2,128,512]{3,2,1,0:T(8,128)(2,1)}, u32[]{:S(2)}) copy-start(bf16[4,2,128,512]{3,2,1,0:T(8,128)(2,1)} %get-tuple-element.28) | copy-start | bytes 3145732
  201.0 2.6 %copy-start.2 = (bf16[4,256,1024]{2,1,0:T(8,128)(2,1)S(1)}, bf16[4,256,1024]{2,1,0:T(8,128)(2,1)}, u32[]{:S(2)}) copy-start(bf16[4,256,1024]{2,1,0:T(8,128)(2,1)} %get-tuple-element.30) | copy-start | bytes 6291460
  203.6 2.6 %copy-start.1 = (bf16[4,256,1024]{2,1,0:T(8,128)(2,1)S(1)}, bf16[4,256,1024]{2,1,0:T(8,128)(2,1)}, u32[]{:S(2)}) copy-start(bf16[4,256,1024]{2,1,0:T(8,128)(2,1)} %get-tuple-element.29) | copy-start | bytes 6291460
  206.2 2.6 %copy-start.6 = (bf16[4,256,1024]{2,1,0:T(8,128)(2,1)S(1)}, bf16[4,256,1024]{2,1,0:T(8,128)(2,1)}, u32[]{:S(2)}) copy-start(bf16[4,256,1024]{2,1,0:T(8,128)(2,1)} %get-tuple-element.31) | copy-start | bytes 6291460
  206.2 2.6 %copy-start.7 = (bf16[4,2,128,512]{3,2,1,0:T(8,128)(2,1)S(1)}, bf16[4,2,128,512]{3,2,1,0:T(8,128)(2,1)}, u32[]{:S(2)}) copy-start(bf16[4,2,128,512]{3,2,1,0:T(8,128)(2,1)} %get-tuple-element.32) | copy-start | bytes 3145732
  208.8 2.6 %copy-start.5 = (bf16[2,128,256]{2,1,0:T(8,128)(2,1)S(1)}, bf16[2,128,256]{2,1,0:T(8,128)(2,1)}, u32[]{:S(2)}) copy-start(bf16[2,128,256]{2,1,0:T(8,128)(2,1)} %get-tuple-element.21) | copy-start | bytes 393220
  208.8 3.3 %copy-start.4 = (f32[2,128,256]{2,1,0:T(8,128)S(1)}, f32[2,128,256]{2,1,0:T(8,128)}, u32[]{:S(2)}) copy-start(f32[2,128,256]{2,1,0:T(8,128)} %get-tuple-element.22) | copy-start | bytes 786436
  208.8 4.0 %copy-start.3 = (f32[256,512]{1,0:T(8,128)S(1)}, f32[256,512]{1,0:T(8,128)}, u32[]{:S(2)}) copy-start(f32[256,512]{1,0:T(8,128)} %get-tuple-element.47) | copy-start | bytes 1572868

commit v6 on v5

--- a/solution.py
+++ b/solution.py
@@ -36,24 +36,47 @@
     def __init__(self, send, recv):
         self.send, self.recv, self.all = send, recv, []
 
+    def make(self, src, dst, i, j, peer):
+        return pltpu.make_async_remote_copy(
+            src_ref=src, dst_ref=dst, send_sem=self.send.at[i], recv_sem=self.recv.at[j],
+            device_id=peer, device_id_type=MESH)
+
+    def slot(self):
+        assert len(self.all) < self.send.shape[0]
+        self.all.append(None)
+        return len(self.all) - 1
+
     def __call__(self, src, dst, **peer):
-        i = len(self.all)
-        assert i < self.send.shape[0]
-        c = pltpu.make_async_remote_copy(
-            src_ref=src, dst_ref=dst, send_sem=self.send.at[i], recv_sem=self.recv.at[i],
-            device_id=peer, device_id_type=MESH)
+        i = self.slot()
+        c = self.make(src, dst, i, i, peer)
         c.start()
-        self.all.append(Copy(c))
-        return self.all[-1]
+        self.all[i] = Copy(c)
+        return self.all[i]
+
+    def only(self, pred, src, dst, land=None, **peer):
+        i = self.slot()
+        c = self.make(src, dst, i, i if land is None else land.i, peer)
+
+        @pl.when(pred)
+        def _():
+            c.start()
+
+        self.all[i] = Copy(c, pred, i)
+        return self.all[i]
 
     def drain(self):
         for c in self.all:
-            c.c.wait_send()
+            if c is None:
+                continue
+            if c.pred is None:
+                c.c.wait_send()
+            else:
+                pl.when(c.pred)(c.c.wait_send)
 
 
 class Copy:
-    def __init__(self, c):
-        self.c, self.open = c, True
+    def __init__(self, c, pred=None, i=None):
+        self.c, self.open, self.pred, self.i = c, True, pred, i
 
     def wait_recv(self):
         if self.open:
@@ -186,6 +209,27 @@
             fw.append(net(blk(c ^ (2 * m)), blk(c ^ (2 * m)), cols=c ^ 1))
         return fw
 
+    line = Z == 4
+    mid = ((z + 1) // 2) % 2
+
+    def line_start(blk):
+        b = blk(c)
+        z2 = net(b, b, cols=c ^ 4)
+        z3 = net.only(mid == 1, b, b, cols=c ^ 6)
+        return [net(b, b, cols=c ^ 2), z2, z3], net(b, b, cols=c ^ 1)
+
+    def line_relay(blk, zs):
+        zs[1].wait_recv()
+        b = blk(c ^ 4)
+        net.only(mid == 1, b, b, zs[2], cols=c ^ 2)
+
+    def line_forward(blk, zs):
+        fw = []
+        for m in (2, 1, 3):
+            zs[m - 1].wait_recv()
+            fw.append(net(blk(c ^ (2 * m)), blk(c ^ (2 * m)), cols=c ^ 1))
+        return fw
+
     def cols_finish(own, fw):
         own.wait_recv()
         for f in fw:
@@ -314,7 +358,52 @@
             out.append(net(ps.at[m], pr.at[m], cols=c ^ (2 * m)))
         return out
 
+    class Line:
+        def __init__(self, p, pa, ps, pr):
+            self.ps, self.pr = ps, pr
+            for m in (3, 1, 2):
+                ps[m] = (p[core, z ^ m].astype(F32) + pa[z ^ m].astype(F32)).astype(BF)
+                if m == 3:
+                    self.i, self.j = net.slot(), net.slot()
+                    far = net.make(ps.at[3], pr.at[3 * mid], self.i, self.j + mid * (self.i - self.j),
+                                   {"cols": c ^ (2 + 4 * mid)})
+                    far.start()
+                    net.all[self.i] = Copy(far)
+                if m == 1:
+                    self.c1 = net(ps.at[1], pr.at[1], cols=c ^ 2)
+
+            @pl.when(mid == 0)
+            def _():
+                pr[3] = jnp.zeros(pr.shape[1:], BF)
+
+        def relay(self):
+            ps, pr = self.ps, self.pr
+
+            @pl.when(mid == 1)
+            def _():
+                net.make(ps.at[3], pr.at[0], self.i, self.j, {"cols": c ^ 2}).wait_recv()
+                ps[2] = (ps[2].astype(F32) + pr[0].astype(F32)).astype(BF)
+
+            self.c2 = net(ps.at[2], pr.at[2], cols=c ^ 4)
+
+        def total(self, p, pa):
+            ps, pr = self.ps, self.pr
+            self.c1.wait_recv()
+            self.c2.wait_recv()
+
+            @pl.when(mid == 1)
+            def _():
+                net.make(ps.at[3], pr.at[3], self.i, self.i, {"cols": c ^ 6}).wait_recv()
+
+            return (p[core, z].astype(F32) + pa[z].astype(F32) + pr[1].astype(F32) + pr[2].astype(F32)
+                    + pr[3].astype(F32))
+
+    def line_send(p, pa, ps, pr):
+        return Line(p, pa, ps, pr) if line else zsend(p, pa, ps, pr)
+
     def zsum(p, pa, pr, cps):
+        if isinstance(cps, Line):
+            return cps.total(p, pa)
         tot = p[core, z].astype(F32) + pa[z].astype(F32)
         for m in range(1, Z):
             cps[m - 1].wait_recv()
@@ -506,8 +595,8 @@
 
     def dblk(j):
         return dmix.at[:, at(j * TH, TH), :]
-    m_z = [net(dmt, dblk(c), cols=c ^ (2 * m)) for m in range(1, Z)]
-    m_p = net(dmt, dblk(c), cols=c ^ 1)
+    l_m.wait()
+    m_z, m_p = line_start(dblk) if line else cols_start(dblk)
 
     def ffn_block(k):
         s = r ^ k
@@ -520,6 +609,8 @@
     h_f = cols_forward(wsblk(h1w), h_z)
     for d in hdc[1:]:
         d.forward()
+    if line:
+        line_relay(dblk, m_z)
     for k in order:
         for d in hdc:
             d.wait(k)
@@ -528,9 +619,8 @@
     cols_finish(h_p, h_f)
     lout += [local(hda, hd_out), local(h1w, h1w_out)]
     k3.wait_recv()
-    m_f = cols_forward(dblk, m_z)
-    z3 = zsend(p3, p3a, p3s, p3r)
-    l_m.wait()
+    m_f = line_forward(dblk, m_z) if line else cols_forward(dblk, m_z)
+    z3 = line_send(p3, p3a, p3s, p3r)
     cols_finish(m_p, m_f)
 
     for k in order:
@@ -557,12 +647,17 @@
             for t in range(NT):
                 p4[t, j % 2, j // 2, :, ns] = piece(val, j, t).astype(BF)
     k4 = [pre(p4.at[t], p4a.at[t]) for t in range(NT)]
+    if line:
+        z3.relay()
     z4 = []
     for t in range(NT):
         k4[t].wait_recv()
-        z4.append(zsend(p4.at[t], p4a.at[t], p4s.at[t], p4r.at[t]))
+        z4.append(line_send(p4.at[t], p4a.at[t], p4s.at[t], p4r.at[t]))
+    cgo.relay()
+    if line:
+        for k in z4:
+            k.relay()
     gof[...] = tn(att[...], dmix[:, :, at(r * DR, DR)].reshape(L, DR))
-    cgo.relay()
 
     fs[...] = zsum(p3, p3a, p3r, z3).astype(BF)
     a_f = [net(fs.at[k], ft.at[:, at(r * DR, DR)], rows=r ^ k) for k in order]
@@ -669,7 +764,7 @@
 
 
 def g_sems(R, C, n):
-    return 2 * (R - 1) * (8 + n) + 2 * R * (3 + n) + 8 * (R - 1) + 16 * C + (R + 4) * C // 2
+    return 2 * (R - 1) * (8 + n) + 2 * R * (3 + n) + 8 * (R - 1) + 17 * C + (R + 4) * C // 2
 
 
 def solution(mesh):

time: 214 us -> 211 us (0.986)
  Pallas kernels: 198 us -> 195 us
    pallas_call x1, Pallas kernels: 198 us -> 195 us  [body(): pl.pallas_call(functools.partial(step_kernel, g), out_shape=outs, in_spec...]
where the time goes in v6:
time: 211 us
  Pallas kernels  195 us (92%)
  matrix products  13.1 us (6%)
  local copies, waits for them, and re-layouts  2.19 us (1%)
    pallas_call x1, Pallas kernels, body(): pl.pallas_call(functools.partial(step_kernel, g), out_shape=outs, in_spec...  195 us
    dot_general x6, matrix products, tn(): lax.dot_general(a, b, (((0,), (0,)), ((), ())), preferred_element_type=F32)  13.1 us

profile of v6, /device:TPU:0, one launch (start us, length us, event | category | flops | bytes accessed | tf_op | source)
XLA Modules:
  0.0 210.7 jit_solution(7761527014865253778)
XLA Ops:
  0.6 194.7 %layer_step.1 = (bf16[2,128,256]{2,1,0:T(8,128)(2,1)}, f32[2,128,256]{2,1,0:T(8,128)}, bf16[4,2,128,512]{3,2,1,0:T(8,128)(2,1)}, bf16[4,2,128,512]{3,2,1,0:T(8,1...) custom-call(bf16[2,128,256]{2,1,0:T(8,128)(2,1)} %bitcast.31, ...), custom_call_target="tpu_custom_call" | custom-call | tf_op jit(solution)/shard_map/layer_step/pallas_call | solution.py:748
  195.3 0.0 copy-start.8
  195.4 0.0 copy-start.10
  195.4 0.0 copy-start.9
  195.4 2.8 %fusion.2 = f32[512,256]{1,0:T(8,128)} fusion(bf16[1024,512]{1,0:T(8,128)(2,1)} %bitcast.35, bf16[1024,256]{1,0:T(8,128)(2,1)} %bitcast.40), kind=kOutput, calls=%fused_computation.2 | convolution fusion | flops 268435456 | bytes 2097152 | tf_op jit(solution)/shard_map/dot_general | solution.py:28
  198.2 0.0 copy-done.8
  198.2 0.0 copy-done.10
  198.2 0.0 copy-start.2
  198.2 1.3 fusion.1
  199.4 0.0 copy-done.9
  199.4 1.3 fusion
  200.7 0.0 copy-done
  200.7 0.0 copy-done.2
  200.7 2.6 %fusion.4 = f32[512,1024]{1,0:T(8,128)} fusion(bf16[1024,512]{1,0:T(8,128)(2,1)S(1)} %bitcast.25, bf16[1024,1024]{1,0:T(8,128)(2,1)S(1)} %bitcast.28), kind=kOutput, calls=%fused_computation.4 | convolution fusion | flops 1073741824 | bytes 5242880 | tf_op jit(solution)/shard_map/dot_general | solution.py:28
  203.3 0.0 copy-done.1
  203.3 2.6 %fusion.3 = f32[512,1024]{1,0:T(8,128)} fusion(bf16[1024,512]{1,0:T(8,128)(2,1)S(1)} %bitcast.26, bf16[1024,1024]{1,0:T(8,128)(2,1)S(1)} %bitcast.27), kind=kOutput, calls=%fused_computation.3 | convolution fusion | flops 1073741824 | bytes 5242880 | tf_op jit(solution)/shard_map/dot_general | solution.py:28
  205.9 0.0 copy-done.6
  205.9 0.0 copy-done.7
  205.9 0.0 copy-start.3
  205.9 2.6 %fusion.5 = f32[1024,512]{1,0:T(8,128)} fusion(bf16[1024,1024]{1,0:T(8,128)(2,1)S(1)} %bitcast.33, bf16[1024,512]{1,0:T(8,128)(2,1)S(1)} %bitcast.34), kind=kOutput, calls=%fused_computation.5 | convolution fusion | flops 1073741824 | bytes 5242880 | tf_op jit(solution)/shard_map/dot_general | solution.py:28
  208.5 0.0 copy-done.5
  208.5 0.7 copy.23
  209.2 0.7 copy.24
  209.9 0.8 copy.25
  (8 shorter events, 0.0 us)
Async XLA Ops:
  195.3 2.8 %copy-start.8 = (bf16[4,2,128,512]{3,2,1,0:T(8,128)(2,1)S(1)}, bf16[4,2,128,512]{3,2,1,0:T(8,128)(2,1)}, u32[]{:S(2)}) copy-start(bf16[4,2,128,512]{3,2,1,0:T(8,128)(2,1)} %get-tuple-element.23) | copy-start | bytes 3145732
  195.4 2.8 %copy-start.10 = (bf16[4,256,256]{2,1,0:T(8,128)(2,1)S(1)}, bf16[4,256,256]{2,1,0:T(8,128)(2,1)}, u32[]{:S(2)}) copy-start(bf16[4,256,256]{2,1,0:T(8,128)(2,1)} %get-tuple-element.25) | copy-start | bytes 1572868
  195.4 4.1 %copy-start.9 = (bf16[4,256,256]{2,1,0:T(8,128)(2,1)S(1)}, bf16[4,256,256]{2,1,0:T(8,128)(2,1)}, u32[]{:S(2)}) copy-start(bf16[4,256,256]{2,1,0:T(8,128)(2,1)} %get-tuple-element.24) | copy-start | bytes 1572868
  198.2 2.6 %copy-start = (bf16[4,2,128,512]{3,2,1,0:T(8,128)(2,1)S(1)}, bf16[4,2,128,512]{3,2,1,0:T(8,128)(2,1)}, u32[]{:S(2)}) copy-start(bf16[4,2,128,512]{3,2,1,0:T(8,128)(2,1)} %get-tuple-element.28) | copy-start | bytes 3145732
  198.2 2.6 %copy-start.2 = (bf16[4,256,1024]{2,1,0:T(8,128)(2,1)S(1)}, bf16[4,256,1024]{2,1,0:T(8,128)(2,1)}, u32[]{:S(2)}) copy-start(bf16[4,256,1024]{2,1,0:T(8,128)(2,1)} %get-tuple-element.30) | copy-start | bytes 6291460
  200.7 2.6 %copy-start.1 = (bf16[4,256,1024]{2,1,0:T(8,128)(2,1)S(1)}, bf16[4,256,1024]{2,1,0:T(8,128)(2,1)}, u32[]{:S(2)}) copy-start(bf16[4,256,1024]{2,1,0:T(8,128)(2,1)} %get-tuple-element.29) | copy-start | bytes 6291460
  203.3 2.6 %copy-start.6 = (bf16[4,256,1024]{2,1,0:T(8,128)(2,1)S(1)}, bf16[4,256,1024]{2,1,0:T(8,128)(2,1)}, u32[]{:S(2)}) copy-start(bf16[4,256,1024]{2,1,0:T(8,128)(2,1)} %get-tuple-element.31) | copy-start | bytes 6291460
  203.3 2.6 %copy-start.7 = (bf16[4,2,128,512]{3,2,1,0:T(8,128)(2,1)S(1)}, bf16[4,2,128,512]{3,2,1,0:T(8,128)(2,1)}, u32[]{:S(2)}) copy-start(bf16[4,2,128,512]{3,2,1,0:T(8,128)(2,1)} %get-tuple-element.32) | copy-start | bytes 3145732
  205.9 2.6 %copy-start.5 = (bf16[2,128,256]{2,1,0:T(8,128)(2,1)S(1)}, bf16[2,128,256]{2,1,0:T(8,128)(2,1)}, u32[]{:S(2)}) copy-start(bf16[2,128,256]{2,1,0:T(8,128)(2,1)} %get-tuple-element.21) | copy-start | bytes 393220
  205.9 3.3 %copy-start.4 = (f32[2,128,256]{2,1,0:T(8,128)S(1)}, f32[2,128,256]{2,1,0:T(8,128)}, u32[]{:S(2)}) copy-start(f32[2,128,256]{2,1,0:T(8,128)} %get-tuple-element.22) | copy-start | bytes 786436
  205.9 4.0 %copy-start.3 = (f32[256,512]{1,0:T(8,128)S(1)}, f32[256,512]{1,0:T(8,128)}, u32[]{:S(2)}) copy-start(f32[256,512]{1,0:T(8,128)} %get-tuple-element.47) | copy-start | bytes 1572868

commit v7 on v6

--- a/solution.py
+++ b/solution.py
@@ -155,11 +155,11 @@
 
 def step_kernel(g, *refs):
     (tok, cot, seg_in, freq_in, wq, wk, wv, wo, wg, wu, wd,
-     o_out, gi_out, h1w_out, gw_out, h2w_out, dg_out, du_out, hd_out, dq_out, dk_out, dv_out, go_out,
+     o_out, gi_out, gg_out, gu_out, gd_out, gq_out, gk_out, gv_out, go_out,
      xb, h1, xtl, gtl, h1w, gw, h2w, h2t, wqf, wkf, wvf, wof, wgv, wuv, wdv,
      p1, p1a, p1s, p1r, p2, p2a, p2s, p2r, p3, p3a, p3s, p3r, p4, p4a, p4s, p4r,
      x1, n2, dhs, dhr, dho, gus, gur, guo, hda, dgu, dh2s, dh2t, dxt, dmt, dmix,
-     qb, kb, vb, att, lse, cosb, sinb, mskb, dqkv, gop, gor, gof, fs, ft, lot, git, lob, gib, gif, segr, freq,
+     qb, kb, vb, att, lse, cosb, sinb, mskb, dqkv, gop, gor, gof, fs, ft, lot, git, lob, gib, wgg, wgu, wgd, wqa, segr, freq,
      send, recv, loc) = refs
     R, C, L, TL, D, DR, DC, HC, NT = (g[k] for k in ("R", "C", "L", "TL", "D", "DR", "DC", "HC", "NT"))
     LH, TH = L // NT, TL // NT
@@ -417,7 +417,7 @@
         k1[t].wait_recv()
         z1.append(zsend(p1.at[t], p1a.at[t], p1s.at[t], p1r.at[t]))
     cols_finish(g_p, g_f)
-    lout = [local(gw, gw_out)]
+    lout = []
 
     lff[0].wait()
     order = list(range(1, R))
@@ -496,7 +496,6 @@
         if len(gu) > 1:
             gu[-2].relay()
     gu[-1].relay()
-    lout.append(local(h2w, h2w_out))
     landed(a_h)
     h_z, h_p = cols_start(wsblk(h1w))
 
@@ -563,7 +562,15 @@
         dh2_block(k)
         z2_send(n)
     z2_send(R - 1)
-    lout += [local(dgu.at[0], dg_out), local(dgu.at[1], du_out)]
+    T = R * L
+
+    def wgrad(dst, lhs, rhs):
+        w = 128
+        for i in range(dst.shape[0] // w):
+            dst[i * w:(i + 1) * w, :] = tn(lhs(slice(i * w, (i + 1) * w)), rhs).astype(BF)
+
+    wgrad(wgg, lambda ns: h2w[:, :, :, ns].reshape(T, 128), dgu[0].reshape(T, FC))
+    lout.append(local(wgg, gg_out))
     hdc[0].forward()
 
     a_d = []
@@ -607,6 +614,8 @@
 
     ffn_block(0)
     h_f = cols_forward(wsblk(h1w), h_z)
+    wgrad(wgu, lambda ns: h2w[:, :, :, ns].reshape(T, 128), dgu[1].reshape(T, FC))
+    lout.append(local(wgu, gu_out))
     for d in hdc[1:]:
         d.forward()
     if line:
@@ -617,7 +626,6 @@
         ffn_block(k)
     k3 = pre(p3, p3a)
     cols_finish(h_p, h_f)
-    lout += [local(hda, hd_out), local(h1w, h1w_out)]
     k3.wait_recv()
     m_f = line_forward(dblk, m_z) if line else cols_forward(dblk, m_z)
     z3 = line_send(p3, p3a, p3s, p3r)
@@ -668,11 +676,22 @@
         cps = [net(src.at[t, :, at((c ^ k) * DC, DC)], dst.at[t, my_th, :], cols=c ^ k) for k in range(1, C)]
         return cps, local(src.at[t, :, at(c * DC, DC)], dst.at[t, my_th, :])
 
+    def qkv_grad(k):
+        for i in range(3):
+            t = tn(h1w[r ^ k].reshape(L, DR), dqkv[i, r ^ k])
+            wqa[i] = t if k == 0 else wqa[i] + t
+
+    qkv_grad(0)
+    wgrad(wgd, lambda ns: hda[:, :, ns].reshape(T, 128), gw[...].reshape(T, DR))
+    lout.append(local(wgd, gd_out))
     l_f.wait()
     for k in a_f:
         k.wait_recv()
     lot[...] = (x1[...] + ft[...].astype(F32)).astype(BF).reshape(NT, TH, D)
     i_o = to_io(lot, lob)
+    for k in order[:-1]:
+        cd.wait(k)
+        qkv_grad(k)
     i_g = []
     for t in range(NT):
         rows = slice(t * TH, (t + 1) * TH)
@@ -680,14 +699,14 @@
         dh1 = zsum(p4.at[t], p4a.at[t], p4r.at[t], z4[t])
         git[t] = (dxt[rows, :] + norm_back(dh1, xtl[rows, :], rstd1)).astype(BF)
         i_g.append(to_io(git, gib, t))
+    cd.wait(R - 1)
+    qkv_grad(R - 1)
+    lout += [local(wqa.at[0], gq_out), local(wqa.at[1], gk_out), local(wqa.at[2], gv_out)]
     landed(i_o)
     lout.append(local(lob, o_out))
     for k in i_g:
         landed(k)
-    gif[...] = gib[...].astype(F32)
-    lout.append(local(gif, gi_out))
-    arrived(cd)
-    lout += [local(dqkv.at[0], dq_out), local(dqkv.at[1], dk_out), local(dqkv.at[2], dv_out)]
+    lout.append(local(gib, gi_out))
     cgo.wait()
     gsum = gof[...]
     for k in cgo.ks:
@@ -717,9 +736,8 @@
     S = jax.ShapeDtypeStruct
     V = pltpu.VMEM
     outs = [
-        S((NT, LH, DC), BF), S((NT, LH, DC), F32), *[S((R, NT, LH, DR), BF)] * 3,
-        S((R, L, FC), BF), S((R, L, FC), BF), S((R, L, FC), BF),
-        S((R, L, HC), BF), S((R, L, HC), BF), S((R, L, HC), BF), S((HC, DR), F32),
+        S((NT, LH, DC), BF), S((NT, LH, DC), BF), S((DR, FC), BF), S((DR, FC), BF), S((FC, DR), BF),
+        *[S((DR, HC), F32)] * 3, S((HC, DR), F32),
     ]
     seq = lambda w: [V((NT, 2, Z, TH, w), BF)] + [V((NT, Z, TH, w), BF)] * 3
     seq4 = lambda: [V((2, Z, R, TL, DR), BF), V((Z, R, TL, DR), BF), V((Z, R, TL, DR), BF), V((Z, R, TL, DR), BF)]
@@ -739,7 +757,8 @@
         V((L, HD), F32), V((L, HD), F32), V((L, L), F32),
         V((3, R, L, HC), BF), V((R, HC, DR), BF), V((R, HC, DR), BF), V((HC, DR), F32),
         V((R, TL, DR), BF), V((TL, D), BF), V((NT, TH, D), BF), V((NT, TH, D), BF),
-        V((NT, LH, DC), BF), V((NT, LH, DC), BF), V((NT, LH, DC), F32),
+        V((NT, LH, DC), BF), V((NT, LH, DC), BF),
+        V((DR, FC), BF), V((DR, FC), BF), V((FC, DR), BF), V((3, DR, HC), F32),
         V((1, L), jnp.int32), V((1, HD), F32),
         pltpu.SemaphoreType.DMA((g_sems(R, C, NT * QN),)), pltpu.SemaphoreType.DMA((g_sems(R, C, NT * QN),)),
         pltpu.SemaphoreType.DMA((48,)),
@@ -755,13 +774,43 @@
             collective_id=0, has_side_effects=True, vmem_limit_bytes=67043328),
         name="layer_step",
     )(tokens.reshape(NT, LH, DC), cotangent.reshape(NT, LH, DC), segments, freq, w_query, w_key, w_value, w_out, w_gate, w_up, w_down)
-    layer_out, grad_in, h1w, gw, h2w, dg, du, hd, dq, dk, dv, go = res
-    T = R * L
-    h1w, gw, h2w = (t.reshape(T, DR) for t in (h1w, gw, h2w))
-    gq, gk, gv = (tn(h1w, t.reshape(T, HC)) for t in (dq, dk, dv))
-    ggate, gup, gdown = tn(h2w, dg.reshape(T, FC)), tn(h2w, du.reshape(T, FC)), tn(hd.reshape(T, FC), gw)
-    return layer_out.reshape(L, DC), grad_in.reshape(L, DC), gq, gk, gv, go, ggate, gup, gdown
-
+    layer_out, grad_in, ggate, gup, gdown, gq, gk, gv, go = res
+    return finish(layer_out.reshape(L, DC), grad_in.reshape(L, DC), gq, gk, gv, go, ggate, gup, gdown)
+
+
+def finish(layer_out, *grads):
+    ins = (layer_out,) + grads
+    n = len(ins)
+    types = [BF] + [F32] * len(grads)
+    wide = [i for i in range(n) if ins[i].dtype != types[i]]
+
+    def kern(*refs):
+        src, dst, buf = refs[:n], refs[n:2 * n], refs[2 * n:3 * n]
+        out = dict(zip(wide, refs[3 * n:3 * n + len(wide)]))
+        si, so = refs[-2:]
+        got = [pltpu.make_async_copy(src[i], buf[i], si.at[i]) for i in range(n)]
+        put = [pltpu.make_async_copy(out.get(i, buf[i]), dst[i], so.at[i]) for i in range(n)]
+        for i in reversed(range(n)):
+            got[i].start()
+        for i in reversed(range(n)):
+            got[i].wait()
+            if i in out:
+                out[i][...] = buf[i][...].astype(F32)
+            put[i].start()
+        for i in range(n):
+            put[i].wait()
+
+    A = pl.BlockSpec(memory_space=pl.ANY)
+    V = pltpu.VMEM
+    return pl.pallas_call(
+        kern,
+        out_shape=[jax.ShapeDtypeStruct(a.shape, t) for a, t in zip(ins, types)],
+        in_specs=[A] * n, out_specs=[A] * n,
+        scratch_shapes=[V(a.shape, a.dtype) for a in ins] + [V(ins[i].shape, F32) for i in wide]
+        + [pltpu.SemaphoreType.DMA((n,)), pltpu.SemaphoreType.DMA((n,))],
+        compiler_params=pltpu.CompilerParams(vmem_limit_bytes=67043328),
+        name="finish",
+    )(*ins)
 
 def g_sems(R, C, n):
     return 2 * (R - 1) * (8 + n) + 2 * R * (3 + n) + 8 * (R - 1) + 17 * C + (R + 4) * C // 2

time: 211 us -> 200 us (0.948)
  matrix products: 13.1 us -> 0 us
  Pallas kernels: 195 us -> 199 us
  local copies, waits for them, and re-layouts: 2.19 us -> 0 us
    dot_general x6 -> x0, matrix products: 13.1 us -> none  [tn(): lax.dot_general(a, b, (((0,), (0,)), ((), ())), preferred_element_type=F32)]
    pallas_call x0 -> x1, Pallas kernels: none -> 4.91 us  [finish(): pl.pallas_call(kern, out_shape=[jax.ShapeDtypeStruct(a.shape, t) for a, t...]
    unnamed x25 -> x0, local copies, waits for them, and re-layouts: 2.19 us -> none
where the time goes in v7:
time: 200 us
  Pallas kernels  199 us (100%)
    pallas_call x1, Pallas kernels, body(): pl.pallas_call(functools.partial(step_kernel, g), out_shape=outs, in_spec...  194 us
    pallas_call x1, Pallas kernels, finish(): pl.pallas_call(kern, out_shape=[jax.ShapeDtypeStruct(a.shape, t) for a, t...  4.91 us

profile of v7, /device:TPU:0, one launch (start us, length us, event | category | flops | bytes accessed | tf_op | source)
XLA Modules:
  0.0 200.1 jit_solution(10742581398920067014)
XLA Ops:
  0.6 194.4 %layer_step.1 = (bf16[2,128,256]{2,1,0:T(8,128)(2,1)}, bf16[2,128,256]{2,1,0:T(8,128)(2,1)}, bf16[512,1024]{1,0:T(8,128)(2,1)}, bf16[512,1024]{1,0:T(8,128)(2,1)...) custom-call(bf16[2,128,256]{2,1,0:T(8,128)(2,1)} %bitcast.6, ...), custom_call_target="tpu_custom_call" | custom-call | tf_op jit(solution)/shard_map/layer_step/pallas_call | solution.py:767
  195.1 4.9 %finish.1 = (bf16[256,256]{1,0:T(8,128)(2,1)}, f32[256,256]{1,0:T(8,128)}, f32[512,256]{1,0:T(8,128)}, f32[512,256]{1,0:T(8,128)}, f32[512,256]{1,0:T(8,128)}, /...) custom-call(bf16[256,256]{1,0:T(8,128)(2,1)} %bitcast.4, ...), custom_call_target="tpu_custom_call" | custom-call | tf_op jit(solution)/shard_map/finish/pallas_call | solution.py:805

commit v8 on v7

--- a/solution.py
+++ b/solution.py
@@ -239,10 +239,9 @@
         return xb.at[:, :, at(j * DC, DC)]
 
     cq = w_in(wq, wqf)
+    ga = [net(cot.at[:, at((c ^ k) * TH, TH), :], gtl.at[:, :, at(c * DC, DC)], cols=c ^ k) for k in range(1, C)]
     xz = [net(tok, xblk(c), cols=c ^ (2 * m)) for m in range(1, Z)]
     xp = net(tok, xblk(c), cols=c ^ 1)
-    ga = [net(cot.at[:, at((c ^ k) * TH, TH), :], gtl.at[:, :, at(c * DC, DC)], cols=c ^ k) for k in range(1, C)]
-    ck = w_in(wk, wkf)
 
     for k in lsm:
         k.wait()
@@ -269,14 +268,20 @@
             k.wait_recv()
         cl[1].wait()
 
-    cq.forward()
-    cv = w_in(wv, wvf)
-    lx.wait()
-    xf = cols_forward(xblk, xz)
+    def wsblk(buf, t=slice(None)):
+        return lambda j: buf.at[:, t, at(j * TH, TH), :]
+
     lg.wait()
     for k in ga:
         k.wait_recv()
     a_g = to_ws(gtl, gw)
+    ck = w_in(wk, wkf)
+    cq.forward()
+    landed(a_g)
+    g_z, g_p = cols_start(wsblk(gw))
+    cv = w_in(wv, wvf)
+    lx.wait()
+    xf = cols_forward(xblk, xz)
     ck.forward()
     cols_finish(xp, xf)
 
@@ -298,9 +303,6 @@
     cv.forward()
     co = Gather(net, R, r, lambda h: wo.at[half(HC, h), :], lambda j, h: wof.at[half(HC, h), at(j * DR, DR)])
 
-    def wsblk(buf, t=slice(None)):
-        return lambda j: buf.at[:, t, at(j * TH, TH), :]
-
     heads = HC // HD
 
     def rope(v):
@@ -315,8 +317,6 @@
         for k in range(1, R):
             g.wait(k)
 
-    landed(a_g)
-    g_z, g_p = cols_start(wsblk(gw))
     lws[0].wait()
     arrived(cq)
     qb[...] = rope(nn(h1[...].reshape(L, D), wqf[...])).astype(BF)
@@ -326,6 +326,7 @@
     lws[2].wait()
     arrived(cv)
     vb[...] = nn(h1[...].reshape(L, D), wvf[...]).astype(BF)
+    g_f = cols_forward(wsblk(gw), g_z)
 
     for h in range(heads):
         hs = slice(h * HD, (h + 1) * HD)
@@ -336,17 +337,6 @@
         tot = jnp.sum(e, 1, keepdims=True)
         lse[:, hs] = jnp.broadcast_to(top + jnp.log(tot), (L, HD))
         att[:, hs] = nn((e / tot).astype(BF), vb[:, hs]).astype(BF)
-
-    co.forward()
-    lws[3].wait()
-    arrived(co)
-    W1 = min(512, D)
-    for n in range(D // W1):
-        ns = slice(n * W1, (n + 1) * W1)
-        val = nn(att[...], wof[:, ns])
-        for j in range(C):
-            for t in range(NT):
-                p1[t, j % 2, j // 2, :, ns] = piece(val, j, t).astype(BF)
 
     def pre(p, pa):
         return net(p.at[1 - core], pa, cols=c ^ 1)
@@ -406,20 +396,35 @@
             return cps.total(p, pa)
         tot = p[core, z].astype(F32) + pa[z].astype(F32)
         for m in range(1, Z):
-            cps[m - 1].wait_recv()
+            for cp in cps[m - 1] if isinstance(cps[m - 1], list) else [cps[m - 1]]:
+                cp.wait_recv()
             tot = tot + pr[m].astype(F32)
         return tot
 
-    k1 = [pre(p1.at[t], p1a.at[t]) for t in range(NT)]
-    g_f = cols_forward(wsblk(gw), g_z)
-    z1 = []
-    for t in range(NT):
-        k1[t].wait_recv()
-        z1.append(zsend(p1.at[t], p1a.at[t], p1s.at[t], p1r.at[t]))
-    cols_finish(g_p, g_f)
-    lout = []
-
-    lff[0].wait()
+    def x1_slice(k):
+        ns = at((r ^ k) * DR, DR)
+        val = nn(att[...], wof[:, ns])
+        for j in range(C):
+            for t in range(NT):
+                p1[t, j % 2, j // 2, :, ns] = piece(val, j, t).astype(BF)
+        return net(p1.at[:, 1 - core, :, :, ns], p1a.at[:, :, :, ns], cols=c ^ 1)
+
+    z1 = [[[] for _ in range(1, Z)] for _ in range(NT)]
+
+    def z1_send(k, pre_sum, last=False):
+        ns = at((r ^ k) * DR, DR)
+        pre_sum.wait_recv()
+        for t in range(NT):
+            for m in range(1, Z):
+                p1s[t, m, :, ns] = (p1[t, core, z ^ m, :, ns].astype(F32) + p1a[t, z ^ m, :, ns].astype(F32)).astype(BF)
+                if last:
+                    z1[t][m - 1].append(net(p1s.at[t, m, :, ns], p1r.at[t, m, :, ns], cols=c ^ (2 * m)))
+        if not last:
+            for m in range(1, Z):
+                cp = net(p1s.at[:, m, :, ns], p1r.at[:, m, :, ns], cols=c ^ (2 * m))
+                for t in range(NT):
+                    z1[t][m - 1].append(cp)
+
     order = list(range(1, R))
     FC = wgv.shape[1]
     DN = 2
@@ -433,8 +438,23 @@
         ns = slice(n * DW, (n + 1) * DW)
         return Reduce(net, R, r, lambda k, h: dhs.at[k, half(L, h), ns], lambda k, h: dhr.at[k, half(L, h), ns])
 
+    lws[3].wait()
+    k1 = [x1_slice(0)]
+    co.forward()
+    cols_finish(g_p, g_f)
+    lout = []
+    z1_send(0, k1[0])
+    lff[0].wait()
     dhid_chunk(0)
     dh = [dhid_send(0)]
+    for k in order[:-1]:
+        co.wait(k)
+        k1.append(x1_slice(k))
+    for k in order[:-1]:
+        z1_send(k, k1[k])
+    co.wait(R - 1)
+    k1.append(x1_slice(R - 1))
+    z1_send(R - 1, k1[R - 1], True)
     for n in range(1, DN):
         dhid_chunk(n)
 
@@ -452,21 +472,6 @@
         h2t[t] = n2v.astype(BF)
         return to_ws(h2t, h2w, t)
 
-    h2_c = []
-    for t in range(NT):
-        a_2 = second_norm(t)
-        if t == 0:
-            for n in range(1, DN):
-                dh.append(dhid_send(n))
-            for n in range(DN):
-                dho[:, n * DW:(n + 1) * DW] = nt(gw[r].reshape(L, DR), wdv[n * DW:(n + 1) * DW, :])
-        else:
-            dh[0].relay()
-        landed(a_2)
-        h2_c.append(cols_start(wsblk(h2w, t)))
-    for d in dh[min(NT, 2) - 1:]:
-        d.relay()
-    a_h = to_ws(h1.at[:, my_th, :], h1w)
     lff[1].wait()
     lff[2].wait()
 
@@ -489,9 +494,31 @@
         gu.append(Reduce(net, R, r, lambda k, h: gus.at[k, t, q, :, half(LH, h), :],
                          lambda k, h: gur.at[k, t, q, :, half(LH, h), :]))
 
-    for t, q in parts:
+    def ahead():
+        cols_finish(h2_c[0][1], (line_forward if line else cols_forward)(wsblk(h2w, 0), h2_c[0][0]))
+        gu_chunk(*parts[0])
+
+    h2_c = []
+    for t in range(NT):
+        a_2 = second_norm(t)
+        if t == 0:
+            dh[0].relay()
+            for n in range(1, DN):
+                dh.append(dhid_send(n))
+            for n in range(DN):
+                dho[:, n * DW:(n + 1) * DW] = nt(gw[r].reshape(L, DR), wdv[n * DW:(n + 1) * DW, :])
+        if t:
+            ahead()
+        landed(a_2)
+        h2_c.append((line_start if line else cols_start)(wsblk(h2w, t)))
+        if line:
+            line_relay(wsblk(h2w, t), h2_c[t][0])
+    for d in dh[1:]:
+        d.relay()
+    a_h = to_ws(h1.at[:, my_th, :], h1w)
+    for t, q in parts[len(gu):]:
         if q == 0:
-            cols_finish(h2_c[t][1], cols_forward(wsblk(h2w, t), h2_c[t][0]))
+            cols_finish(h2_c[t][1], (line_forward if line else cols_forward)(wsblk(h2w, t), h2_c[t][0]))
         gu_chunk(t, q)
         if len(gu) > 1:
             gu[-2].relay()
@@ -648,6 +675,7 @@
         dqkv[2, r, :, hs] = tn(pr.astype(BF), da[:, hs]).astype(BF)
     cd = Gather(net, R, r, lambda h: dqkv.at[:, r, half(L, h), :], lambda j, h: dqkv.at[:, j, half(L, h), :])
 
+    W1 = min(512, D)
     for n in range(D // W1):
         ns = slice(n * W1, (n + 1) * W1)
         val = (nt(dqkv[0, r], wqf[ns, :]) + nt(dqkv[1, r], wkf[ns, :]) + nt(dqkv[2, r], wvf[ns, :]))
@@ -813,7 +841,7 @@
     )(*ins)
 
 def g_sems(R, C, n):
-    return 2 * (R - 1) * (8 + n) + 2 * R * (3 + n) + 8 * (R - 1) + 17 * C + (R + 4) * C // 2
+    return 2 * (R - 1) * (8 + n) + 2 * R * (3 + n) + 8 * (R - 1) + 17 * C + (2 * R + 6) * C // 2
 
 
 def solution(mesh):

time: 200 us -> 202 us (1.010)
  no operation moved by 1% of the time
where the time goes in v8:
time: 202 us
  Pallas kernels  201 us (100%)
    pallas_call x1, Pallas kernels, body(): pl.pallas_call(functools.partial(step_kernel, g), out_shape=outs, in_spec...  196 us
    pallas_call x1, Pallas kernels, finish(): pl.pallas_call(kern, out_shape=[jax.ShapeDtypeStruct(a.shape, t) for a, t...  4.91 us

profile of v8, /device:TPU:0, one launch (start us, length us, event | category | flops | bytes accessed | tf_op | source)
XLA Modules:
  0.0 201.9 jit_solution(7981653718579438737)
XLA Ops:
  0.6 196.1 %layer_step.1 = (bf16[2,128,256]{2,1,0:T(8,128)(2,1)}, bf16[2,128,256]{2,1,0:T(8,128)(2,1)}, bf16[512,1024]{1,0:T(8,128)(2,1)}, bf16[512,1024]{1,0:T(8,128)(2,1)...) custom-call(bf16[2,128,256]{2,1,0:T(8,128)(2,1)} %bitcast.6, ...), custom_call_target="tpu_custom_call" | custom-call | tf_op jit(solution)/shard_map/layer_step/pallas_call | solution.py:795
  196.8 4.9 %finish.1 = (bf16[256,256]{1,0:T(8,128)(2,1)}, f32[256,256]{1,0:T(8,128)}, f32[512,256]{1,0:T(8,128)}, f32[512,256]{1,0:T(8,128)}, f32[512,256]{1,0:T(8,128)}, /...) custom-call(bf16[256,256]{1,0:T(8,128)(2,1)} %bitcast.4, ...), custom_call_target="tpu_custom_call" | custom-call | tf_op jit(solution)/shard_map/finish/pallas_call | solution.py:833
